TPU v7x, 256 devices: a whole 4x4x8 slice. The times are simulated.
256 devices in a mesh: space: 128 (over z, x, y_hi, core), tm: 2 (over y_lo).
Axes of the slice: x: 4, y: 4 (y_hi: 2, y_lo: 2; y = y_hi * 2 + y_lo), z: 8, core: 2. Of those that a mesh axis runs over, the one named last changes fastest.
Arguments:
- features: bfloat16 [128, 2, 2, 512, 128], P('space', 'tm'), may hold values from -6 to 6
- cotangent: bfloat16 [128, 2, 2, 512, 128], P('space', 'tm'), may hold values from -6 to 6
- w_first: bfloat16 [27, 128, 128], replicated, may hold values from -0.109375 to 0.109375
- w_second: bfloat16 [27, 128, 128], replicated, may hold values from -0.109375 to 0.109375
- occupancy: int32 [128, 2, 2, 512], P('space', 'tm'), may hold values from 0 to 1, as said below
- neighbors: int32 [128, 2, 2, 27], P('space', 'tm'), may hold values from -1 to 9, as said below
- send_space: int32 [128, 2, 2, 2], P('space', 'tm'), may hold values from -1 to 1, as said below
- send_time: int32 [128, 2, 4], P('space', 'tm'), may hold values from -1 to 5, as said below
Outputs:
- grad_features: bfloat16 [128, 2, 2, 512, 128], P('space', 'tm')
- grad_first: float32 [27, 128, 128], replicated
- grad_second: float32 [27, 128, 128], replicated
Inputs may be any that keep to these rules, and one draw needn't show every extreme that they name: `occupancy`: each device has 1 to 2 active blocks, which come first; on some device all 2 are active. Blocks after the active ones have no occupied voxels. `neighbors`: entries index the extended list of 10 slots; -1 where the neighbouring block is inactive or outside the grid, and in every row of an inactive block. The relation is symmetric: a block's neighbour in one direction has it as neighbour in the opposite direction. `send_space`: positions follow the face's cells; -1 where the cell holds no active block. `send_time`: positions follow the face's cells including one block beyond each slab side, and index the own-plus-space list of 6 slots; -1 where the cell holds no active block or lies outside the grid.
All inputs are finite; a program needn't handle non-finite values.
Results may differ from a plain program's by a relative error of at most 0.0029.
Values may be sent and summed in bfloat16 or wider, within the bound.
No kernel may reach another device: no remote copies, remote signals or barrier semaphores. Data moves between devices by JAX's collectives and lax.ppermute only.
A program may use at most 128 MiB of HBM per device.

v0:
```python
import math

import jax
import jax.numpy as jnp
from jax import lax
from jax.sharding import PartitionSpec as P

EDGE = 8


offsets = [
    (first, second, third) for first in (-1, 0, 1) for second in (-1, 0, 1) for third in (-1, 0, 1)
]


def extended(value, sides, width):
    for axis, dim in sides:
        size, length = (lax.axis_size(axis), value.shape[dim])
        up = [(i, (i + 1) % size) for i in range(size - 1)]
        down = [(j, i) for i, j in up]
        last = lax.slice_in_dim(value, length - width, length, axis=dim)
        initial = lax.slice_in_dim(value, 0, width, axis=dim)
        before = lax.ppermute(last, axis, up)
        after = lax.ppermute(initial, axis, down)
        value = jnp.concatenate([before, value, after], axis=dim)
    return value


def partner(value, axis, bit):
    return lax.ppermute(value, axis, [(i, i ^ 1 << bit) for i in range(lax.axis_size(axis))])


def rim_spans(component, block_edge):
    if component < 0:
        return (slice(block_edge - 1, block_edge), slice(0, 1))
    if component == 0:
        return (slice(0, block_edge), slice(1, block_edge + 1))
    return (slice(0, 1), slice(block_edge + 1, block_edge + 2))


def assemble(store, table, block_edge):
    total_rows = store.shape[0]
    padded = jnp.concatenate([store, jnp.zeros((1,) + store.shape[1:], store.dtype)], axis=0)
    safe_rows = jnp.where(table < 0, total_rows, table)
    pieces = {}
    for number, offset in enumerate(offsets):
        source = [rim_spans(component, block_edge)[0] for component in offset]
        pieces[offset] = jnp.take(
            padded[:, source[0], source[1], source[2]], safe_rows[:, number], axis=0
        )
    layers = []
    for first in (-1, 0, 1):
        columns = []
        for second in (-1, 0, 1):
            columns.append(
                jnp.concatenate([pieces[first, second, third] for third in (-1, 0, 1)], axis=3)
            )
        layers.append(jnp.concatenate(columns, axis=2))
    return jnp.concatenate(layers, axis=1)


def window(canvas, offset, block_edge):
    starts = [1 + component for component in offset]
    region = canvas[
        :,
        starts[0] : starts[0] + block_edge,
        starts[1] : starts[1] + block_edge,
        starts[2] : starts[2] + block_edge,
    ]
    return region.reshape(-1, canvas.shape[-1])


def negate(offset):
    return tuple((-component for component in offset))


def dot_transposed(left, weight):
    return lax.dot_general(
        left, weight, (((1,), (1,)), ((), ())), preferred_element_type=jnp.float32
    )


def dot_outer(left, right):
    return lax.dot_general(
        left, right, (((0,), (0,)), ((), ())), preferred_element_type=jnp.float32
    )


def pick_rows(source, row_index, along_axis):
    size_along = source.shape[along_axis]
    zero_shape = list(source.shape)
    zero_shape[along_axis] = 1
    padded = jnp.concatenate([source, jnp.zeros(zero_shape, source.dtype)], axis=along_axis)
    return jnp.take(padded, jnp.where(row_index < 0, size_along, row_index), axis=along_axis)


def local_pass(x_tile, g_tile, mask_rows, w_first, w_second, block_edge):
    rows = mask_rows.shape[0]
    channels = w_first.shape[-1]
    pre = jnp.zeros((rows, channels), jnp.float32)
    for number, offset in enumerate(offsets):
        pre = pre + jnp.dot(
            window(x_tile, offset, block_edge), w_first[number], preferred_element_type=jnp.float32
        )
    sigmoid_pre = jax.nn.sigmoid(pre)
    hidden = (pre * sigmoid_pre * mask_rows).astype(jnp.bfloat16)
    grad_hidden = jnp.zeros((rows, channels), jnp.float32)
    second_terms = []
    for number, offset in enumerate(offsets):
        back_window = window(g_tile, negate(offset), block_edge)
        grad_hidden = grad_hidden + dot_transposed(back_window, w_second[number])
        second_terms.append(dot_outer(hidden, back_window))
    grad_pre = (grad_hidden * sigmoid_pre * (1.0 + pre * (1.0 - sigmoid_pre)) * mask_rows).astype(
        jnp.bfloat16
    )
    first_terms = [dot_outer(window(x_tile, offset, block_edge), grad_pre) for offset in offsets]
    return (grad_pre, jnp.stack(first_terms), jnp.stack(second_terms))


def body(features, cotangent, w_first, w_second, occupancy, neighbors, send_space, send_time):
    blocks, voxels, channels = (features.shape[2], features.shape[3], features.shape[4])
    block_edge = EDGE
    rim_slots = send_space.shape[3]
    mask_rows = occupancy.reshape(blocks * voxels, 1).astype(jnp.float32)
    mask_cells = occupancy.reshape(blocks, voxels, 1).astype(jnp.bfloat16)
    masked_x = features.reshape(blocks, voxels, channels) * mask_cells
    masked_g = cotangent.reshape(blocks, voxels, channels) * mask_cells
    space_sends = send_space.reshape(2, rim_slots)
    time_sends = send_time.reshape(-1)
    table = neighbors.reshape(blocks, neighbors.shape[3])
    paired = jnp.stack([masked_x, masked_g]).reshape(
        2, blocks, block_edge, block_edge, block_edge, channels
    )
    outgoing = pick_rows(paired, space_sends, 1)
    bordered = extended(outgoing, (("space", 1),), 1)
    below = bordered[:, 0]
    above = bordered[:, 3]
    base = jnp.concatenate([paired, below, above], axis=1)
    toward_time = pick_rows(base, time_sends, 1)
    across = partner(toward_time, "tm", 0)
    shaped = jnp.concatenate([base, across], axis=1)
    x_tile = assemble(shaped[0], table, block_edge)
    g_tile = assemble(shaped[1], table, block_edge)
    grad_pre, first_part, second_part = local_pass(
        x_tile, g_tile, mask_rows, w_first, w_second, block_edge
    )
    da_cells = grad_pre.reshape(blocks, block_edge, block_edge, block_edge, channels)
    da_out = pick_rows(da_cells, space_sends, 0)
    da_border = extended(da_out, (("space", 0),), 1)
    da_below = da_border[0]
    da_above = da_border[3]
    da_base = jnp.concatenate([da_cells, da_below, da_above], axis=0)
    da_toward = pick_rows(da_base, time_sends, 0)
    da_across = partner(da_toward, "tm", 0)
    da_store = jnp.concatenate([da_base, da_across], axis=0)
    da_tile = assemble(da_store, table, block_edge)
    conv_rows = jnp.zeros((blocks * voxels, channels), jnp.float32)
    for number, offset in enumerate(offsets):
        conv_rows = conv_rows + dot_transposed(
            window(da_tile, negate(offset), block_edge), w_first[number]
        )
    grad_rows = (
        cotangent.reshape(blocks * voxels, channels).astype(jnp.float32) + conv_rows * mask_rows
    )
    grad_features = grad_rows.astype(jnp.bfloat16).reshape(features.shape)
    scale = 1.0 / math.sqrt(lax.axis_size("space") * lax.axis_size("tm") * blocks * voxels)
    first_sum, second_sum = lax.psum((first_part, second_part), ("space", "tm"))
    return (grad_features, first_sum * scale, second_sum * scale)


def solution(mesh):
    placed = (
        P("space", "tm", None, None, None),
        P("space", "tm", None, None, None),
        P(),
        P(),
        P("space", "tm", None, None),
        P("space", "tm", None, None),
        P("space", "tm", None, None),
        P("space", "tm", None),
    )
    return jax.shard_map(
        body,
        mesh=mesh,
        in_specs=placed,
        out_specs=(P("space", "tm", None, None, None), P(), P()),
        check_vma=False,
    )
```

profile of v0, /device:TPU:1, one launch (start us, length us, event | category | flops | bytes accessed | tf_op | source)
XLA Modules:
  0.0 581.5 jit_solution(6243704931924489264)
XLA Ops:
  13.6 6.2 %collective-permute-start = (bf16[2,1,2,8,8,8,128]{6,5,4,3,2,0,1:T(8,128)(2,1)S(1)}, bf16[2,1,2,8,8,8,128]{6,5,4,3,2,0,1:T(8,128)(2,1)S(1)}, u32[]{:S(2)}, u32[]{:S(2)}) collective-permute-start(bf16[2,1,2,8,8,8,128]{6,5,4,3,2,0,1:T(8,128)(2,1)S(1)} %get-tuple-element.121), channel_id=1, source_target_pairs={{0,2},{2,4},{4,6},{6,8},{8,10},{10,12},{12,14},{14,16},{16,18},{18... | collective-permute-start | bytes 1572872 | tf_op jit(solution)/shard_map/ppermute | solution.py:23
  19.8 1.9 collective-permute-start.1
  49.3 19.2 %collective-permute-done.2 = bf16[2,4,8,8,8,128]{5,4,3,2,0,1:T(8,128)(2,1)S(1)} collective-permute-done((bf16[2,4,8,8,8,128]{5,4,3,2,0,1:T(8,128)(2,1)S(1)}, bf16[2,4,8,8,8,128]{5,4,3,2,0,1:T(8,128)(2,1)S(1)}, u32[]{:S(2)}, u32[]{:S(2)}) %collective-permute-start.2) | collective-permute-done | bytes 1048608 | tf_op jit(solution)/shard_map/ppermute | solution.py:30
  69.6 2.3 slice_bitcast_fusion
  85.9 2.0 gather_fusion.6
  87.9 2.2 gather_fusion.41
  90.1 2.2 gather_fusion.5
  112.3 2.0 gather_fusion.50
  114.3 2.0 gather_fusion.14
  124.7 2.0 gather_fusion.54
  126.7 2.0 gather_fusion.18
  128.7 2.0 gather_fusion.20
  130.7 2.0 gather_fusion.56
  132.7 2.2 gather_fusion.53
  134.9 2.2 gather_fusion.17
  139.9 2.0 gather_fusion.48
  141.9 2.0 gather_fusion.12
  145.1 2.2 gather_fusion.11
  152.5 1.7 copy.294
  160.3 1.6 gather_fusion.45
  188.8 1.6 gather_fusion.35
  207.0 1.6 gather_fusion.26
  280.0 5.8 collective-permute-start.3
  285.7 1.9 collective-permute-start.4
  289.5 5.5 collective-permute-done.4
  297.8 9.3 %collective-permute-done.5 = bf16[4,8,8,8,128]{4,3,2,1,0:T(8,128)(2,1)} collective-permute-done((bf16[4,8,8,8,128]{4,3,2,1,0:T(8,128)(2,1)}, bf16[4,8,8,8,128]{4,3,2,1,0:T(8,128)(2,1)}, u32[]{:S(2)}, u32[]{:S(2)}) %collective-permute-start.5) | collective-permute-done | bytes 524320 | tf_op jit(solution)/shard_map/ppermute | solution.py:30
  314.1 1.7 gather_fusion.59
  321.1 1.6 gather_fusion.80
  323.5 1.6 gather_fusion.65
  340.5 1.6 gather_fusion.71
  360.0 210.1 %all-reduce.7.cloned.1.call-done = (f32[27,128,128]{2,1,0:T(8,128)}, f32[27,128,128]{2,1,0:T(8,128)}) async-done(((f32[27,128,128]{2,1,0:T(8,128)}, f32[27,128,128]{2,1,0:T(8,128)}), (f32[27,128,128]{2,1,0:T(8,128)}, f32[27,128,128]{2,1,0:T(8,128)})) %all-reduce.7.cloned.1.call-update) | async-done | bytes 3538960 | tf_op jit(solution)/shard_map/psum | solution.py:167
  570.0 3.0 broadcast_multiply_fusion
  (725 shorter events, 257.4 us)
Async XLA Ops:
  7.2 562.9 %all-reduce.7.cloned.1.call-start = ((), (), s32[]{:S(2)}) async-start(), calls=%async_computation | async-start | bytes 7077888 | tf_op jit(solution)/shard_map/psum | solution.py:167
  13.6 29.5 %collective-permute-start = (bf16[2,1,2,8,8,8,128]{6,5,4,3,2,0,1:T(8,128)(2,1)S(1)}, bf16[2,1,2,8,8,8,128]{6,5,4,3,2,0,1:T(8,128)(2,1)S(1)}, u32[]{:S(2)}, u32[]{:S(2)}) collective-permute-start(bf16[2,1,2,8,8,8,128]{6,5,4,3,2,0,1:T(8,128)(2,1)S(1)} %get-tuple-element.121), channel_id=1, source_target_pairs={{0,2},{2,4},{4,6},{6,8},{8,10},{10,12},{12,14},{14,16},{16,18},{18... | collective-permute-start | bytes 1572872 | tf_op jit(solution)/shard_map/ppermute | solution.py:23
  19.8 23.3 %collective-permute-start.1 = (bf16[2,1,2,8,8,8,128]{6,5,4,3,2,0,1:T(8,128)(2,1)S(1)}, bf16[2,1,2,8,8,8,128]{6,5,4,3,2,0,1:T(8,128)(2,1)S(1)}, u32[]{:S(2)}, u32[]{:S(2)}) collective-permute-start(bf16[2,1,2,8,8,8,128]{6,5,4,3,2,0,1:T(8,128)(2,1)S(1)} %get-tuple-element.120), channel_id=1, source_target_pairs={{2,0},{4,2},{6,4},{8,6},{10,8},{12,10},{14,12},{16,14},{18,16},{20... | collective-permute-start | bytes 1572872 | tf_op jit(solution)/shard_map/ppermute | solution.py:24
  21.7 23.3 %copy-start.122 = (pred[4]{0:T(512)(128)(4,1)}, pred[4]{0:T(512)(128)(4,1)S(1)}, u32[]{:S(2)}) copy-start(pred[4]{0:T(512)(128)(4,1)S(1)} %compare_and_fusion.27) | copy-start | bytes 16
  28.8 15.4 %copy-start.104 = (s32[1024]{0:T(1024)}, s32[1024]{0:T(1024)S(1)}, u32[]{:S(2)}) copy-start(s32[1024]{0:T(1024)S(1)} %pad_clamp_fusion.27) | copy-start | bytes 12292
  45.2 23.3 %collective-permute-start.2 = (bf16[2,4,8,8,8,128]{5,4,3,2,0,1:T(8,128)(2,1)S(1)}, bf16[2,4,8,8,8,128]{5,4,3,2,0,1:T(8,128)(2,1)S(1)}, u32[]{:S(2)}, u32[]{:S(2)}) collective-permute-start(bf16[2,4,8,8,8,128]{5,4,3,2,0,1:T(8,128)(2,1)S(1)} %select_bitcast_fusion), channel_id=1, source_target_pairs={{0,1},{1,0},{2,3},{3,2},{4,5},{5,4},{6,7},{7,6},{8,9},{9,8},{10,11... | collective-permute-start | bytes 3145736 | tf_op jit(solution)/shard_map/ppermute | solution.py:30
  152.5 11.6 %copy-start.86 = (bf16[2,8,128]{2,1,0:T(8,128)(2,1)S(1)}, bf16[2,8,128]{2,1,0:T(8,128)(2,1)}, u32[]{:S(2)}) copy-start(bf16[2,8,128]{2,1,0:T(8,128)(2,1)} %gather_fusion.42) | copy-start | bytes 12292
  152.5 11.6 %copy-start.87 = (bf16[2,8,128]{2,1,0:T(8,128)(2,1)S(1)}, bf16[2,8,128]{2,1,0:T(8,128)(2,1)}, u32[]{:S(2)}) copy-start(bf16[2,8,128]{2,1,0:T(8,128)(2,1)} %gather_fusion.6) | copy-start | bytes 12292
  157.1 14.7 %copy-start.66 = (bf16[2,8,8,128]{3,2,1,0:T(8,128)(2,1)S(1)}, bf16[2,8,8,128]{3,2,1,0:T(8,128)(2,1)}, u32[]{:S(2)}) copy-start(bf16[2,8,8,128]{3,2,1,0:T(8,128)(2,1)} %gather_fusion.53) | copy-start | bytes 98308
  157.1 14.7 %copy-start.67 = (bf16[2,8,8,128]{3,2,1,0:T(8,128)(2,1)S(1)}, bf16[2,8,8,128]{3,2,1,0:T(8,128)(2,1)}, u32[]{:S(2)}) copy-start(bf16[2,8,8,128]{3,2,1,0:T(8,128)(2,1)} %gather_fusion.17) | copy-start | bytes 98308
  158.5 14.7 %copy-start.68 = (bf16[2,8,8,128]{3,2,1,0:T(8,128)(2,1)S(1)}, bf16[2,8,8,128]{3,2,1,0:T(8,128)(2,1)}, u32[]{:S(2)}) copy-start(bf16[2,8,8,128]{3,2,1,0:T(8,128)(2,1)} %gather_fusion.47) | copy-start | bytes 98308
  158.6 14.7 %copy-start.69 = (bf16[2,8,8,128]{3,2,1,0:T(8,128)(2,1)S(1)}, bf16[2,8,8,128]{3,2,1,0:T(8,128)(2,1)}, u32[]{:S(2)}) copy-start(bf16[2,8,8,128]{3,2,1,0:T(8,128)(2,1)} %gather_fusion.11) | copy-start | bytes 98308
  280.0 9.5 %collective-permute-start.3 = (bf16[1,2,8,8,8,128]{5,4,3,2,1,0:T(8,128)(2,1)S(1)}, bf16[1,2,8,8,8,128]{5,4,3,2,1,0:T(8,128)(2,1)S(1)}, u32[]{:S(2)}, u32[]{:S(2)}) collective-permute-start(bf16[1,2,8,8,8,128]{5,4,3,2,1,0:T(8,128)(2,1)S(1)} %get-tuple-element.195), channel_id=1, source_target_pairs={{0,2},{2,4},{4,6},{6,8},{8,10},{10,12},{12,14},{14,16},{16,18},{18... | collective-permute-start | bytes 786440 | tf_op jit(solution)/shard_map/ppermute | solution.py:23
  285.7 9.2 %collective-permute-start.4 = (bf16[1,2,8,8,8,128]{5,4,3,2,1,0:T(8,128)(2,1)S(1)}, bf16[1,2,8,8,8,128]{5,4,3,2,1,0:T(8,128)(2,1)S(1)}, u32[]{:S(2)}, u32[]{:S(2)}) collective-permute-start(bf16[1,2,8,8,8,128]{5,4,3,2,1,0:T(8,128)(2,1)S(1)} %get-tuple-element.194), channel_id=1, source_target_pairs={{2,0},{4,2},{6,4},{8,6},{10,8},{12,10},{14,12},{16,14},{18,16},{20... | collective-permute-start | bytes 786440 | tf_op jit(solution)/shard_map/ppermute | solution.py:24
  296.8 10.3 %collective-permute-start.5 = (bf16[4,8,8,8,128]{4,3,2,1,0:T(8,128)(2,1)}, bf16[4,8,8,8,128]{4,3,2,1,0:T(8,128)(2,1)}, u32[]{:S(2)}, u32[]{:S(2)}) collective-permute-start(bf16[4,8,8,8,128]{4,3,2,1,0:T(8,128)(2,1)} %broadcast_select_fusion), channel_id=1, source_target_pairs={{0,1},{1,0},{2,3},{3,2},{4,5},{5,4},{6,7},{7,6},{8,9},{9,8},{10,11... | collective-permute-start | bytes 1572872 | tf_op jit(solution)/shard_map/ppermute | solution.py:30
  314.1 11.7 %copy-start.64 = (bf16[11,1,8,1,128]{4,3,2,1,0:T(2,128)(2,1)S(1)}, bf16[11,1,8,1,128]{4,3,2,1,0:T(2,128)(2,1)}, u32[]{:S(2)}) copy-start(bf16[11,1,8,1,128]{4,3,2,1,0:T(2,128)(2,1)} %get-tuple-element.54) | copy-start | bytes 67588
  314.1 13.2 %copy-start.63 = (bf16[11,1,8,1,128]{4,3,2,1,0:T(2,128)(2,1)S(1)}, bf16[11,1,8,1,128]{4,3,2,1,0:T(2,128)(2,1)}, u32[]{:S(2)}) copy-start(bf16[11,1,8,1,128]{4,3,2,1,0:T(2,128)(2,1)} %get-tuple-element.55) | copy-start | bytes 67588
  314.1 13.9 %copy-start.96 = (pred[2]{0:T(512)(128)(4,1)S(1)}, pred[2]{0:T(512)(128)(4,1)}, u32[]{:S(2)}) copy-start(pred[2]{0:T(512)(128)(4,1)} %get-tuple-element.271) | copy-start | bytes 10
  314.1 14.0 %copy-start.62 = (bf16[11,8,1,1,128]{4,3,2,1,0:T(2,128)(2,1)S(1)}, bf16[11,8,1,1,128]{4,3,2,1,0:T(2,128)(2,1)}, u32[]{:S(2)}) copy-start(bf16[11,8,1,1,128]{4,3,2,1,0:T(2,128)(2,1)} %get-tuple-element.61) | copy-start | bytes 67588
  314.1 14.7 %copy-start.124 = (pred[2]{0:T(512)(128)(4,1)S(1)}, pred[2]{0:T(512)(128)(4,1)}, u32[]{:S(2)}) copy-start(pred[2]{0:T(512)(128)(4,1)} %compare_and_fusion.19) | copy-start | bytes 10
  314.1 14.8 %copy-start.61 = (bf16[11,8,1,1,128]{4,3,2,1,0:T(2,128)(2,1)S(1)}, bf16[11,8,1,1,128]{4,3,2,1,0:T(2,128)(2,1)}, u32[]{:S(2)}) copy-start(bf16[11,8,1,1,128]{4,3,2,1,0:T(2,128)(2,1)} %get-tuple-element.62) | copy-start | bytes 67588
  314.1 15.4 %copy-start.111 = (pred[2]{0:T(512)(128)(4,1)S(1)}, pred[2]{0:T(512)(128)(4,1)}, u32[]{:S(2)}) copy-start(pred[2]{0:T(512)(128)(4,1)} %get-tuple-element.298) | copy-start | bytes 10
  315.8 15.3 %copy-start.94 = (pred[2]{0:T(512)(128)(4,1)S(1)}, pred[2]{0:T(512)(128)(4,1)}, u32[]{:S(2)}) copy-start(pred[2]{0:T(512)(128)(4,1)} %get-tuple-element.269) | copy-start | bytes 10
  315.8 16.8 %copy-start.92 = (pred[2]{0:T(512)(128)(4,1)S(1)}, pred[2]{0:T(512)(128)(4,1)}, u32[]{:S(2)}) copy-start(pred[2]{0:T(512)(128)(4,1)} %get-tuple-element.275) | copy-start | bytes 10
  315.8 16.8 %copy-start.76 = (bf16[11,1,1,1,128]{4,3,2,1,0:T(2,128)(2,1)S(1)}, bf16[11,1,1,1,128]{4,3,2,1,0:T(2,128)(2,1)}, u32[]{:S(2)}) copy-start(bf16[11,1,1,1,128]{4,3,2,1,0:T(2,128)(2,1)} %get-tuple-element.43) | copy-start | bytes 8452
  315.8 17.5 %copy-start.101 = (pred[2]{0:T(512)(128)(4,1)S(1)}, pred[2]{0:T(512)(128)(4,1)}, u32[]{:S(2)}) copy-start(pred[2]{0:T(512)(128)(4,1)} %get-tuple-element.268) | copy-start | bytes 10
  315.9 17.5 %copy-start.75 = (bf16[11,1,1,1,128]{4,3,2,1,0:T(2,128)(2,1)S(1)}, bf16[11,1,1,1,128]{4,3,2,1,0:T(2,128)(2,1)}, u32[]{:S(2)}) copy-start(bf16[11,1,1,1,128]{4,3,2,1,0:T(2,128)(2,1)} %get-tuple-element.44) | copy-start | bytes 8452
  315.9 18.2 %copy-start.103 = (pred[2]{0:T(512)(128)(4,1)S(1)}, pred[2]{0:T(512)(128)(4,1)}, u32[]{:S(2)}) copy-start(pred[2]{0:T(512)(128)(4,1)} %get-tuple-element.270) | copy-start | bytes 10
  315.9 18.3 %copy-start.74 = (bf16[11,1,1,1,128]{4,3,2,1,0:T(2,128)(2,1)S(1)}, bf16[11,1,1,1,128]{4,3,2,1,0:T(2,128)(2,1)}, u32[]{:S(2)}) copy-start(bf16[11,1,1,1,128]{4,3,2,1,0:T(2,128)(2,1)} %get-tuple-element.45) | copy-start | bytes 8452
  315.9 19.0 %copy-start.99 = (pred[2]{0:T(512)(128)(4,1)S(1)}, pred[2]{0:T(512)(128)(4,1)}, u32[]{:S(2)}) copy-start(pred[2]{0:T(512)(128)(4,1)} %get-tuple-element.274) | copy-start | bytes 10
  315.9 19.0 %copy-start.73 = (bf16[11,1,1,1,128]{4,3,2,1,0:T(2,128)(2,1)S(1)}, bf16[11,1,1,1,128]{4,3,2,1,0:T(2,128)(2,1)}, u32[]{:S(2)}) copy-start(bf16[11,1,1,1,128]{4,3,2,1,0:T(2,128)(2,1)} %get-tuple-element.42) | copy-start | bytes 8452
  315.9 19.7 %copy-start.119 = (pred[2]{0:T(512)(128)(4,1)S(1)}, pred[2]{0:T(512)(128)(4,1)}, u32[]{:S(2)}) copy-start(pred[2]{0:T(512)(128)(4,1)} %get-tuple-element.276) | copy-start | bytes 10
  (101 other events, 289.5 us)
Sparse Core Ops, SparseCore 0:
  297.8 272.2 all-reduce.6
where the time goes:
time: 591 us; the launch traced here: 581 us
  waiting for transfers between devices  244 us (41%)
  local copies, waits for them, and re-layouts  168 us (28%)
  matrix products  71.5 us (12%)
  other arithmetic  63.4 us (11%)
  starting transfers between devices  17.3 us (3%)
  between operations  17 us (3%)
    psum x1, waiting for transfers between devices, body(): first_sum, second_sum = lax.psum((first_part, second_part), ('space', 'tm'))  210 us
    gather x81, local copies, waits for them, and re-layouts, assemble(): jnp.take(padded[:, source[0], source[1], source[2]], safe_rows[:, number]...  97.2 us
    dot_general x54, matrix products, dot_transposed(): lax.dot_general(left, weight, (((1,), (1,)), ((), ())), preferred_element...  34.2 us
    unnamed x313, local copies, waits for them, and re-layouts  33.7 us
    dot_general x54, matrix products, dot_outer(): lax.dot_general(left, right, (((0,), (0,)), ((), ())), preferred_element_...  31.7 us
    ppermute x2, waiting for transfers between devices, partner(): lax.ppermute(value, axis, [(i, i ^ 1 << bit) for i in range(lax.axis_size...  28.5 us
    select_n x81, other arithmetic, assemble(): jnp.take(padded[:, source[0], source[1], source[2]], safe_rows[:, number]...  22.3 us
    gather x23, other arithmetic  13.7 us
  transfers between devices with their start and end apart: 7, of which 4 were waited for; matrix products, arithmetic and copies ran while one was open for 13% of the time, Pallas kernels for 0%

commit v1 on v0

v1 whole, which is shorter than its diff:
```python
import functools
import math

import jax
import jax.numpy as jnp
from jax import lax
from jax.experimental import pallas as pl
from jax.experimental.pallas import tpu as pltpu
from jax.sharding import Mesh
from jax.sharding import PartitionSpec as P

SPLIT = {"z": 8, "x": 4, "yh": 2, "c": 2}
SPACE = ("z", "x", "yh", "c")
TIME = "yl"
PLANE = ("x", "yh", "yl")

E = 8
CH = 128
FACE = E * E
VOX = E * FACE
BLK = 2
ROWS = BLK * VOX
BF = jnp.bfloat16
F32 = jnp.float32

WINDOWS = [(dt, dx) for dt in (-1, 0, 1) for dx in (-1, 0, 1)]

VM = pl.BlockSpec(memory_space=pltpu.VMEM)
SM = pl.BlockSpec(memory_space=pltpu.SMEM)
PARAMS = pltpu.CompilerParams(vmem_limit_bytes=56 * 1024 * 1024)


def pick(index, options, shape, dtype):
    value = jnp.zeros(shape, dtype)
    for number, option in options:
        value = jnp.where(index == number, option, value)
    return value


def store_faces(values, sends, half, refs):
    prev_ref, next_ref, time_ref, prev_diag, next_diag = refs
    for i, blocks in enumerate(values):
        planes = [block.reshape(E, FACE, CH) for block in blocks]
        lows = [plane[:, :E].reshape(FACE, CH) for plane in planes]
        highs = [plane[:, FACE - E :].reshape(FACE, CH) for plane in planes]
        times = [jnp.where(half == 0, plane[E - 1], plane[0]) for plane in planes]
        for slot in range(BLK):
            time_ref[i, slot] = times[slot].astype(time_ref.dtype)
            low, high = sends[0, slot], sends[1, slot]
            prev_ref[i, slot] = pick(low, list(enumerate(lows)), (FACE, CH), F32).astype(BF)
            next_ref[i, slot] = pick(high, list(enumerate(highs)), (FACE, CH), F32).astype(BF)
            prev_diag[i, slot] = pick(
                low, [(b, t[:E]) for b, t in enumerate(times)], (E, CH), F32
            ).astype(BF)
            next_diag[i, slot] = pick(
                high, [(b, t[FACE - E :]) for b, t in enumerate(times)], (E, CH), F32
            ).astype(BF)


def face_shapes(n):
    return [
        jax.ShapeDtypeStruct((n, BLK, rows, CH), BF) for rows in (FACE, FACE, FACE, E, E)
    ]


def pack_kernel(sends, half, f_ref, g_ref, occ_ref, xg_ref, mask_ref, *faces):
    values = [[], []]
    for b in range(BLK):
        row = occ_ref[b : b + 1, :].astype(F32)
        mask = jnp.broadcast_to(row, (CH, VOX)).T
        mask_ref[b] = mask
        for i, ref in enumerate((f_ref, g_ref)):
            masked = ref[b].astype(F32) * mask
            xg_ref[i, b] = masked.astype(BF)
            values[i].append(masked)
    store_faces(values, sends, half[0], faces)


def build(tile, n, own, table, peer, halos):
    below, above, across, below_diag, above_diag = halos
    end = FACE + E
    for b in range(BLK):
        for i in range(n):
            tile[i, b, 1 : E + 1, E:end] = own[i, b].astype(F32).reshape(E, FACE, CH)
    for b in range(BLK):
        for dt in (-1, 0, 1):
            for dx in (-1, 0, 1):
                if dt == 0 and dx == 0:
                    continue
                slot = table[b, (dt + 1) * 9 + (dx + 1) * 3 + 1]
                side, side_diag = (below, below_diag) if dx < 0 else (above, above_diag)
                first = BLK if dx < 0 else 2 * BLK
                far = peer[jnp.clip(slot - 3 * BLK, 0, 2 * BLK - 1)]
                far = jnp.where(slot >= 3 * BLK, far, -1)
                for i in range(n):
                    if dt == 0:
                        rows = slice(FACE - E, FACE) if dx < 0 else slice(0, E)
                        where = slice(0, E) if dx < 0 else slice(end, end + E)
                        value = jnp.zeros((E, E, CH), F32)
                        for j in range(BLK):
                            face = own[i, j].astype(F32).reshape(E, FACE, CH)[:, rows]
                            value = jnp.where(slot == j, face, value)
                            halo = side[i, j].astype(F32).reshape(E, E, CH)
                            value = jnp.where(slot == first + j, halo, value)
                        tile[i, b, 1 : E + 1, where] = value
                        continue
                    plane = slice(VOX - FACE, VOX) if dt < 0 else slice(0, FACE)
                    to = 0 if dt < 0 else E + 1
                    if dx == 0:
                        value = jnp.zeros((FACE, CH), F32)
                        for j in range(BLK):
                            value = jnp.where(slot == j, own[i, j, plane].astype(F32), value)
                            value = jnp.where(far == j, across[i, j].astype(F32), value)
                        tile[i, b, to, E:end] = value
                        continue
                    rows = slice(FACE - E, FACE) if dx < 0 else slice(0, E)
                    where = slice(0, E) if dx < 0 else slice(end, end + E)
                    value = jnp.zeros((E, CH), F32)
                    for j in range(BLK):
                        edge = own[i, j, plane].astype(F32)[rows]
                        value = jnp.where(slot == j, edge, value)
                        edge = side[i, j].astype(F32)
                        edge = edge[FACE - E :] if dt < 0 else edge[:E]
                        value = jnp.where(slot == first + j, edge, value)
                        edge = across[i, j].astype(F32)[rows]
                        value = jnp.where(far == j, edge, value)
                        value = jnp.where(far == first + j, side_diag[i, j].astype(F32), value)
                    tile[i, b, to, where] = value


def columns(tile, i, sign, cols):
    for w, (dt, dx) in enumerate(WINDOWS):
        t, x = 1 + sign * dt, E * (1 + sign * dx)
        for b in range(BLK):
            window = tile[i, b, t : t + E, x : x + FACE].reshape(VOX, CH)
            cols[b * VOX : (b + 1) * VOX, w * CH : (w + 1) * CH] = window.astype(BF)


def shift(value, step):
    y = lax.broadcasted_iota(jnp.int32, value.shape, 0) % E
    moved = pltpu.roll(value, (-step) % value.shape[0], 0)
    return jnp.where(y == (E - 1 if step > 0 else 0), 0.0, moved)


def lanes(value, dy):
    return value[:, (dy + 1) * CH : (dy + 2) * CH]


def gather_y(parts, sign):
    return lanes(parts, 0) + shift(lanes(parts, 1), sign) + shift(lanes(parts, -1), -sign)


def transposed(cols, w_ref, wide):
    for k in range(27):
        w, d = divmod(k, 3)
        wide[d * CH : (d + 1) * CH, w * CH : (w + 1) * CH] = w_ref[k]
    parts = lax.dot_general(
        cols[...], wide[...], (((1,), (1,)), ((), ())), preferred_element_type=F32
    )
    return gather_y(parts, -1)


def outer(left, right):
    return lax.dot_general(left, right, (((0,), (0,)), ((), ())), preferred_element_type=F32)


def local_kernel(
    table, peer, sends, half, core, xg, mask_ref, w1, w2, h0, h1, h2, h3, h4,
    gp_ref, keep_ref, send_ref, f0, f1, f2, f3, f4, tile, xcol, gcol, wide, tall,
):
    build(tile, 2, xg, table, peer, (h0, h1, h2, h3, h4))
    columns(tile, 0, 1, xcol)
    columns(tile, 1, -1, gcol)
    mask = mask_ref[...].reshape(ROWS, CH)
    for k in range(27):
        w, d = divmod(k, 3)
        tall[w * CH : (w + 1) * CH, d * CH : (d + 1) * CH] = w1[k]
    parts = jnp.dot(xcol[...], tall[...], preferred_element_type=F32)
    pre = gather_y(parts, 1)
    sig = jax.nn.sigmoid(pre)
    hidden = (pre * sig * mask).astype(BF).astype(F32)
    shifted = jnp.concatenate([shift(hidden, -1), hidden, shift(hidden, 1)], axis=1).astype(BF)
    second = outer(shifted, gcol[...])
    grad_hidden = transposed(gcol, w2, wide)
    grad_pre = (grad_hidden * sig * (1.0 + pre * (1.0 - sig)) * mask).astype(BF)
    gp_ref[...] = grad_pre.reshape(1, BLK, VOX, CH)
    grad_pre = grad_pre.astype(F32)
    blocks = [[grad_pre[b * VOX : (b + 1) * VOX] for b in range(BLK)]]
    store_faces(blocks, sends, half[0], (f0, f1, f2, f3, f4))
    shifted = jnp.concatenate(
        [shift(grad_pre, 1), grad_pre, shift(grad_pre, -1)], axis=1
    ).astype(BF)
    first = outer(xcol[...], shifted)
    mine = core[0] == 0
    for k in range(27):
        w, d = divmod(k, 3)
        a = second[d * CH : (d + 1) * CH, w * CH : (w + 1) * CH]
        b = first[w * CH : (w + 1) * CH, d * CH : (d + 1) * CH]
        keep_ref[k] = jnp.where(mine, a, b)
        send_ref[k] = jnp.where(mine, b, a).astype(BF)


def input_kernel(
    table, peer, gp, mask_ref, cot, w1, h0, h1, h2, h3, h4, out, tile, dcol, wide
):
    build(tile, 1, gp, table, peer, (h0, h1, h2, h3, h4))
    columns(tile, 0, -1, dcol)
    total = transposed(dcol, w1, wide) * mask_ref[...].reshape(ROWS, CH)
    total = cot[...].astype(F32).reshape(ROWS, CH) + total
    out[...] = total.astype(BF).reshape(BLK, VOX, CH)


def pack(f, g, occ, sends, half):
    return pl.pallas_call(
        pack_kernel,
        out_shape=[
            jax.ShapeDtypeStruct((2, BLK, VOX, CH), BF),
            jax.ShapeDtypeStruct((BLK, VOX, CH), F32),
            *face_shapes(2),
        ],
        in_specs=[SM, SM, VM, VM, VM],
        out_specs=[VM] * 7,
        compiler_params=PARAMS,
        name="pack",
    )(sends, half, f, g, occ)


def local_pass(table, peer, sends, half, core, xg, mask, w1, w2, halos):
    return pl.pallas_call(
        local_kernel,
        out_shape=[
            jax.ShapeDtypeStruct((1, BLK, VOX, CH), BF),
            jax.ShapeDtypeStruct((27, CH, CH), F32),
            jax.ShapeDtypeStruct((27, CH, CH), BF),
            *face_shapes(1),
        ],
        in_specs=[SM] * 5 + [VM] * 9,
        out_specs=[VM] * 8,
        scratch_shapes=[
            pltpu.VMEM((2, BLK, E + 2, (E + 2) * E, CH), F32),
            pltpu.VMEM((ROWS, 9 * CH), BF),
            pltpu.VMEM((ROWS, 9 * CH), BF),
            pltpu.VMEM((3 * CH, 9 * CH), BF),
            pltpu.VMEM((9 * CH, 3 * CH), BF),
        ],
        compiler_params=PARAMS,
        name="local_pass",
    )(table, peer, sends, half, core, xg, mask, w1, w2, *halos)


def input_grad(table, peer, gp, mask, cot, w1, halos):
    return pl.pallas_call(
        input_kernel,
        out_shape=jax.ShapeDtypeStruct((BLK, VOX, CH), BF),
        in_specs=[SM] * 2 + [VM] * 9,
        out_specs=VM,
        scratch_shapes=[
            pltpu.VMEM((1, BLK, E + 2, (E + 2) * E, CH), F32),
            pltpu.VMEM((ROWS, 9 * CH), BF),
            pltpu.VMEM((3 * CH, 9 * CH), BF),
        ],
        compiler_params=PARAMS,
        name="input_grad",
    )(table, peer, gp, mask, cot, w1, *halos)


def swap(value, axis):
    return lax.ppermute(value, axis, [(0, 1), (1, 0)])


def exchange(faces):
    to_prev, to_next, to_time, to_prev_diag, to_next_diag = faces
    size = math.prod(lax.axis_size(axis) for axis in SPACE)
    up = [(i, i + 1) for i in range(size - 1)]
    down = [(i + 1, i) for i in range(size - 1)]
    cross = lambda pairs: [(2 * i + t, 2 * j + 1 - t) for i, j in pairs for t in (0, 1)]
    both = (*SPACE, TIME)
    return (
        lax.ppermute(to_next, SPACE, up),
        lax.ppermute(to_prev, SPACE, down),
        swap(to_time, TIME),
        lax.ppermute(to_next_diag, both, cross(up)),
        lax.ppermute(to_prev_diag, both, cross(down)),
    )


def spread(value, axes):
    size = math.prod(lax.axis_size(axis) for axis in axes)
    copies = jnp.broadcast_to(value[None], (size, *value.shape))
    return lax.all_to_all(copies, axes, 0, 0)


def reduce_all(keep, send, scale):
    total = keep + swap(send, "c").astype(F32)
    plane = math.prod(lax.axis_size(axis) for axis in PLANE)
    rows = 27 * CH // plane
    parts = lax.all_to_all(total.astype(BF).reshape(plane, rows, CH), PLANE, 0, 0)
    total = jnp.sum(parts.astype(F32), axis=0)
    depth = lax.axis_size("z")
    parts = lax.all_to_all(total.reshape(depth, rows // depth, CH), "z", 0, 0)
    total = (jnp.sum(parts, axis=0) * scale).astype(BF)
    total = spread(total, ("z",)).reshape(rows, CH)
    mine = spread(total, PLANE).reshape(27, CH, CH)
    other = swap(mine, "c")
    even = lax.axis_index("c") == 0
    second = jnp.where(even, mine, other).astype(F32)
    first = jnp.where(even, other, mine).astype(F32)
    return first, second


def body(features, cotangent, w_first, w_second, occupancy, neighbors, send_space, send_time):
    f, g = (a.reshape(BLK, VOX, CH) for a in (features, cotangent))
    half = lax.axis_index(TIME).astype(jnp.int32).reshape(1)
    core = lax.axis_index("c").astype(jnp.int32).reshape(1)
    sends = send_space.reshape(2, BLK)
    table = neighbors.reshape(BLK, 27)
    peer = swap(send_time.reshape(2 * BLK), TIME)
    xg, mask, *faces = pack(f, g, occupancy.reshape(BLK, VOX), sends, half)
    halos = exchange(faces)
    gp, keep, send, *faces = local_pass(
        table, peer, sends, half, core, xg, mask, w_first, w_second, halos
    )
    halos = exchange(faces)
    out = input_grad(table, peer, gp, mask, g, w_first, halos)
    devices = math.prod(lax.axis_size(axis) for axis in (*SPACE, TIME))
    first, second = reduce_all(keep, send, 1.0 / math.sqrt(devices * ROWS))
    return out.reshape(features.shape), first, second


def solution(mesh):
    fine = Mesh(
        mesh.devices.reshape(*SPLIT.values(), mesh.shape["tm"]), (*SPACE, TIME)
    )
    split = lambda rank: P(SPACE, TIME, *[None] * (rank - 2))
    return jax.shard_map(
        body,
        mesh=fine,
        in_specs=(
            split(5), split(5), P(), P(), split(4), split(4), split(4), split(3),
        ),
        out_specs=(split(5), P(), P()),
        check_vma=False,
    )
```

time: 591 us -> 140 us (0.24)
  the two profiles are of different devices: /device:TPU:1 before, /device:TPU:31 now
where the time goes in v1:
time: 140 us; the launch traced here: 139 us
  blocking collectives  57.6 us (41%)
  starting transfers between devices  41.1 us (29%)
  waiting for transfers between devices  18.6 us (13%)
  Pallas kernels  15.9 us (11%)
  other arithmetic  3.92 us (3%)
  local copies, waits for them, and re-layouts  1.42 us (1%)
    all_to_all x2, blocking collectives, spread(): return lax.all_to_all(copies, axes, 0, 0)  24.1 us
    all_to_all x1, blocking collectives, reduce_all(): parts = lax.all_to_all(total.reshape(depth, rows // depth, CH), 'z', 0, 0)  17.1 us
    all_to_all x1, blocking collectives, reduce_all(): lax.all_to_all(total.astype(BF).reshape(plane, rows, CH), PLANE, 0, 0)  16.4 us
    ppermute x2, starting transfers between devices, exchange(): lax.ppermute(to_next_diag, both, cross(up))  15.6 us
    ppermute x2, waiting for transfers between devices, exchange(): lax.ppermute(to_prev_diag, both, cross(down))  15.2 us
    ppermute x2, starting transfers between devices, exchange(): lax.ppermute(to_next, SPACE, up)  9.91 us
    pallas_call x1, Pallas kernels, local_pass(): pl.pallas_call(local_kernel, out_shape=[jax.ShapeDtypeStruct((1, BLK, VOX...  9.63 us
    ppermute x5, starting transfers between devices, swap(): return lax.ppermute(value, axis, [(0, 1), (1, 0)])  7.91 us
  transfers between devices with their start and end apart: 13, of which 4 were waited for; matrix products, arithmetic and copies ran while one was open for 0% of the time, Pallas kernels for 3%

profile of v1, /device:TPU:31, one launch (start us, length us, event | category | flops | bytes accessed | tf_op | source)
XLA Modules:
  0.0 139.5 jit_solution(11034682760842527108)
XLA Ops:
  0.6 2.3 %pack.1 = (bf16[2,2,512,128]{3,2,1,0:T(8,128)(2,1)}, f32[2,512,128]{2,1,0:T(8,128)}, bf16[2,2,64,128]{3,2,1,0:T(8,128)(2,1)}, bf16[2,2,64,128]{3,2,1,0:T(8,128)(...) custom-call(s32[2,2]{1,0:T(2,128)} %bitcast.19, ...), custom_call_target="tpu_custom_call" | custom-call | tf_op jit(solution)/shard_map/pack/pallas_call | solution.py:214
  2.9 4.7 %collective-permute-start.1 = (bf16[2,2,64,128]{3,2,1,0:T(8,128)(2,1)}, bf16[2,2,64,128]{3,2,1,0:T(8,128)(2,1)S(1)}, u32[]{:S(2)}, u32[]{:S(2)}) collective-permute-start(bf16[2,2,64,128]{3,2,1,0:T(8,128)(2,1)} %get-tuple-element.20), channel_id=1, source_target_pairs={{0,2},{2,4},{4,6},{6,8},{8,10},{10,12},{12,14},{14,16},{16,18},{18... | collective-permute-start | bytes 196616 | tf_op jit(solution)/shard_map/ppermute | solution.py:279
  7.6 1.9 %collective-permute-start.2 = (bf16[2,2,64,128]{3,2,1,0:T(8,128)(2,1)}, bf16[2,2,64,128]{3,2,1,0:T(8,128)(2,1)S(1)}, u32[]{:S(2)}, u32[]{:S(2)}) collective-permute-start(bf16[2,2,64,128]{3,2,1,0:T(8,128)(2,1)} %get-tuple-element.21), channel_id=1, source_target_pairs={{2,0},{4,2},{6,4},{8,6},{10,8},{12,10},{14,12},{16,14},{18,16},{20... | collective-permute-start | bytes 196616 | tf_op jit(solution)/shard_map/ppermute | solution.py:280
  9.5 0.1 collective-permute-start.3
  9.6 1.5 %collective-permute-start = (s32[4]{0:T(128)}, s32[4]{0:T(128)S(1)}, u32[]{:S(2)}, u32[]{:S(2)}) collective-permute-start(s32[4]{0:T(128)} %bitcast.23), channel_id=1, source_target_pairs={{0,1},{1,0},{2,3},{3,2},{4,5},{5,4},{6,7},{7,6},{8,9},{9,8},{10,11... | collective-permute-start | bytes 56 | tf_op jit(solution)/shard_map/ppermute | solution.py:268
  11.1 7.7 %collective-permute-start.4 = (bf16[2,2,8,128]{3,2,1,0:T(8,128)(2,1)}, bf16[2,2,8,128]{3,2,1,0:T(8,128)(2,1)S(1)}, u32[]{:S(2)}, u32[]{:S(2)}) collective-permute-start(bf16[2,2,8,128]{3,2,1,0:T(8,128)(2,1)} %get-tuple-element.23), channel_id=1, source_target_pairs={{0,3},{1,2},{2,5},{3,4},{4,7},{5,6},{6,9},{7,8},{8,11},{9,10},{10,... | collective-permute-start | bytes 24584 | tf_op jit(solution)/shard_map/ppermute | solution.py:282
  18.8 1.9 %collective-permute-start.5 = (bf16[2,2,8,128]{3,2,1,0:T(8,128)(2,1)}, bf16[2,2,8,128]{3,2,1,0:T(8,128)(2,1)S(1)}, u32[]{:S(2)}, u32[]{:S(2)}) collective-permute-start(bf16[2,2,8,128]{3,2,1,0:T(8,128)(2,1)} %get-tuple-element.24), channel_id=1, source_target_pairs={{2,1},{3,0},{4,3},{5,2},{6,5},{7,4},{8,7},{9,6},{10,9},{11,8},{12,... | collective-permute-start | bytes 24584 | tf_op jit(solution)/shard_map/ppermute | solution.py:283
  20.8 7.4 %collective-permute-done.5.h4 = bf16[2,2,8,128]{3,2,1,0:T(8,128)(2,1)S(1)} collective-permute-done((bf16[2,2,8,128]{3,2,1,0:T(8,128)(2,1)}, bf16[2,2,8,128]{3,2,1,0:T(8,128)(2,1)S(1)}, u32[]{:S(2)}, u32[]{:S(2)}) %collective-permute-start.5) | collective-permute-done | bytes 8224 | tf_op jit(solution)/shard_map/ppermute | solution.py:283
  28.3 0.5 copy-done.7
  28.8 0.0 copy-done
  28.9 9.6 %local_pass.1 = (bf16[1,2,512,128]{3,2,1,0:T(8,128)(2,1)}, f32[27,128,128]{2,1,0:T(8,128)}, bf16[27,128,128]{2,1,0:T(8,128)(2,1)}, bf16[1,2,64,128]{3,2,1,0:T(8,...) custom-call(s32[2,27]{1,0:T(2,128)} %bitcast.21, ...), custom_call_target="tpu_custom_call" | custom-call | tf_op jit(solution)/shard_map/local_pass/pallas_call | solution.py:229
  38.5 0.1 collective-permute-start.11
  38.6 2.6 %collective-permute-done.11 = bf16[27,128,128]{2,1,0:T(8,128)(2,1)S(1)} collective-permute-done((bf16[27,128,128]{2,1,0:T(8,128)(2,1)}, bf16[27,128,128]{2,1,0:T(8,128)(2,1)S(1)}, u32[]{:S(2)}, u32[]{:S(2)}) %collective-permute-start.11) | collective-permute-done | bytes 884768 | tf_op jit(solution)/shard_map/ppermute | solution.py:268
  41.2 1.8 %add_convert_fusion = bf16[27,128,128]{2,1,0:T(8,128)(2,1)S(1)} fusion(f32[27,128,128]{2,1,0:T(8,128)} %get-tuple-element.31, bf16[27,128,128]{2,1,0:T(8,128)(2,1)S(1)} %collective-permute-done.11), kind=kLoop, calls=%fused_computation.1 | loop fusion | flops 1327104 | bytes 3538944 | tf_op jit(solution)/shard_map/convert_element_type | solution.py:297
  43.0 16.4 %all_to_all.20 = bf16[16,216,128]{2,1,0:T(8,128)(2,1)S(1)} all-to-all(bf16[16,216,128]{2,1,0:T(8,128)(2,1)S(1)} %bitcast.11), channel_id=1, replica_groups=mesh['z'=8,'x'=4,'yh'=2,'c'=2,'yl'=2] {'x','yh','yl'}, dimensions={0} | all-to-all | bytes 1769472 | tf_op jit(solution)/shard_map/all_to_all | solution.py:297
  59.4 0.1 convert_reduce_fusion
  59.6 17.1 %all_to_all.21 = f32[8,27,128]{2,1,0:T(8,128)S(1)} all-to-all(f32[8,27,128]{2,1,0:T(8,128)S(1)} %reshape.57), channel_id=1, replica_groups=mesh['z'=8,'x'=4,'yh'=2,'c'=2,'yl'=2] {'z'}, dimensions={0} | all-to-all | bytes 221184 | tf_op jit(solution)/shard_map/all_to_all | solution.py:300
  76.7 9.6 %all_to_all.22 = bf16[8,27,128]{2,1,0:T(8,128)(2,1)S(1)} all-to-all(bf16[8,27,128]{2,1,0:T(8,128)(2,1)S(1)} %broadcast_in_dim.6), channel_id=1, replica_groups=mesh['z'=8,'x'=4,'yh'=2,'c'=2,'yl'=2] {'z'}, dimensions={0} | all-to-all | bytes 110592 | tf_op jit(solution)/shard_map/all_to_all | solution.py:290
  86.4 0.1 broadcast_in_dim.15
  86.5 14.5 %all_to_all.23 = bf16[16,216,128]{2,1,0:T(8,128)(2,1)S(1)} all-to-all(bf16[16,216,128]{2,1,0:T(8,128)(2,1)S(1)} %broadcast_in_dim.15), channel_id=1, replica_groups=mesh['z'=8,'x'=4,'yh'=2,'c'=2,'yl'=2] {'x','yh','yl'}, dimensions={0} | all-to-all | bytes 1769472 | tf_op jit(solution)/shard_map/all_to_all | solution.py:290
  101.0 5.4 %collective-permute-start.12 = (bf16[27,128,128]{2,1,0:T(8,128)(2,1)S(1)}, bf16[27,128,128]{2,1,0:T(8,128)(2,1)S(1)}, u32[]{:S(2)}, u32[]{:S(2)}) collective-permute-start(bf16[27,128,128]{2,1,0:T(8,128)(2,1)S(1)} %bitcast.12), channel_id=1, source_target_pairs={{0,2},{2,0},{1,3},{3,1},{4,6},{6,4},{5,7},{7,5},{8,10},{10,8},{9,1... | collective-permute-start | bytes 2654216 | tf_op jit(solution)/shard_map/ppermute | solution.py:268
  106.4 5.2 %collective-permute-start.6 = (bf16[1,2,64,128]{3,2,1,0:T(8,128)(2,1)S(1)}, bf16[1,2,64,128]{3,2,1,0:T(8,128)(2,1)S(1)}, u32[]{:S(2)}, u32[]{:S(2)}) collective-permute-start(bf16[1,2,64,128]{3,2,1,0:T(8,128)(2,1)S(1)} %copy-done.13), channel_id=1, source_target_pairs={{0,2},{2,4},{4,6},{6,8},{8,10},{10,12},{12,14},{14,16},{16,18},{18... | collective-permute-start | bytes 98312 | tf_op jit(solution)/shard_map/ppermute | solution.py:279
  111.7 1.9 %collective-permute-start.7 = (bf16[1,2,64,128]{3,2,1,0:T(8,128)(2,1)S(1)}, bf16[1,2,64,128]{3,2,1,0:T(8,128)(2,1)S(1)}, u32[]{:S(2)}, u32[]{:S(2)}) collective-permute-start(bf16[1,2,64,128]{3,2,1,0:T(8,128)(2,1)S(1)} %copy-done.12), channel_id=1, source_target_pairs={{2,0},{4,2},{6,4},{8,6},{10,8},{12,10},{14,12},{16,14},{18,16},{20... | collective-permute-start | bytes 98312 | tf_op jit(solution)/shard_map/ppermute | solution.py:280
  113.6 0.9 collective-permute-start.8
  114.5 7.9 %collective-permute-start.9 = (bf16[1,2,8,128]{3,2,1,0:T(8,128)(2,1)S(1)}, bf16[1,2,8,128]{3,2,1,0:T(8,128)(2,1)S(1)}, u32[]{:S(2)}, u32[]{:S(2)}) collective-permute-start(bf16[1,2,8,128]{3,2,1,0:T(8,128)(2,1)S(1)} %copy-done.15), channel_id=1, source_target_pairs={{0,3},{1,2},{2,5},{3,4},{4,7},{5,6},{6,9},{7,8},{8,11},{9,10},{10,... | collective-permute-start | bytes 12296 | tf_op jit(solution)/shard_map/ppermute | solution.py:282
  122.4 0.7 collective-permute-done.9.h3
  123.1 1.9 %collective-permute-start.10 = (bf16[1,2,8,128]{3,2,1,0:T(8,128)(2,1)S(1)}, bf16[1,2,8,128]{3,2,1,0:T(8,128)(2,1)S(1)}, u32[]{:S(2)}, u32[]{:S(2)}) collective-permute-start(bf16[1,2,8,128]{3,2,1,0:T(8,128)(2,1)S(1)} %copy-done.14), channel_id=1, source_target_pairs={{2,1},{3,0},{4,3},{5,2},{6,5},{7,4},{8,7},{9,6},{10,9},{11,8},{12,... | collective-permute-start | bytes 12296 | tf_op jit(solution)/shard_map/ppermute | solution.py:283
  125.1 7.8 %collective-permute-done.10.h4 = bf16[1,2,8,128]{3,2,1,0:T(8,128)(2,1)S(1)} collective-permute-done((bf16[1,2,8,128]{3,2,1,0:T(8,128)(2,1)S(1)}, bf16[1,2,8,128]{3,2,1,0:T(8,128)(2,1)S(1)}, u32[]{:S(2)}, u32[]{:S(2)}) %collective-permute-start.10) | collective-permute-done | bytes 4128 | tf_op jit(solution)/shard_map/ppermute | solution.py:283
  132.9 0.5 copy-done.9
  133.4 0.0 copy-done.3
  133.5 4.0 %input_grad.1 = bf16[2,512,128]{2,1,0:T(8,128)(2,1)} custom-call(s32[2,27]{1,0:T(2,128)} %bitcast.22, s32[4]{0:T(128)} %copy-done.10, bf16[1,2,512,128]{3,2,1,0:T(8,128)(2,1)} %get-tuple-element.25.gp, f32[2,512,128]{2,1,0:T(8,128)} %get-tuple-element.19.mask_ref, bf16[2,512,128]{2,1,0:T(8,128)(2,1)} %bitcast.15, bf16[27,128,128]{2,1,0:T(8,128)(2,1)} %w1.3, ...), custom_call_target="tpu_custom_call" | custom-call | tf_op jit(solution)/shard_map/input_grad/pallas_call | solution.py:252
  137.5 2.0 %select_convert_fusion = (f32[27,128,128]{2,1,0:T(8,128)}, f32[27,128,128]{2,1,0:T(8,128)}) fusion(bf16[27,128,128]{2,1,0:T(8,128)(2,1)S(1)} %bitcast.13, bf16[27,128,128]{2,1,0:T(8,128)(2,1)S(1)} %collective-permute-done.12, pred[]{:T(512)S(6)} %eq.3), kind=kLoop, calls=%fused_computation.2 | loop fusion | flops 1769472 | bytes 5308417 | tf_op jit(solution)/shard_map/convert_element_type | solution.py:306
  (42 shorter events, 0.2 us)
Async XLA Ops:
  2.9 25.3 %collective-permute-start.1 = (bf16[2,2,64,128]{3,2,1,0:T(8,128)(2,1)}, bf16[2,2,64,128]{3,2,1,0:T(8,128)(2,1)S(1)}, u32[]{:S(2)}, u32[]{:S(2)}) collective-permute-start(bf16[2,2,64,128]{3,2,1,0:T(8,128)(2,1)} %get-tuple-element.20), channel_id=1, source_target_pairs={{0,2},{2,4},{4,6},{6,8},{8,10},{10,12},{12,14},{14,16},{16,18},{18... | collective-permute-start | bytes 196616 | tf_op jit(solution)/shard_map/ppermute | solution.py:279
  7.6 20.6 %collective-permute-start.2 = (bf16[2,2,64,128]{3,2,1,0:T(8,128)(2,1)}, bf16[2,2,64,128]{3,2,1,0:T(8,128)(2,1)S(1)}, u32[]{:S(2)}, u32[]{:S(2)}) collective-permute-start(bf16[2,2,64,128]{3,2,1,0:T(8,128)(2,1)} %get-tuple-element.21), channel_id=1, source_target_pairs={{2,0},{4,2},{6,4},{8,6},{10,8},{12,10},{14,12},{16,14},{18,16},{20... | collective-permute-start | bytes 196616 | tf_op jit(solution)/shard_map/ppermute | solution.py:280
  9.5 18.7 %collective-permute-start.3 = (bf16[2,2,64,128]{3,2,1,0:T(8,128)(2,1)}, bf16[2,2,64,128]{3,2,1,0:T(8,128)(2,1)S(1)}, u32[]{:S(2)}, u32[]{:S(2)}) collective-permute-start(bf16[2,2,64,128]{3,2,1,0:T(8,128)(2,1)} %get-tuple-element.22), channel_id=1, source_target_pairs={{0,1},{1,0},{2,3},{3,2},{4,5},{5,4},{6,7},{7,6},{8,9},{9,8},{10,11... | collective-permute-start | bytes 196616 | tf_op jit(solution)/shard_map/ppermute | solution.py:268
  9.6 9.2 %collective-permute-start = (s32[4]{0:T(128)}, s32[4]{0:T(128)S(1)}, u32[]{:S(2)}, u32[]{:S(2)}) collective-permute-start(s32[4]{0:T(128)} %bitcast.23), channel_id=1, source_target_pairs={{0,1},{1,0},{2,3},{3,2},{4,5},{5,4},{6,7},{7,6},{8,9},{9,8},{10,11... | collective-permute-start | bytes 56 | tf_op jit(solution)/shard_map/ppermute | solution.py:268
  11.1 9.7 %collective-permute-start.4 = (bf16[2,2,8,128]{3,2,1,0:T(8,128)(2,1)}, bf16[2,2,8,128]{3,2,1,0:T(8,128)(2,1)S(1)}, u32[]{:S(2)}, u32[]{:S(2)}) collective-permute-start(bf16[2,2,8,128]{3,2,1,0:T(8,128)(2,1)} %get-tuple-element.23), channel_id=1, source_target_pairs={{0,3},{1,2},{2,5},{3,4},{4,7},{5,6},{6,9},{7,8},{8,11},{9,10},{10,... | collective-permute-start | bytes 24584 | tf_op jit(solution)/shard_map/ppermute | solution.py:282
  18.8 9.5 %copy-start.10 = (s32[4]{0:T(128)}, s32[4]{0:T(128)S(1)}, u32[]{:S(2)}) copy-start(s32[4]{0:T(128)S(1)} %collective-permute-done.peer) | copy-start | bytes 52
  18.8 9.4 %collective-permute-start.5 = (bf16[2,2,8,128]{3,2,1,0:T(8,128)(2,1)}, bf16[2,2,8,128]{3,2,1,0:T(8,128)(2,1)S(1)}, u32[]{:S(2)}, u32[]{:S(2)}) collective-permute-start(bf16[2,2,8,128]{3,2,1,0:T(8,128)(2,1)} %get-tuple-element.24), channel_id=1, source_target_pairs={{2,1},{3,0},{4,3},{5,2},{6,5},{7,4},{8,7},{9,6},{10,9},{11,8},{12,... | collective-permute-start | bytes 24584 | tf_op jit(solution)/shard_map/ppermute | solution.py:283
  20.7 7.5 %copy-start.6 = (bf16[2,2,8,128]{3,2,1,0:T(8,128)(2,1)}, bf16[2,2,8,128]{3,2,1,0:T(8,128)(2,1)S(1)}, u32[]{:S(2)}) copy-start(bf16[2,2,8,128]{3,2,1,0:T(8,128)(2,1)S(1)} %collective-permute-done.4.h3) | copy-start | bytes 24580
  28.2 0.6 copy-start.7
  28.2 0.6 copy-start
  28.2 0.6 copy-start.1
  28.2 0.6 copy-start.2
  38.5 2.7 %collective-permute-start.11 = (bf16[27,128,128]{2,1,0:T(8,128)(2,1)}, bf16[27,128,128]{2,1,0:T(8,128)(2,1)S(1)}, u32[]{:S(2)}, u32[]{:S(2)}) collective-permute-start(bf16[27,128,128]{2,1,0:T(8,128)(2,1)} %get-tuple-element.32), channel_id=1, source_target_pairs={{0,2},{2,0},{1,3},{3,1},{4,6},{6,4},{5,7},{7,5},{8,10},{10,8},{9,1... | collective-permute-start | bytes 2654216 | tf_op jit(solution)/shard_map/ppermute | solution.py:268
  59.6 46.8 %copy-start.13 = (bf16[1,2,64,128]{3,2,1,0:T(8,128)(2,1)S(1)}, bf16[1,2,64,128]{3,2,1,0:T(8,128)(2,1)}, u32[]{:S(2)}) copy-start(bf16[1,2,64,128]{3,2,1,0:T(8,128)(2,1)} %get-tuple-element.26) | copy-start | bytes 98308
  59.6 52.1 %copy-start.12 = (bf16[1,2,64,128]{3,2,1,0:T(8,128)(2,1)S(1)}, bf16[1,2,64,128]{3,2,1,0:T(8,128)(2,1)}, u32[]{:S(2)}) copy-start(bf16[1,2,64,128]{3,2,1,0:T(8,128)(2,1)} %get-tuple-element.27) | copy-start | bytes 98308
  59.6 54.0 %copy-start.11 = (bf16[1,2,64,128]{3,2,1,0:T(8,128)(2,1)S(1)}, bf16[1,2,64,128]{3,2,1,0:T(8,128)(2,1)}, u32[]{:S(2)}) copy-start(bf16[1,2,64,128]{3,2,1,0:T(8,128)(2,1)} %get-tuple-element.28) | copy-start | bytes 98308
  59.6 54.9 %copy-start.15 = (bf16[1,2,8,128]{3,2,1,0:T(8,128)(2,1)S(1)}, bf16[1,2,8,128]{3,2,1,0:T(8,128)(2,1)}, u32[]{:S(2)}) copy-start(bf16[1,2,8,128]{3,2,1,0:T(8,128)(2,1)} %get-tuple-element.29) | copy-start | bytes 12292
  59.6 63.5 %copy-start.14 = (bf16[1,2,8,128]{3,2,1,0:T(8,128)(2,1)S(1)}, bf16[1,2,8,128]{3,2,1,0:T(8,128)(2,1)}, u32[]{:S(2)}) copy-start(bf16[1,2,8,128]{3,2,1,0:T(8,128)(2,1)} %get-tuple-element.30) | copy-start | bytes 12292
  101.0 36.5 %collective-permute-start.12 = (bf16[27,128,128]{2,1,0:T(8,128)(2,1)S(1)}, bf16[27,128,128]{2,1,0:T(8,128)(2,1)S(1)}, u32[]{:S(2)}, u32[]{:S(2)}) collective-permute-start(bf16[27,128,128]{2,1,0:T(8,128)(2,1)S(1)} %bitcast.12), channel_id=1, source_target_pairs={{0,2},{2,0},{1,3},{3,1},{4,6},{6,4},{5,7},{7,5},{8,10},{10,8},{9,1... | collective-permute-start | bytes 2654216 | tf_op jit(solution)/shard_map/ppermute | solution.py:268
  106.4 26.4 %collective-permute-start.6 = (bf16[1,2,64,128]{3,2,1,0:T(8,128)(2,1)S(1)}, bf16[1,2,64,128]{3,2,1,0:T(8,128)(2,1)S(1)}, u32[]{:S(2)}, u32[]{:S(2)}) collective-permute-start(bf16[1,2,64,128]{3,2,1,0:T(8,128)(2,1)S(1)} %copy-done.13), channel_id=1, source_target_pairs={{0,2},{2,4},{4,6},{6,8},{8,10},{10,12},{12,14},{14,16},{16,18},{18... | collective-permute-start | bytes 98312 | tf_op jit(solution)/shard_map/ppermute | solution.py:279
  111.7 21.2 %collective-permute-start.7 = (bf16[1,2,64,128]{3,2,1,0:T(8,128)(2,1)S(1)}, bf16[1,2,64,128]{3,2,1,0:T(8,128)(2,1)S(1)}, u32[]{:S(2)}, u32[]{:S(2)}) collective-permute-start(bf16[1,2,64,128]{3,2,1,0:T(8,128)(2,1)S(1)} %copy-done.12), channel_id=1, source_target_pairs={{2,0},{4,2},{6,4},{8,6},{10,8},{12,10},{14,12},{16,14},{18,16},{20... | collective-permute-start | bytes 98312 | tf_op jit(solution)/shard_map/ppermute | solution.py:280
  113.6 19.2 %collective-permute-start.8 = (bf16[1,2,64,128]{3,2,1,0:T(8,128)(2,1)S(1)}, bf16[1,2,64,128]{3,2,1,0:T(8,128)(2,1)S(1)}, u32[]{:S(2)}, u32[]{:S(2)}) collective-permute-start(bf16[1,2,64,128]{3,2,1,0:T(8,128)(2,1)S(1)} %copy-done.11), channel_id=1, source_target_pairs={{0,1},{1,0},{2,3},{3,2},{4,5},{5,4},{6,7},{7,6},{8,9},{9,8},{10,11... | collective-permute-start | bytes 98312 | tf_op jit(solution)/shard_map/ppermute | solution.py:268
  114.5 8.7 %collective-permute-start.9 = (bf16[1,2,8,128]{3,2,1,0:T(8,128)(2,1)S(1)}, bf16[1,2,8,128]{3,2,1,0:T(8,128)(2,1)S(1)}, u32[]{:S(2)}, u32[]{:S(2)}) collective-permute-start(bf16[1,2,8,128]{3,2,1,0:T(8,128)(2,1)S(1)} %copy-done.15), channel_id=1, source_target_pairs={{0,3},{1,2},{2,5},{3,4},{4,7},{5,6},{6,9},{7,8},{8,11},{9,10},{10,... | collective-permute-start | bytes 12296 | tf_op jit(solution)/shard_map/ppermute | solution.py:282
  123.1 9.7 %copy-start.8 = (bf16[1,2,8,128]{3,2,1,0:T(8,128)(2,1)}, bf16[1,2,8,128]{3,2,1,0:T(8,128)(2,1)S(1)}, u32[]{:S(2)}) copy-start(bf16[1,2,8,128]{3,2,1,0:T(8,128)(2,1)S(1)} %collective-permute-done.9.h3) | copy-start | bytes 12292
  123.1 9.7 %collective-permute-start.10 = (bf16[1,2,8,128]{3,2,1,0:T(8,128)(2,1)S(1)}, bf16[1,2,8,128]{3,2,1,0:T(8,128)(2,1)S(1)}, u32[]{:S(2)}, u32[]{:S(2)}) collective-permute-start(bf16[1,2,8,128]{3,2,1,0:T(8,128)(2,1)S(1)} %copy-done.14), channel_id=1, source_target_pairs={{2,1},{3,0},{4,3},{5,2},{6,5},{7,4},{8,7},{9,6},{10,9},{11,8},{12,... | collective-permute-start | bytes 12296 | tf_op jit(solution)/shard_map/ppermute | solution.py:283
  132.8 0.6 copy-start.9
  132.8 0.6 copy-start.3
  132.8 0.6 copy-start.4
  132.9 0.6 copy-start.5

commit v2 on v1

v2 whole, which is shorter than its diff:
```python
import functools
import math

import jax
import jax.numpy as jnp
from jax import lax
from jax.experimental import pallas as pl
from jax.experimental.pallas import tpu as pltpu
from jax.sharding import Mesh
from jax.sharding import PartitionSpec as P

SPLIT = {"z": 8, "x": 4, "yh": 2, "c": 2}
SPACE = ("z", "x", "yh", "c")
TIME = "yl"
PLANE = ("x", "yh", "yl")

E = 8
CH = 128
FACE = E * E
VOX = E * FACE
BLK = 2
ROWS = BLK * VOX
RIM = 4 * FACE + 4 * E
BF = jnp.bfloat16
F32 = jnp.float32

WINDOWS = [(dt, dx) for dt in (-1, 0, 1) for dx in (-1, 0, 1)]

VM = pl.BlockSpec(memory_space=pltpu.VMEM)
SM = pl.BlockSpec(memory_space=pltpu.SMEM)
PARAMS = pltpu.CompilerParams(vmem_limit_bytes=56 * 1024 * 1024)


def stack_rows(parts):
    return jnp.concatenate([part.reshape(-1, CH) for part in parts], axis=0)


def pack_kernel(sends, when, half, core, f_ref, g_ref, occ_ref, xg_ref, mask_ref, *messages):
    even_ref, odd_ref, time_ref, even_diag, odd_diag = messages
    even = core[0] == 0
    sides, times, corners = [], [], []
    for b in range(BLK):
        row = occ_ref[b : b + 1, :].astype(F32)
        mask = jnp.broadcast_to(row, (CH, VOX)).T
        mask_ref[b] = mask
        values = []
        for i, ref in enumerate((f_ref, g_ref)):
            masked = ref[b].astype(F32) * mask
            xg_ref[i, b] = masked.astype(BF)
            values.append(masked.reshape(E, FACE, CH))
        mask = mask.reshape(E, FACE, CH)
        low = stack_rows([v[:, : 2 * E] for v in values] + [mask[:, :E]])
        high = stack_rows([v[:, FACE - 2 * E :] for v in values] + [mask[:, FACE - E :]])
        sides.append((low, high))
        first = half[0] == 0
        edge = [jnp.where(first, v[E - 2 :], v[:2]) for v in values]
        edge.append(jnp.where(first, mask[E - 1 :], mask[:1]))
        times.append(stack_rows(edge))
        pad = jnp.zeros((E, CH), F32)
        low = stack_rows([v[:, : 2 * E] for v in edge[:2]] + [edge[2][:, :E], pad])
        high = stack_rows(
            [v[:, FACE - 2 * E :] for v in edge[:2]] + [edge[2][:, FACE - E :], pad]
        )
        corners.append((low, high))
    rows = lax.broadcasted_iota(jnp.int32, (2 * E, CH), 0)
    note = jnp.zeros((2 * E, CH), F32)
    for p in range(2 * BLK):
        note = jnp.where(rows == p, when[p].astype(F32), note)
    for side_ref, diag_ref, up in ((even_ref, even_diag, even), (odd_ref, odd_diag, ~even)):
        for slot in range(BLK):
            index = jnp.where(up, sends[1, slot], sends[0, slot])
            for ref, options in ((side_ref, sides), (diag_ref, corners)):
                value = jnp.zeros(options[0][0].shape, F32)
                for b, (low, high) in enumerate(options):
                    value = jnp.where(index == b, jnp.where(up, high, low), value)
                ref[slot] = value.astype(BF)
    for b in range(BLK):
        time_ref[b] = jnp.concatenate([times[b], note], axis=0).astype(BF)


def select(flag, value, other):
    if flag.ndim == 0:
        return jnp.where(flag, value, other)
    tiles = lambda v: v.reshape(-1, E, CH)
    chosen = jnp.where(jnp.broadcast_to(flag, tiles(value).shape), tiles(value), tiles(other))
    return chosen.reshape(value.shape)


def build(targets, owns, table, even, halos):
    even_side, odd_side, across, even_diag, odd_diag = (
        [ref[j].astype(F32) for j in range(BLK)] for ref in halos
    )
    either = lambda a, b: [jnp.where(even, p, q) for p, q in zip(a, b)]
    below, below_diag = either(odd_side, even_side), either(odd_diag, even_diag)
    above, above_diag = either(even_side, odd_side), either(even_diag, odd_diag)
    notes = [
        jnp.broadcast_to(across[0][5 * FACE + p : 5 * FACE + p + 1], (E, CH))
        for p in range(2 * BLK)
    ]
    for (tile, w, _, _), own in zip(targets, owns):
        for b in range(BLK):
            tile[b, w : w + E, w * E : w * E + FACE] = own[b]
    for b in range(BLK):
        for dt, dx in WINDOWS:
            if dt == 0 and dx == 0:
                continue
            slot = table[b, (dt + 1) * 9 + (dx + 1) * 3 + 1]
            side, diag = (below, below_diag) if dx < 0 else (above, above_diag)
            first = BLK if dx < 0 else 2 * BLK
            far = jnp.full((E, CH), -1.0, F32)
            for p, note in enumerate(notes):
                far = jnp.where(slot == 3 * BLK + p, note, far)
            for (tile, w, row, corner), own in zip(targets, owns):
                ts = {-1: slice(E - w, E), 0: slice(0, E), 1: slice(0, w)}[dt]
                xs = {-1: slice(FACE - w * E, FACE), 0: slice(0, FACE), 1: slice(0, w * E)}[dx]
                to_t = {-1: slice(0, w), 0: slice(w, w + E), 1: slice(w + E, 2 * w + E)}[dt]
                end = w * E + FACE
                to_x = {-1: slice(0, w * E), 0: slice(w * E, end), 1: slice(end, end + w * E)}[dx]
                value = jnp.zeros(own[0][ts, xs].shape, F32)
                for j in range(BLK):
                    value = select(slot == j, own[j][ts, xs], value)
                    if dx != 0:
                        face = side[j][row : row + FACE * w].reshape(E, w * E, CH)
                        value = select(slot == first + j, face[ts], value)
                    if dt != 0:
                        face = across[j][row : row + FACE * w].reshape(w, FACE, CH)
                        value = select(far == j, face[:, xs], value)
                    if dt != 0 and dx != 0:
                        face = diag[j][corner : corner + E * w * w].reshape(w, w * E, CH)
                        value = select(far == first + j, face, value)
                tile[b, to_t, to_x] = value


def pieces(tile, b, w, dt, dx):
    cut = lambda t, nt, x, nx: tile[
        b, w + t + dt : w + t + dt + nt, E * (w + x + dx) : E * (w + x + dx + nx)
    ].reshape(nt * nx * E, CH)
    rim = [(-1, 1, -1, E + 2), (E, 1, -1, E + 2), (0, E, -1, 1), (0, E, E, 1)]
    return cut(0, E, 0, E), lambda: [cut(*part) for part in rim]


def columns(tile, w, sign, cols, rim):
    for k, (dt, dx) in enumerate(WINDOWS):
        lane = slice(k * CH, (k + 1) * CH)
        for b in range(BLK):
            core, ring = pieces(tile, b, w, sign * dt, sign * dx)
            cols[b * VOX : (b + 1) * VOX, lane] = core.astype(BF)
            if rim:
                at = ROWS + b * RIM
                cols[at : at + RIM, lane] = jnp.concatenate(ring(), axis=0).astype(BF)


def shift(value, step):
    y = lax.broadcasted_iota(jnp.int32, value.shape, 0) % E
    moved = pltpu.roll(value, (-step) % value.shape[0], 0)
    return jnp.where(y == (E - 1 if step > 0 else 0), 0.0, moved)


def lanes(value, dy):
    return value[:, (dy + 1) * CH : (dy + 2) * CH]


def gather_y(parts, sign):
    return lanes(parts, 0) + shift(lanes(parts, 1), sign) + shift(lanes(parts, -1), -sign)


def transposed(cols, w_ref, wide):
    for k in range(27):
        w, d = divmod(k, 3)
        wide[d * CH : (d + 1) * CH, w * CH : (w + 1) * CH] = w_ref[k]
    parts = lax.dot_general(
        cols[...], wide[...], (((1,), (1,)), ((), ())), preferred_element_type=F32
    )
    return gather_y(parts, -1)


def outer(left, right):
    return lax.dot_general(left, right, (((0,), (0,)), ((), ())), preferred_element_type=F32)


def local_kernel(
    table, core, xg, mask_ref, w1, w2, h0, h1, h2, h3, h4,
    gp_ref, keep_ref, send_ref, xtile, gtile, mtile, xcol, gcol, wide, tall,
):
    owns = [[xg[i, b].astype(F32).reshape(E, FACE, CH) for b in range(BLK)] for i in range(2)]
    owns.append([mask_ref[b].reshape(E, FACE, CH) for b in range(BLK)])
    targets = [
        (xtile, 2, 0, 0),
        (gtile, 2, 2 * FACE, 4 * E),
        (mtile, 1, 4 * FACE, 8 * E),
    ]
    even = core[0] == 0
    build(targets, owns, table, even, (h0, h1, h2, h3, h4))
    columns(xtile, 2, 1, xcol, True)
    columns(gtile, 2, -1, gcol, True)
    parts = [pieces(mtile, b, 1, 0, 0) for b in range(BLK)]
    mask = jnp.concatenate([p[0] for p in parts] + parts[0][1]() + parts[1][1](), axis=0)
    for k in range(27):
        w, d = divmod(k, 3)
        tall[w * CH : (w + 1) * CH, d * CH : (d + 1) * CH] = w1[k]
    parts = jnp.dot(xcol[...], tall[...], preferred_element_type=F32)
    pre = gather_y(parts, 1)
    sig = jax.nn.sigmoid(pre)
    hidden = (pre[:ROWS] * sig[:ROWS] * mask[:ROWS]).astype(BF).astype(F32)
    shifted = jnp.concatenate([shift(hidden, -1), hidden, shift(hidden, 1)], axis=1).astype(BF)
    second = outer(shifted, gcol[:ROWS])
    grad_hidden = transposed(gcol, w2, wide)
    grad_pre = (grad_hidden * sig * (1.0 + pre * (1.0 - sig)) * mask).astype(BF).astype(F32)
    for b in range(BLK):
        at = ROWS + b * RIM
        side = (E + 2) * E
        gp_ref[b, 1 : E + 1, E : E + FACE] = grad_pre[b * VOX : (b + 1) * VOX].reshape(E, FACE, CH)
        gp_ref[b, 0] = grad_pre[at : at + side]
        gp_ref[b, E + 1] = grad_pre[at + side : at + 2 * side]
        at += 2 * side
        gp_ref[b, 1 : E + 1, 0:E] = grad_pre[at : at + FACE].reshape(E, E, CH)
        gp_ref[b, 1 : E + 1, E + FACE :] = grad_pre[at + FACE : at + 2 * FACE].reshape(E, E, CH)
    grad_pre = grad_pre[:ROWS]
    shifted = jnp.concatenate(
        [shift(grad_pre, 1), grad_pre, shift(grad_pre, -1)], axis=1
    ).astype(BF)
    first = outer(xcol[:ROWS], shifted)
    for k in range(27):
        w, d = divmod(k, 3)
        a = second[d * CH : (d + 1) * CH, w * CH : (w + 1) * CH]
        b = first[w * CH : (w + 1) * CH, d * CH : (d + 1) * CH]
        keep_ref[k] = jnp.where(even, a, b)
        send_ref[k] = jnp.where(even, b, a).astype(BF)


def input_kernel(gp, mask_ref, cot, w1, out, dcol, wide):
    columns(gp, 1, -1, dcol, False)
    total = transposed(dcol, w1, wide) * mask_ref[...].reshape(ROWS, CH)
    total = cot[...].astype(F32).reshape(ROWS, CH) + total
    out[...] = total.astype(BF).reshape(BLK, VOX, CH)


def pack(f, g, occ, sends, when, half, core):
    shapes = [5 * FACE, 5 * FACE, 5 * FACE + 2 * E, 10 * E, 10 * E]
    return pl.pallas_call(
        pack_kernel,
        out_shape=[
            jax.ShapeDtypeStruct((2, BLK, VOX, CH), BF),
            jax.ShapeDtypeStruct((BLK, VOX, CH), F32),
            *[jax.ShapeDtypeStruct((BLK, rows, CH), BF) for rows in shapes],
        ],
        in_specs=[SM] * 4 + [VM] * 3,
        out_specs=[VM] * 7,
        compiler_params=PARAMS,
        name="pack",
    )(sends, when, half, core, f, g, occ)


def local_pass(table, core, xg, mask, w1, w2, halos):
    return pl.pallas_call(
        local_kernel,
        out_shape=[
            jax.ShapeDtypeStruct((BLK, E + 2, (E + 2) * E, CH), F32),
            jax.ShapeDtypeStruct((27, CH, CH), F32),
            jax.ShapeDtypeStruct((27, CH, CH), BF),
        ],
        in_specs=[SM] * 2 + [VM] * 9,
        out_specs=[VM] * 3,
        scratch_shapes=[
            pltpu.VMEM((BLK, E + 4, (E + 4) * E, CH), F32),
            pltpu.VMEM((BLK, E + 4, (E + 4) * E, CH), F32),
            pltpu.VMEM((BLK, E + 2, (E + 2) * E, CH), F32),
            pltpu.VMEM((ROWS + BLK * RIM, 9 * CH), BF),
            pltpu.VMEM((ROWS + BLK * RIM, 9 * CH), BF),
            pltpu.VMEM((3 * CH, 9 * CH), BF),
            pltpu.VMEM((9 * CH, 3 * CH), BF),
        ],
        compiler_params=PARAMS,
        name="local_pass",
    )(table, core, xg, mask, w1, w2, *halos)


def input_grad(gp, mask, cot, w1):
    return pl.pallas_call(
        input_kernel,
        out_shape=jax.ShapeDtypeStruct((BLK, VOX, CH), BF),
        in_specs=[VM] * 4,
        out_specs=VM,
        scratch_shapes=[
            pltpu.VMEM((ROWS, 9 * CH), BF),
            pltpu.VMEM((3 * CH, 9 * CH), BF),
        ],
        compiler_params=PARAMS,
        name="input_grad",
    )(gp, mask, cot, w1)


def swap(value, axis):
    return lax.ppermute(value, axis, [(0, 1), (1, 0)])


def exchange(messages):
    even_side, odd_side, time, even_diag, odd_diag = messages
    size = math.prod(lax.axis_size(axis) for axis in SPACE)
    both = lambda start: [
        pair for i in range(start, size - 1, 2) for pair in ((i, i + 1), (i + 1, i))
    ]
    cross = lambda pairs: [(2 * i + t, 2 * j + 1 - t) for i, j in pairs for t in (0, 1)]
    return (
        lax.ppermute(even_side, SPACE, both(0)),
        lax.ppermute(odd_side, SPACE, both(1)),
        swap(time, TIME),
        lax.ppermute(even_diag, (*SPACE, TIME), cross(both(0))),
        lax.ppermute(odd_diag, (*SPACE, TIME), cross(both(1))),
    )


def spread(value, axes):
    size = math.prod(lax.axis_size(axis) for axis in axes)
    copies = jnp.broadcast_to(value[None], (size, *value.shape))
    return lax.all_to_all(copies, axes, 0, 0)


def reduce_all(keep, send, scale):
    total = keep + swap(send, "c").astype(F32)
    plane = math.prod(lax.axis_size(axis) for axis in PLANE)
    rows = 27 * CH // plane
    parts = lax.all_to_all(total.astype(BF).reshape(plane, rows, CH), PLANE, 0, 0)
    total = jnp.sum(parts.astype(F32), axis=0)
    depth = lax.axis_size("z")
    parts = lax.all_to_all(total.reshape(depth, rows // depth, CH), "z", 0, 0)
    total = (jnp.sum(parts, axis=0) * scale).astype(BF)
    total = spread(total, ("z",)).reshape(rows, CH)
    mine = spread(total, PLANE).reshape(27, CH, CH)
    other = swap(mine, "c")
    even = lax.axis_index("c") == 0
    second = jnp.where(even, mine, other).astype(F32)
    first = jnp.where(even, other, mine).astype(F32)
    return first, second


def body(features, cotangent, w_first, w_second, occupancy, neighbors, send_space, send_time):
    f, g = (a.reshape(BLK, VOX, CH) for a in (features, cotangent))
    half = lax.axis_index(TIME).astype(jnp.int32).reshape(1)
    core = lax.axis_index("c").astype(jnp.int32).reshape(1)
    sends = send_space.reshape(2, BLK)
    table = neighbors.reshape(BLK, 27)
    when = send_time.reshape(2 * BLK)
    xg, mask, *messages = pack(f, g, occupancy.reshape(BLK, VOX), sends, when, half, core)
    halos = exchange(messages)
    gp, keep, send = local_pass(table, core, xg, mask, w_first, w_second, halos)
    out = input_grad(gp, mask, g, w_first)
    devices = math.prod(lax.axis_size(axis) for axis in (*SPACE, TIME))
    first, second = reduce_all(keep, send, 1.0 / math.sqrt(devices * ROWS))
    return out.reshape(features.shape), first, second


def solution(mesh):
    fine = Mesh(
        mesh.devices.reshape(*SPLIT.values(), mesh.shape["tm"]), (*SPACE, TIME)
    )
    split = lambda rank: P(SPACE, TIME, *[None] * (rank - 2))
    return jax.shard_map(
        body,
        mesh=fine,
        in_specs=(
            split(5), split(5), P(), P(), split(4), split(4), split(4), split(3),
        ),
        out_specs=(split(5), P(), P()),
        check_vma=False,
    )
```

time: 140 us -> 110 us (0.79)
  the two profiles are of different devices: /device:TPU:31 before, /device:TPU:1 now
where the time goes in v2:
time: 110 us; the launch traced here: 109 us
  blocking collectives  63 us (57%)
  Pallas kernels  18.3 us (17%)
  starting transfers between devices  16.9 us (15%)
  waiting for transfers between devices  5.43 us (5%)
  other arithmetic  3.92 us (4%)
    all_to_all x2, blocking collectives, spread(): return lax.all_to_all(copies, axes, 0, 0)  24.2 us
    all_to_all x1, blocking collectives, reduce_all(): lax.all_to_all(total.astype(BF).reshape(plane, rows, CH), PLANE, 0, 0)  21.7 us
    all_to_all x1, blocking collectives, reduce_all(): parts = lax.all_to_all(total.reshape(depth, rows // depth, CH), 'z', 0, 0)  17.2 us
    pallas_call x1, Pallas kernels, local_pass(): pl.pallas_call(local_kernel, out_shape=[jax.ShapeDtypeStruct((BLK, E + 2,...  11.8 us
    ppermute x3, starting transfers between devices, swap(): return lax.ppermute(value, axis, [(0, 1), (1, 0)])  7.51 us
    ppermute x1, starting transfers between devices, exchange(): lax.ppermute(odd_side, SPACE, both(1))  4.19 us
    pallas_call x1, Pallas kernels, input_grad(): pl.pallas_call(input_kernel, out_shape=jax.ShapeDtypeStruct((BLK, VOX, CH...  4.04 us
    ppermute x1, starting transfers between devices, exchange(): lax.ppermute(odd_diag, (*SPACE, TIME), cross(both(1)))  3.95 us
  transfers between devices with their start and end apart: 7, of which 3 were waited for; matrix products, arithmetic and copies ran while one was open for 0% of the time, Pallas kernels for 4%

profile of v2, /device:TPU:1, one launch (start us, length us, event | category | flops | bytes accessed | tf_op | source)
XLA Modules:
  0.0 109.3 jit_solution(424898091164494303)
XLA Ops:
  0.6 2.4 %pack.1 = (bf16[2,2,512,128]{3,2,1,0:T(8,128)(2,1)}, f32[2,512,128]{2,1,0:T(8,128)}, bf16[2,320,128]{2,1,0:T(8,128)(2,1)}, bf16[2,320,128]{2,1,0:T(8,128)(2,1)},...) custom-call(s32[2,2]{1,0:T(2,128)} %bitcast.19, s32[4]{0:T(128)} %bitcast.21, ...), custom_call_target="tpu_custom_call" | custom-call | tf_op jit(solution)/shard_map/pack/pallas_call | solution.py:240
  3.1 2.1 %collective-permute-start.2 = (bf16[2,336,128]{2,1,0:T(8,128)(2,1)}, bf16[2,336,128]{2,1,0:T(8,128)(2,1)S(1)}, u32[]{:S(2)}, u32[]{:S(2)}) collective-permute-start(bf16[2,336,128]{2,1,0:T(8,128)(2,1)} %get-tuple-element.17), channel_id=1, source_target_pairs={{0,1},{1,0},{2,3},{3,2},{4,5},{5,4},{6,7},{7,6},{8,9},{9,8},{10,11... | collective-permute-start | bytes 516104 | tf_op jit(solution)/shard_map/ppermute | solution.py:294
  5.2 1.2 %collective-permute-start = (bf16[2,320,128]{2,1,0:T(8,128)(2,1)}, bf16[2,320,128]{2,1,0:T(8,128)(2,1)S(1)}, u32[]{:S(2)}, u32[]{:S(2)}) collective-permute-start(bf16[2,320,128]{2,1,0:T(8,128)(2,1)} %get-tuple-element.15), channel_id=1, source_target_pairs={{0,2},{2,0},{4,6},{6,4},{8,10},{10,8},{12,14},{14,12},{16,18},{18,... | collective-permute-start | bytes 491528 | tf_op jit(solution)/shard_map/ppermute | solution.py:305
  6.4 4.2 %collective-permute-start.1 = (bf16[2,320,128]{2,1,0:T(8,128)(2,1)}, bf16[2,320,128]{2,1,0:T(8,128)(2,1)S(1)}, u32[]{:S(2)}, u32[]{:S(2)}) collective-permute-start(bf16[2,320,128]{2,1,0:T(8,128)(2,1)} %get-tuple-element.16), channel_id=1, source_target_pairs={{2,4},{4,2},{6,8},{8,6},{10,12},{12,10},{14,16},{16,14},{18,20},{2... | collective-permute-start | bytes 491528 | tf_op jit(solution)/shard_map/ppermute | solution.py:306
  10.5 0.1 collective-permute-start.3
  10.6 3.9 %collective-permute-start.4 = (bf16[2,80,128]{2,1,0:T(8,128)(2,1)}, bf16[2,80,128]{2,1,0:T(8,128)(2,1)S(1)}, u32[]{:S(2)}, u32[]{:S(2)}) collective-permute-start(bf16[2,80,128]{2,1,0:T(8,128)(2,1)} %get-tuple-element.19), channel_id=1, source_target_pairs={{2,5},{3,4},{4,3},{5,2},{6,9},{7,8},{8,7},{9,6},{10,13},{11,12},{1... | collective-permute-start | bytes 122888 | tf_op jit(solution)/shard_map/ppermute | solution.py:309
  14.6 1.5 %collective-permute-done.3.h3 = bf16[2,80,128]{2,1,0:T(8,128)(2,1)S(1)} collective-permute-done((bf16[2,80,128]{2,1,0:T(8,128)(2,1)}, bf16[2,80,128]{2,1,0:T(8,128)(2,1)S(1)}, u32[]{:S(2)}, u32[]{:S(2)}) %collective-permute-start.3) | collective-permute-done | bytes 40992 | tf_op jit(solution)/shard_map/ppermute | solution.py:308
  16.2 1.2 %collective-permute-done.4.h4 = bf16[2,80,128]{2,1,0:T(8,128)(2,1)S(1)} collective-permute-done((bf16[2,80,128]{2,1,0:T(8,128)(2,1)}, bf16[2,80,128]{2,1,0:T(8,128)(2,1)S(1)}, u32[]{:S(2)}, u32[]{:S(2)}) %collective-permute-start.4) | collective-permute-done | bytes 40992 | tf_op jit(solution)/shard_map/ppermute | solution.py:309
  17.4 0.0 collective-permute-done.h0
  17.4 0.0 collective-permute-done.1.h1
  17.4 0.0 copy-start.2
  17.4 0.0 collective-permute-done.2.h2
  17.4 0.0 copy-start
  17.4 0.0 copy-done.3
  17.4 0.6 copy-done.4
  18.0 0.1 copy-done.1
  18.1 0.1 copy-done.2
  18.2 0.0 copy-done
  18.2 11.8 %local_pass.1 = (f32[2,10,80,128]{3,2,1,0:T(8,128)}, f32[27,128,128]{2,1,0:T(8,128)}, bf16[27,128,128]{2,1,0:T(8,128)(2,1)}) custom-call(s32[2,27]{1,0:T(2,128)} %bitcast.20, s32[1]{0:T(128)} %bitcast.1.core, bf16[2,2,512,128]{3,2,1,0:T(8,128)(2,1)} %get-tuple-element.13.xg, f32[2,512,128]{2,1,0:T(8,128)} %get-tuple-element.14.mask_ref, ...), custom_call_target="tpu_custom_call" | custom-call | tf_op jit(solution)/shard_map/local_pass/pallas_call | solution.py:255
  30.0 0.0 collective-permute-start.5
  30.0 2.6 %collective-permute-done.5 = bf16[27,128,128]{2,1,0:T(8,128)(2,1)S(1)} collective-permute-done((bf16[27,128,128]{2,1,0:T(8,128)(2,1)}, bf16[27,128,128]{2,1,0:T(8,128)(2,1)S(1)}, u32[]{:S(2)}, u32[]{:S(2)}) %collective-permute-start.5) | collective-permute-done | bytes 884768 | tf_op jit(solution)/shard_map/ppermute | solution.py:294
  32.6 1.8 %add_convert_fusion = bf16[27,128,128]{2,1,0:T(8,128)(2,1)S(1)} fusion(f32[27,128,128]{2,1,0:T(8,128)} %get-tuple-element.21, bf16[27,128,128]{2,1,0:T(8,128)(2,1)S(1)} %collective-permute-done.5), kind=kLoop, calls=%fused_computation.1 | loop fusion | flops 1327104 | bytes 3538944 | tf_op jit(solution)/shard_map/convert_element_type | solution.py:323
  34.4 21.7 %all_to_all.20 = bf16[16,216,128]{2,1,0:T(8,128)(2,1)S(1)} all-to-all(bf16[16,216,128]{2,1,0:T(8,128)(2,1)S(1)} %bitcast.11), channel_id=1, replica_groups=mesh['z'=8,'x'=4,'yh'=2,'c'=2,'yl'=2] {'x','yh','yl'}, dimensions={0} | all-to-all | bytes 1769472 | tf_op jit(solution)/shard_map/all_to_all | solution.py:323
  56.1 0.1 convert_reduce_fusion
  56.2 17.2 %all_to_all.21 = f32[8,27,128]{2,1,0:T(8,128)S(1)} all-to-all(f32[8,27,128]{2,1,0:T(8,128)S(1)} %reshape.57), channel_id=1, replica_groups=mesh['z'=8,'x'=4,'yh'=2,'c'=2,'yl'=2] {'z'}, dimensions={0} | all-to-all | bytes 221184 | tf_op jit(solution)/shard_map/all_to_all | solution.py:326
  73.4 9.6 %all_to_all.22 = bf16[8,27,128]{2,1,0:T(8,128)(2,1)S(1)} all-to-all(bf16[8,27,128]{2,1,0:T(8,128)(2,1)S(1)} %broadcast_in_dim.6), channel_id=1, replica_groups=mesh['z'=8,'x'=4,'yh'=2,'c'=2,'yl'=2] {'z'}, dimensions={0} | all-to-all | bytes 110592 | tf_op jit(solution)/shard_map/all_to_all | solution.py:316
  83.1 0.1 broadcast_in_dim.15
  83.2 14.6 %all_to_all.23 = bf16[16,216,128]{2,1,0:T(8,128)(2,1)S(1)} all-to-all(bf16[16,216,128]{2,1,0:T(8,128)(2,1)S(1)} %broadcast_in_dim.15), channel_id=1, replica_groups=mesh['z'=8,'x'=4,'yh'=2,'c'=2,'yl'=2] {'x','yh','yl'}, dimensions={0} | all-to-all | bytes 1769472 | tf_op jit(solution)/shard_map/all_to_all | solution.py:316
  97.8 5.4 %collective-permute-start.6 = (bf16[27,128,128]{2,1,0:T(8,128)(2,1)S(1)}, bf16[27,128,128]{2,1,0:T(8,128)(2,1)S(1)}, u32[]{:S(2)}, u32[]{:S(2)}) collective-permute-start(bf16[27,128,128]{2,1,0:T(8,128)(2,1)S(1)} %bitcast.12), channel_id=1, source_target_pairs={{0,2},{2,0},{1,3},{3,1},{4,6},{6,4},{5,7},{7,5},{8,10},{10,8},{9,1... | collective-permute-start | bytes 2654216 | tf_op jit(solution)/shard_map/ppermute | solution.py:294
  103.2 4.0 %input_grad.1 = bf16[2,512,128]{2,1,0:T(8,128)(2,1)} custom-call(f32[2,10,80,128]{3,2,1,0:T(8,128)} %get-tuple-element.20.gp, f32[2,512,128]{2,1,0:T(8,128)} %get-tuple-element.14.mask_ref, bf16[2,512,128]{2,1,0:T(8,128)(2,1)} %bitcast.15, bf16[27,128,128]{2,1,0:T(8,128)(2,1)} %w1.3), custom_call_target="tpu_custom_call" | custom-call | tf_op jit(solution)/shard_map/input_grad/pallas_call | solution.py:279
  107.2 0.0 collective-permute-done.6
  107.2 2.0 %select_convert_fusion = (f32[27,128,128]{2,1,0:T(8,128)}, f32[27,128,128]{2,1,0:T(8,128)}) fusion(bf16[27,128,128]{2,1,0:T(8,128)(2,1)S(1)} %bitcast.13, bf16[27,128,128]{2,1,0:T(8,128)(2,1)S(1)} %collective-permute-done.6, pred[]{:T(512)S(6)} %eq.3), kind=kLoop, calls=%fused_computation.2 | loop fusion | flops 1769472 | bytes 5308417 | tf_op jit(solution)/shard_map/convert_element_type | solution.py:332
  (8 shorter events, 0.1 us)
Async XLA Ops:
  3.1 14.4 %collective-permute-start.2 = (bf16[2,336,128]{2,1,0:T(8,128)(2,1)}, bf16[2,336,128]{2,1,0:T(8,128)(2,1)S(1)}, u32[]{:S(2)}, u32[]{:S(2)}) collective-permute-start(bf16[2,336,128]{2,1,0:T(8,128)(2,1)} %get-tuple-element.17), channel_id=1, source_target_pairs={{0,1},{1,0},{2,3},{3,2},{4,5},{5,4},{6,7},{7,6},{8,9},{9,8},{10,11... | collective-permute-start | bytes 516104 | tf_op jit(solution)/shard_map/ppermute | solution.py:294
  5.2 12.2 %collective-permute-start = (bf16[2,320,128]{2,1,0:T(8,128)(2,1)}, bf16[2,320,128]{2,1,0:T(8,128)(2,1)S(1)}, u32[]{:S(2)}, u32[]{:S(2)}) collective-permute-start(bf16[2,320,128]{2,1,0:T(8,128)(2,1)} %get-tuple-element.15), channel_id=1, source_target_pairs={{0,2},{2,0},{4,6},{6,4},{8,10},{10,8},{12,14},{14,12},{16,18},{18,... | collective-permute-start | bytes 491528 | tf_op jit(solution)/shard_map/ppermute | solution.py:305
  6.4 11.0 %collective-permute-start.1 = (bf16[2,320,128]{2,1,0:T(8,128)(2,1)}, bf16[2,320,128]{2,1,0:T(8,128)(2,1)S(1)}, u32[]{:S(2)}, u32[]{:S(2)}) collective-permute-start(bf16[2,320,128]{2,1,0:T(8,128)(2,1)} %get-tuple-element.16), channel_id=1, source_target_pairs={{2,4},{4,2},{6,8},{8,6},{10,12},{12,10},{14,16},{16,14},{18,20},{2... | collective-permute-start | bytes 491528 | tf_op jit(solution)/shard_map/ppermute | solution.py:306
  10.5 5.6 %collective-permute-start.3 = (bf16[2,80,128]{2,1,0:T(8,128)(2,1)}, bf16[2,80,128]{2,1,0:T(8,128)(2,1)S(1)}, u32[]{:S(2)}, u32[]{:S(2)}) collective-permute-start(bf16[2,80,128]{2,1,0:T(8,128)(2,1)} %get-tuple-element.18), channel_id=1, source_target_pairs={{0,3},{1,2},{2,1},{3,0},{4,7},{5,6},{6,5},{7,4},{8,11},{9,10},{10,... | collective-permute-start | bytes 122888 | tf_op jit(solution)/shard_map/ppermute | solution.py:308
  10.6 6.7 %collective-permute-start.4 = (bf16[2,80,128]{2,1,0:T(8,128)(2,1)}, bf16[2,80,128]{2,1,0:T(8,128)(2,1)S(1)}, u32[]{:S(2)}, u32[]{:S(2)}) collective-permute-start(bf16[2,80,128]{2,1,0:T(8,128)(2,1)} %get-tuple-element.19), channel_id=1, source_target_pairs={{2,5},{3,4},{4,3},{5,2},{6,9},{7,8},{8,7},{9,6},{10,13},{11,12},{1... | collective-permute-start | bytes 122888 | tf_op jit(solution)/shard_map/ppermute | solution.py:309
  16.1 1.3 %copy-start.3 = (bf16[2,80,128]{2,1,0:T(8,128)(2,1)}, bf16[2,80,128]{2,1,0:T(8,128)(2,1)S(1)}, u32[]{:S(2)}) copy-start(bf16[2,80,128]{2,1,0:T(8,128)(2,1)S(1)} %collective-permute-done.3.h3) | copy-start | bytes 122884
  17.4 0.6 copy-start.4
  17.4 0.7 copy-start.1
  17.4 0.8 copy-start.2
  17.4 0.8 copy-start
  30.0 2.6 %collective-permute-start.5 = (bf16[27,128,128]{2,1,0:T(8,128)(2,1)}, bf16[27,128,128]{2,1,0:T(8,128)(2,1)S(1)}, u32[]{:S(2)}, u32[]{:S(2)}) collective-permute-start(bf16[27,128,128]{2,1,0:T(8,128)(2,1)} %get-tuple-element.22), channel_id=1, source_target_pairs={{0,2},{2,0},{1,3},{3,1},{4,6},{6,4},{5,7},{7,5},{8,10},{10,8},{9,1... | collective-permute-start | bytes 2654216 | tf_op jit(solution)/shard_map/ppermute | solution.py:294
  97.8 9.4 %collective-permute-start.6 = (bf16[27,128,128]{2,1,0:T(8,128)(2,1)S(1)}, bf16[27,128,128]{2,1,0:T(8,128)(2,1)S(1)}, u32[]{:S(2)}, u32[]{:S(2)}) collective-permute-start(bf16[27,128,128]{2,1,0:T(8,128)(2,1)S(1)} %bitcast.12), channel_id=1, source_target_pairs={{0,2},{2,0},{1,3},{3,1},{4,6},{6,4},{5,7},{7,5},{8,10},{10,8},{9,1... | collective-permute-start | bytes 2654216 | tf_op jit(solution)/shard_map/ppermute | solution.py:294

commit v3 on v2

--- a/solution.py
+++ b/solution.py
@@ -28,7 +28,7 @@
 
 VM = pl.BlockSpec(memory_space=pltpu.VMEM)
 SM = pl.BlockSpec(memory_space=pltpu.SMEM)
-PARAMS = pltpu.CompilerParams(vmem_limit_bytes=56 * 1024 * 1024)
+PARAMS = pltpu.CompilerParams(vmem_limit_bytes=32 * 1024 * 1024)
 
 
 def stack_rows(parts):
@@ -139,14 +139,14 @@
     return cut(0, E, 0, E), lambda: [cut(*part) for part in rim]
 
 
-def columns(tile, w, sign, cols, rim):
+def columns(tile, w, sign, cols, blocks, rim):
     for k, (dt, dx) in enumerate(WINDOWS):
         lane = slice(k * CH, (k + 1) * CH)
-        for b in range(BLK):
+        for i, b in enumerate(blocks):
             core, ring = pieces(tile, b, w, sign * dt, sign * dx)
-            cols[b * VOX : (b + 1) * VOX, lane] = core.astype(BF)
+            cols[i * VOX : (i + 1) * VOX, lane] = core.astype(BF)
             if rim:
-                at = ROWS + b * RIM
+                at = ROWS + i * RIM
                 cols[at : at + RIM, lane] = jnp.concatenate(ring(), axis=0).astype(BF)
 
 
@@ -191,8 +191,8 @@
     ]
     even = core[0] == 0
     build(targets, owns, table, even, (h0, h1, h2, h3, h4))
-    columns(xtile, 2, 1, xcol, True)
-    columns(gtile, 2, -1, gcol, True)
+    columns(xtile, 2, 1, xcol, range(BLK), True)
+    columns(gtile, 2, -1, gcol, range(BLK), True)
     parts = [pieces(mtile, b, 1, 0, 0) for b in range(BLK)]
     mask = jnp.concatenate([p[0] for p in parts] + parts[0][1]() + parts[1][1](), axis=0)
     for k in range(27):
@@ -228,11 +228,16 @@
         send_ref[k] = jnp.where(even, b, a).astype(BF)
 
 
-def input_kernel(gp, mask_ref, cot, w1, out, dcol, wide):
-    columns(gp, 1, -1, dcol, False)
-    total = transposed(dcol, w1, wide) * mask_ref[...].reshape(ROWS, CH)
-    total = cot[...].astype(F32).reshape(ROWS, CH) + total
-    out[...] = total.astype(BF).reshape(BLK, VOX, CH)
+def input_kernel(block, gp, mask_ref, cot, w1, *refs):
+    *before, out, dcol, wide = refs
+    columns(gp, 1, -1, dcol, [block], False)
+    total = transposed(dcol, w1, wide) * mask_ref[block]
+    total = (cot[block].astype(F32) + total).astype(BF)
+    if before:
+        out[:block] = before[0][...]
+        out[block] = total
+    else:
+        out[0] = total
 
 
 def pack(f, g, occ, sends, when, half, core):
@@ -275,19 +280,19 @@
     )(table, core, xg, mask, w1, w2, *halos)
 
 
-def input_grad(gp, mask, cot, w1):
+def input_grad(block, gp, mask, cot, w1, *before):
     return pl.pallas_call(
-        input_kernel,
-        out_shape=jax.ShapeDtypeStruct((BLK, VOX, CH), BF),
-        in_specs=[VM] * 4,
+        functools.partial(input_kernel, block),
+        out_shape=jax.ShapeDtypeStruct((BLK if before else 1, VOX, CH), BF),
+        in_specs=[VM] * (4 + len(before)),
         out_specs=VM,
         scratch_shapes=[
-            pltpu.VMEM((ROWS, 9 * CH), BF),
+            pltpu.VMEM((VOX, 9 * CH), BF),
             pltpu.VMEM((3 * CH, 9 * CH), BF),
         ],
         compiler_params=PARAMS,
-        name="input_grad",
-    )(gp, mask, cot, w1)
+        name="input_grad%d" % block,
+    )(gp, mask, cot, w1, *before)
 
 
 def swap(value, axis):
@@ -316,22 +321,24 @@
     return lax.all_to_all(copies, axes, 0, 0)
 
 
-def reduce_all(keep, send, scale):
-    total = keep + swap(send, "c").astype(F32)
+def reduce_all(keep, send, scale, early):
+    total = (keep + swap(send, "c").astype(F32)).astype(BF)
+    total, early = lax.optimization_barrier((total, early))
     plane = math.prod(lax.axis_size(axis) for axis in PLANE)
     rows = 27 * CH // plane
-    parts = lax.all_to_all(total.astype(BF).reshape(plane, rows, CH), PLANE, 0, 0)
+    parts = lax.all_to_all(total.reshape(plane, rows, CH), PLANE, 0, 0)
     total = jnp.sum(parts.astype(F32), axis=0)
     depth = lax.axis_size("z")
     parts = lax.all_to_all(total.reshape(depth, rows // depth, CH), "z", 0, 0)
     total = (jnp.sum(parts, axis=0) * scale).astype(BF)
     total = spread(total, ("z",)).reshape(rows, CH)
     mine = spread(total, PLANE).reshape(27, CH, CH)
+    mine, early = lax.optimization_barrier((mine, early))
     other = swap(mine, "c")
     even = lax.axis_index("c") == 0
     second = jnp.where(even, mine, other).astype(F32)
     first = jnp.where(even, other, mine).astype(F32)
-    return first, second
+    return first, second, early
 
 
 def body(features, cotangent, w_first, w_second, occupancy, neighbors, send_space, send_time):
@@ -344,9 +351,11 @@
     xg, mask, *messages = pack(f, g, occupancy.reshape(BLK, VOX), sends, when, half, core)
     halos = exchange(messages)
     gp, keep, send = local_pass(table, core, xg, mask, w_first, w_second, halos)
-    out = input_grad(gp, mask, g, w_first)
+    early = input_grad(0, gp, mask, g, w_first)
     devices = math.prod(lax.axis_size(axis) for axis in (*SPACE, TIME))
-    first, second = reduce_all(keep, send, 1.0 / math.sqrt(devices * ROWS))
+    scale = 1.0 / math.sqrt(devices * ROWS)
+    first, second, early = reduce_all(keep, send, scale, early)
+    out = input_grad(1, gp, mask, g, w_first, early)
     return out.reshape(features.shape), first, second
 
 

time: 110 us -> 109 us (level)
  local copies, waits for them, and re-layouts: 0.92 us -> 7.1 us
  Pallas kernels: 18.3 us -> 12.5 us
    unnamed x10 -> x20, local copies, waits for them, and re-layouts: 0.74 us -> 6.93 us
    pallas_call x1, Pallas kernels: 11.8 us -> 9.07 us  [local_pass(): pl.pallas_call(local_kernel, out_shape=[jax.ShapeDtypeStruct((BLK, E + 2,...]
    pallas_call x1, Pallas kernels: 2.43 us -> 0.85 us  [pack(): pl.pallas_call(pack_kernel, out_shape=[jax.ShapeDtypeStruct((2, BLK, VOX,...]
    pallas_call x1 -> x2, Pallas kernels: 4.04 us -> 2.54 us  [input_grad(): pl.pallas_call(functools.partial(input_kernel, block), out_shape=jax.Shap...]
    convert_element_type x1, other arithmetic: 1.76 us -> 0.27 us  [reduce_all(): total = (keep + swap(send, 'c').astype(F32)).astype(BF)]
    convert_element_type x1, other arithmetic: 2.02 us -> 3.19 us  [reduce_all(): second = jnp.where(even, mine, other).astype(F32)]
  transfers between devices with their start and end apart: 7 -> 7, of which waited for: 3 -> 4; matrix products, arithmetic and copies ran while one was open for 0% -> 0% of each run, Pallas kernels for 4% -> 2%
where the time goes in v3:
time: 109 us
  blocking collectives  63 us (58%)
  starting transfers between devices  17.1 us (16%)
  Pallas kernels  12.5 us (11%)
  local copies, waits for them, and re-layouts  7.1 us (7%)
  waiting for transfers between devices  4.61 us (4%)
  other arithmetic  3.59 us (3%)
    all_to_all x2, blocking collectives, spread(): return lax.all_to_all(copies, axes, 0, 0)  24.2 us
    all_to_all x1, blocking collectives, reduce_all(): parts = lax.all_to_all(total.reshape(plane, rows, CH), PLANE, 0, 0)  21.7 us
    all_to_all x1, blocking collectives, reduce_all(): parts = lax.all_to_all(total.reshape(depth, rows // depth, CH), 'z', 0, 0)  17.1 us
    pallas_call x1, Pallas kernels, local_pass(): pl.pallas_call(local_kernel, out_shape=[jax.ShapeDtypeStruct((BLK, E + 2,...  9.07 us
    ppermute x3, starting transfers between devices, swap(): return lax.ppermute(value, axis, [(0, 1), (1, 0)])  7.69 us
    unnamed x20, local copies, waits for them, and re-layouts  6.93 us
    ppermute x1, starting transfers between devices, exchange(): lax.ppermute(odd_side, SPACE, both(1))  4.17 us
    ppermute x1, starting transfers between devices, exchange(): lax.ppermute(odd_diag, (*SPACE, TIME), cross(both(1)))  3.95 us
  transfers between devices with their start and end apart: 7, of which 4 were waited for; matrix products, arithmetic and copies ran while one was open for 0% of the time, Pallas kernels for 2%

profile of v3, /device:TPU:1, one launch (start us, length us, event | category | flops | bytes accessed | tf_op | source)
XLA Modules:
  0.0 108.7 jit_solution(5402578860600820940)
XLA Ops:
  0.6 0.9 copy-done.2
  1.6 0.9 copy-done.5
  2.5 0.7 copy-done.6
  3.2 0.7 copy-done.7
  3.9 0.7 copy-done.9
  4.6 0.9 pack.1
  5.4 2.2 %collective-permute-start.2 = (bf16[2,336,128]{2,1,0:T(8,128)(2,1)S(1)}, bf16[2,336,128]{2,1,0:T(8,128)(2,1)S(1)}, u32[]{:S(2)}, u32[]{:S(2)}) collective-permute-start(bf16[2,336,128]{2,1,0:T(8,128)(2,1)S(1)} %get-tuple-element.21), channel_id=1, source_target_pairs={{0,1},{1,0},{2,3},{3,2},{4,5},{5,4},{6,7},{7,6},{8,9},{9,8},{10,11... | collective-permute-start | bytes 516104 | tf_op jit(solution)/shard_map/ppermute | solution.py:299
  7.6 1.2 %collective-permute-start = (bf16[2,320,128]{2,1,0:T(8,128)(2,1)S(1)}, bf16[2,320,128]{2,1,0:T(8,128)(2,1)S(1)}, u32[]{:S(2)}, u32[]{:S(2)}) collective-permute-start(bf16[2,320,128]{2,1,0:T(8,128)(2,1)S(1)} %get-tuple-element.19), channel_id=1, source_target_pairs={{0,2},{2,0},{4,6},{6,4},{8,10},{10,8},{12,14},{14,12},{16,18},{18,... | collective-permute-start | bytes 491528 | tf_op jit(solution)/shard_map/ppermute | solution.py:310
  8.8 4.2 %collective-permute-start.1 = (bf16[2,320,128]{2,1,0:T(8,128)(2,1)S(1)}, bf16[2,320,128]{2,1,0:T(8,128)(2,1)S(1)}, u32[]{:S(2)}, u32[]{:S(2)}) collective-permute-start(bf16[2,320,128]{2,1,0:T(8,128)(2,1)S(1)} %get-tuple-element.20), channel_id=1, source_target_pairs={{2,4},{4,2},{6,8},{8,6},{10,12},{12,10},{14,16},{16,14},{18,20},{2... | collective-permute-start | bytes 491528 | tf_op jit(solution)/shard_map/ppermute | solution.py:311
  13.0 0.1 collective-permute-start.3
  13.1 3.9 %collective-permute-start.4 = (bf16[2,80,128]{2,1,0:T(8,128)(2,1)S(1)}, bf16[2,80,128]{2,1,0:T(8,128)(2,1)S(1)}, u32[]{:S(2)}, u32[]{:S(2)}) collective-permute-start(bf16[2,80,128]{2,1,0:T(8,128)(2,1)S(1)} %get-tuple-element.23), channel_id=1, source_target_pairs={{2,5},{3,4},{4,3},{5,2},{6,9},{7,8},{8,7},{9,6},{10,13},{11,12},{1... | collective-permute-start | bytes 122888 | tf_op jit(solution)/shard_map/ppermute | solution.py:314
  17.0 1.3 %collective-permute-done.3.h3 = bf16[2,80,128]{2,1,0:T(8,128)(2,1)S(1)} collective-permute-done((bf16[2,80,128]{2,1,0:T(8,128)(2,1)S(1)}, bf16[2,80,128]{2,1,0:T(8,128)(2,1)S(1)}, u32[]{:S(2)}, u32[]{:S(2)}) %collective-permute-start.3) | collective-permute-done | bytes 40992 | tf_op jit(solution)/shard_map/ppermute | solution.py:313
  18.4 1.2 %collective-permute-done.4.h4 = bf16[2,80,128]{2,1,0:T(8,128)(2,1)S(1)} collective-permute-done((bf16[2,80,128]{2,1,0:T(8,128)(2,1)S(1)}, bf16[2,80,128]{2,1,0:T(8,128)(2,1)S(1)}, u32[]{:S(2)}, u32[]{:S(2)}) %collective-permute-start.4) | collective-permute-done | bytes 40992 | tf_op jit(solution)/shard_map/ppermute | solution.py:314
  19.6 0.0 copy-start
  19.6 1.2 %copy-done = bf16[27,128,128]{2,1,0:T(8,128)(2,1)S(1)} copy-done((bf16[27,128,128]{2,1,0:T(8,128)(2,1)S(1)}, bf16[27,128,128]{2,1,0:T(8,128)(2,1)}, u32[]{:S(2)}) %copy-start) | copy-done | bytes 884760
  20.8 1.2 %copy-done.4 = bf16[27,128,128]{2,1,0:T(8,128)(2,1)S(1)} copy-done((bf16[27,128,128]{2,1,0:T(8,128)(2,1)S(1)}, bf16[27,128,128]{2,1,0:T(8,128)(2,1)}, u32[]{:S(2)}) %copy-start.4) | copy-done | bytes 884760
  22.0 0.7 copy-done.8
  22.7 9.1 %local_pass.1 = (f32[2,10,80,128]{3,2,1,0:T(8,128)S(1)}, f32[27,128,128]{2,1,0:T(8,128)S(1)}, bf16[27,128,128]{2,1,0:T(8,128)(2,1)S(1)}) custom-call(s32[2,27]{1,0:T(2,128)S(1)} %bitcast.17, s32[1]{0:T(128)} %bitcast.1.core, bf16[2,2,512,128]{3,2,1,0:T(8,128)(2,1)S(1)} %get-tuple-element.17.xg, f32[2,512,128]{2,1,0:T(8,128)S(1)} %get-tuple-element.18.mask_ref, ...), custom_call_target="tpu_custom_call" | custom-call | tf_op jit(solution)/shard_map/local_pass/pallas_call | solution.py:260
  31.7 0.1 collective-permute-start.5
  31.9 0.9 input_grad0.1.refs_0_
  32.8 1.5 %collective-permute-done.5 = bf16[27,128,128]{2,1,0:T(8,128)(2,1)S(1)} collective-permute-done((bf16[27,128,128]{2,1,0:T(8,128)(2,1)S(1)}, bf16[27,128,128]{2,1,0:T(8,128)(2,1)S(1)}, u32[]{:S(2)}, u32[]{:S(2)}) %collective-permute-start.5) | collective-permute-done | bytes 884768 | tf_op jit(solution)/shard_map/ppermute | solution.py:299
  34.3 0.3 add_convert_fusion
  34.5 21.7 %all_to_all.20 = bf16[16,216,128]{2,1,0:T(8,128)(2,1)S(1)} all-to-all(bf16[16,216,128]{2,1,0:T(8,128)(2,1)S(1)} %bitcast.19), channel_id=1, replica_groups=mesh['z'=8,'x'=4,'yh'=2,'c'=2,'yl'=2] {'x','yh','yl'}, dimensions={0} | all-to-all | bytes 1769472 | tf_op jit(solution)/shard_map/all_to_all | solution.py:329
  56.2 0.1 convert_reduce_fusion
  56.3 17.1 %all_to_all.21 = f32[8,27,128]{2,1,0:T(8,128)S(1)} all-to-all(f32[8,27,128]{2,1,0:T(8,128)S(1)} %reshape.56), channel_id=1, replica_groups=mesh['z'=8,'x'=4,'yh'=2,'c'=2,'yl'=2] {'z'}, dimensions={0} | all-to-all | bytes 221184 | tf_op jit(solution)/shard_map/all_to_all | solution.py:332
  73.5 9.6 %all_to_all.22 = bf16[8,27,128]{2,1,0:T(8,128)(2,1)S(1)} all-to-all(bf16[8,27,128]{2,1,0:T(8,128)(2,1)S(1)} %broadcast_in_dim.6), channel_id=1, replica_groups=mesh['z'=8,'x'=4,'yh'=2,'c'=2,'yl'=2] {'z'}, dimensions={0} | all-to-all | bytes 110592 | tf_op jit(solution)/shard_map/all_to_all | solution.py:321
  83.2 0.1 broadcast_in_dim.15
  83.3 14.6 %all_to_all.23 = bf16[16,216,128]{2,1,0:T(8,128)(2,1)S(1)} all-to-all(bf16[16,216,128]{2,1,0:T(8,128)(2,1)S(1)} %broadcast_in_dim.15), channel_id=1, replica_groups=mesh['z'=8,'x'=4,'yh'=2,'c'=2,'yl'=2] {'x','yh','yl'}, dimensions={0} | all-to-all | bytes 1769472 | tf_op jit(solution)/shard_map/all_to_all | solution.py:321
  97.9 5.4 %collective-permute-start.6 = (bf16[27,128,128]{2,1,0:T(8,128)(2,1)S(1)}, bf16[27,128,128]{2,1,0:T(8,128)(2,1)}, u32[]{:S(2)}, u32[]{:S(2)}) collective-permute-start(bf16[27,128,128]{2,1,0:T(8,128)(2,1)S(1)} %bitcast.20), channel_id=1, source_target_pairs={{0,2},{2,0},{1,3},{3,1},{4,6},{6,4},{5,7},{7,5},{8,10},{10,8},{9,1... | collective-permute-start | bytes 2654216 | tf_op jit(solution)/shard_map/ppermute | solution.py:299
  103.3 1.6 %input_grad1.1 = bf16[2,512,128]{2,1,0:T(8,128)(2,1)} custom-call(f32[2,10,80,128]{3,2,1,0:T(8,128)S(1)} %get-tuple-element.24.gp, f32[2,512,128]{2,1,0:T(8,128)S(1)} %get-tuple-element.18.mask_ref, bf16[2,512,128]{2,1,0:T(8,128)(2,1)S(1)} %bitcast.13, bf16[27,128,128]{2,1,0:T(8,128)(2,1)S(1)} %copy-done.1, bf16[1,512,128]{2,1,0:T(8,128)(2,1)S(1)} %input_grad0.1.refs_0_), custom_call_target="tpu_custom_call" | custom-call | tf_op jit(solution)/shard_map/input_grad1/pallas_call | solution.py:284
  104.9 0.6 collective-permute-done.6
  105.5 3.2 %select_convert_fusion = (f32[27,128,128]{2,1,0:T(8,128)}, f32[27,128,128]{2,1,0:T(8,128)}) fusion(bf16[27,128,128]{2,1,0:T(8,128)(2,1)S(1)} %bitcast.21, bf16[27,128,128]{2,1,0:T(8,128)(2,1)} %collective-permute-done.6, pred[]{:T(512)S(6)} %eq.3), kind=kLoop, calls=%fused_computation.2 | loop fusion | flops 1769472 | bytes 5308417 | tf_op jit(solution)/shard_map/convert_element_type | solution.py:339
  (19 shorter events, 0.1 us)
Async XLA Ops:
  0.6 1.0 copy-start.2
  1.6 0.9 copy-start.5
  2.5 0.7 copy-start.6
  3.2 0.7 copy-start.7
  3.9 0.7 copy-start.9
  4.6 27.3 %copy-start.3 = (bf16[1,1,2,512,128]{4,3,2,1,0:T(8,128)(2,1)S(1)}, bf16[1,1,2,512,128]{4,3,2,1,0:T(8,128)(2,1)}, u32[]{:S(2)}) copy-start(bf16[1,1,2,512,128]{4,3,2,1,0:T(8,128)(2,1)} %param.9) | copy-start | bytes 786436
  5.4 14.2 %collective-permute-start.2 = (bf16[2,336,128]{2,1,0:T(8,128)(2,1)S(1)}, bf16[2,336,128]{2,1,0:T(8,128)(2,1)S(1)}, u32[]{:S(2)}, u32[]{:S(2)}) collective-permute-start(bf16[2,336,128]{2,1,0:T(8,128)(2,1)S(1)} %get-tuple-element.21), channel_id=1, source_target_pairs={{0,1},{1,0},{2,3},{3,2},{4,5},{5,4},{6,7},{7,6},{8,9},{9,8},{10,11... | collective-permute-start | bytes 516104 | tf_op jit(solution)/shard_map/ppermute | solution.py:299
  7.6 12.0 %collective-permute-start = (bf16[2,320,128]{2,1,0:T(8,128)(2,1)S(1)}, bf16[2,320,128]{2,1,0:T(8,128)(2,1)S(1)}, u32[]{:S(2)}, u32[]{:S(2)}) collective-permute-start(bf16[2,320,128]{2,1,0:T(8,128)(2,1)S(1)} %get-tuple-element.19), channel_id=1, source_target_pairs={{0,2},{2,0},{4,6},{6,4},{8,10},{10,8},{12,14},{14,12},{16,18},{18,... | collective-permute-start | bytes 491528 | tf_op jit(solution)/shard_map/ppermute | solution.py:310
  8.8 10.8 %collective-permute-start.1 = (bf16[2,320,128]{2,1,0:T(8,128)(2,1)S(1)}, bf16[2,320,128]{2,1,0:T(8,128)(2,1)S(1)}, u32[]{:S(2)}, u32[]{:S(2)}) collective-permute-start(bf16[2,320,128]{2,1,0:T(8,128)(2,1)S(1)} %get-tuple-element.20), channel_id=1, source_target_pairs={{2,4},{4,2},{6,8},{8,6},{10,12},{12,10},{14,16},{16,14},{18,20},{2... | collective-permute-start | bytes 491528 | tf_op jit(solution)/shard_map/ppermute | solution.py:311
  13.0 5.4 %collective-permute-start.3 = (bf16[2,80,128]{2,1,0:T(8,128)(2,1)S(1)}, bf16[2,80,128]{2,1,0:T(8,128)(2,1)S(1)}, u32[]{:S(2)}, u32[]{:S(2)}) collective-permute-start(bf16[2,80,128]{2,1,0:T(8,128)(2,1)S(1)} %get-tuple-element.22), channel_id=1, source_target_pairs={{0,3},{1,2},{2,1},{3,0},{4,7},{5,6},{6,5},{7,4},{8,11},{9,10},{10,... | collective-permute-start | bytes 122888 | tf_op jit(solution)/shard_map/ppermute | solution.py:313
  13.1 6.5 %collective-permute-start.4 = (bf16[2,80,128]{2,1,0:T(8,128)(2,1)S(1)}, bf16[2,80,128]{2,1,0:T(8,128)(2,1)S(1)}, u32[]{:S(2)}, u32[]{:S(2)}) collective-permute-start(bf16[2,80,128]{2,1,0:T(8,128)(2,1)S(1)} %get-tuple-element.23), channel_id=1, source_target_pairs={{2,5},{3,4},{4,3},{5,2},{6,9},{7,8},{8,7},{9,6},{10,13},{11,12},{1... | collective-permute-start | bytes 122888 | tf_op jit(solution)/shard_map/ppermute | solution.py:314
  19.6 1.2 %copy-start = (bf16[27,128,128]{2,1,0:T(8,128)(2,1)S(1)}, bf16[27,128,128]{2,1,0:T(8,128)(2,1)}, u32[]{:S(2)}) copy-start(bf16[27,128,128]{2,1,0:T(8,128)(2,1)} %w1.5) | copy-start | bytes 2654212
  20.8 1.2 %copy-start.4 = (bf16[27,128,128]{2,1,0:T(8,128)(2,1)S(1)}, bf16[27,128,128]{2,1,0:T(8,128)(2,1)}, u32[]{:S(2)}) copy-start(bf16[27,128,128]{2,1,0:T(8,128)(2,1)} %w2.1) | copy-start | bytes 2654212
  22.0 0.7 copy-start.8
  22.7 9.2 %copy-start.1 = (bf16[27,128,128]{2,1,0:T(8,128)(2,1)S(1)}, bf16[27,128,128]{2,1,0:T(8,128)(2,1)}, u32[]{:S(2)}) copy-start(bf16[27,128,128]{2,1,0:T(8,128)(2,1)} %w1.5) | copy-start | bytes 2654212
  31.7 2.5 %collective-permute-start.5 = (bf16[27,128,128]{2,1,0:T(8,128)(2,1)S(1)}, bf16[27,128,128]{2,1,0:T(8,128)(2,1)S(1)}, u32[]{:S(2)}, u32[]{:S(2)}) collective-permute-start(bf16[27,128,128]{2,1,0:T(8,128)(2,1)S(1)} %get-tuple-element.26), channel_id=1, source_target_pairs={{0,2},{2,0},{1,3},{3,1},{4,6},{6,4},{5,7},{7,5},{8,10},{10,8},{9,1... | collective-permute-start | bytes 2654216 | tf_op jit(solution)/shard_map/ppermute | solution.py:299
  97.9 7.6 %collective-permute-start.6 = (bf16[27,128,128]{2,1,0:T(8,128)(2,1)S(1)}, bf16[27,128,128]{2,1,0:T(8,128)(2,1)}, u32[]{:S(2)}, u32[]{:S(2)}) collective-permute-start(bf16[27,128,128]{2,1,0:T(8,128)(2,1)S(1)} %bitcast.20), channel_id=1, source_target_pairs={{0,2},{2,0},{1,3},{3,1},{4,6},{6,4},{5,7},{7,5},{8,10},{10,8},{9,1... | collective-permute-start | bytes 2654216 | tf_op jit(solution)/shard_map/ppermute | solution.py:299

commit v4 on v3

--- a/solution.py
+++ b/solution.py
@@ -28,6 +28,9 @@
 
 VM = pl.BlockSpec(memory_space=pltpu.VMEM)
 SM = pl.BlockSpec(memory_space=pltpu.SMEM)
+HB = pl.BlockSpec(memory_space=pltpu.HBM)
+DMA = pltpu.SemaphoreType.DMA
+I32 = jnp.int32
 PARAMS = pltpu.CompilerParams(vmem_limit_bytes=32 * 1024 * 1024)
 
 
@@ -35,8 +38,18 @@
     return jnp.concatenate([part.reshape(-1, CH) for part in parts], axis=0)
 
 
-def pack_kernel(sends, when, half, core, f_ref, g_ref, occ_ref, xg_ref, mask_ref, *messages):
-    even_ref, odd_ref, time_ref, even_diag, odd_diag = messages
+def load(sems, pairs):
+    copies = [pltpu.make_async_copy(src, dst, sems.at[i]) for i, (src, dst) in enumerate(pairs)]
+    for copy in copies:
+        copy.start()
+    return copies
+
+
+def pack_kernel(half, core, f, g, occ, sends_in, when_in, xg_ref, mask_ref, *refs):
+    even_ref, odd_ref, time_ref, even_diag, odd_diag, *scratch, sems = refs
+    f_ref, g_ref, occ_ref, sends, when = scratch
+    for copy in load(sems, list(zip((f, g, occ, sends_in, when_in), scratch))):
+        copy.wait()
     even = core[0] == 0
     sides, times, corners = [], [], []
     for b in range(BLK):
@@ -65,7 +78,7 @@
     rows = lax.broadcasted_iota(jnp.int32, (2 * E, CH), 0)
     note = jnp.zeros((2 * E, CH), F32)
     for p in range(2 * BLK):
-        note = jnp.where(rows == p, when[p].astype(F32), note)
+        note = jnp.where(rows == p, when[0, p].astype(F32), note)
     for side_ref, diag_ref, up in ((even_ref, even_diag, even), (odd_ref, odd_diag, ~even)):
         for slot in range(BLK):
             index = jnp.where(up, sends[1, slot], sends[0, slot])
@@ -86,7 +99,7 @@
     return chosen.reshape(value.shape)
 
 
-def build(targets, owns, table, even, halos):
+def build(targets, owns, table, ready, even, halos):
     even_side, odd_side, across, even_diag, odd_diag = (
         [ref[j].astype(F32) for j in range(BLK)] for ref in halos
     )
@@ -100,6 +113,7 @@
     for (tile, w, _, _), own in zip(targets, owns):
         for b in range(BLK):
             tile[b, w : w + E, w * E : w * E + FACE] = own[b]
+    ready()
     for b in range(BLK):
         for dt, dx in WINDOWS:
             if dt == 0 and dx == 0:
@@ -179,9 +193,11 @@
 
 
 def local_kernel(
-    table, core, xg, mask_ref, w1, w2, h0, h1, h2, h3, h4,
-    gp_ref, keep_ref, send_ref, xtile, gtile, mtile, xcol, gcol, wide, tall,
+    core, xg, mask_ref, table_in, w1_in, w2_in, h0, h1, h2, h3, h4,
+    gp_ref, keep_ref, send_ref,
+    xtile, gtile, mtile, xcol, gcol, wide, tall, table, w1, w2, sems,
 ):
+    copies = load(sems, [(table_in, table), (w1_in, w1), (w2_in, w2)])
     owns = [[xg[i, b].astype(F32).reshape(E, FACE, CH) for b in range(BLK)] for i in range(2)]
     owns.append([mask_ref[b].reshape(E, FACE, CH) for b in range(BLK)])
     targets = [
@@ -190,11 +206,12 @@
         (mtile, 1, 4 * FACE, 8 * E),
     ]
     even = core[0] == 0
-    build(targets, owns, table, even, (h0, h1, h2, h3, h4))
+    build(targets, owns, table, copies[0].wait, even, (h0, h1, h2, h3, h4))
     columns(xtile, 2, 1, xcol, range(BLK), True)
     columns(gtile, 2, -1, gcol, range(BLK), True)
     parts = [pieces(mtile, b, 1, 0, 0) for b in range(BLK)]
     mask = jnp.concatenate([p[0] for p in parts] + parts[0][1]() + parts[1][1](), axis=0)
+    copies[1].wait()
     for k in range(27):
         w, d = divmod(k, 3)
         tall[w * CH : (w + 1) * CH, d * CH : (d + 1) * CH] = w1[k]
@@ -204,6 +221,7 @@
     hidden = (pre[:ROWS] * sig[:ROWS] * mask[:ROWS]).astype(BF).astype(F32)
     shifted = jnp.concatenate([shift(hidden, -1), hidden, shift(hidden, 1)], axis=1).astype(BF)
     second = outer(shifted, gcol[:ROWS])
+    copies[2].wait()
     grad_hidden = transposed(gcol, w2, wide)
     grad_pre = (grad_hidden * sig * (1.0 + pre * (1.0 - sig)) * mask).astype(BF).astype(F32)
     for b in range(BLK):
@@ -228,16 +246,40 @@
         send_ref[k] = jnp.where(even, b, a).astype(BF)
 
 
-def input_kernel(block, gp, mask_ref, cot, w1, *refs):
-    *before, out, dcol, wide = refs
+def input_block(block, gp, mask_ref, cot, w1, dcol, wide):
     columns(gp, 1, -1, dcol, [block], False)
     total = transposed(dcol, w1, wide) * mask_ref[block]
-    total = (cot[block].astype(F32) + total).astype(BF)
-    if before:
-        out[:block] = before[0][...]
-        out[block] = total
-    else:
-        out[0] = total
+    return (cot[block].astype(F32) + total).astype(BF)
+
+
+def early_kernel(gp, mask_ref, cot, w1, out, dcol, wide):
+    out[...] = input_block(0, gp, mask_ref, cot, w1, dcol, wide)
+
+
+def to_half(core, mine, value, first, second, sem, act):
+    even = (core[0] == 0) if mine else (core[0] != 0)
+    for flag, target in ((even, second), (~even, first)):
+        copy = pltpu.make_async_copy(value, target, sem)
+        pl.when(flag)(copy.start if act == "start" else copy.wait)
+
+
+def late_kernel(core, gp, mask_ref, cot, w1, early, mine, out, first, second, *scratch):
+    dcol, wide, value, sem = scratch
+    value[...] = mine[...].astype(F32)
+    to_half(core, True, value, first, second, sem, "start")
+    out[0] = early[...]
+    out[1] = input_block(1, gp, mask_ref, cot, w1, dcol, wide)
+    to_half(core, True, value, first, second, sem, "wait")
+
+
+def last_kernel(core, other, first_in, second_in, first, second, value, sem):
+    value[...] = other[...].astype(F32)
+    to_half(core, False, value, first, second, sem, "start")
+    to_half(core, False, value, first, second, sem, "wait")
+
+
+def in_place(value):
+    return pltpu.with_memory_space_constraint(value, pltpu.HBM)
 
 
 def pack(f, g, occ, sends, when, half, core):
@@ -249,11 +291,19 @@
             jax.ShapeDtypeStruct((BLK, VOX, CH), F32),
             *[jax.ShapeDtypeStruct((BLK, rows, CH), BF) for rows in shapes],
         ],
-        in_specs=[SM] * 4 + [VM] * 3,
+        in_specs=[SM] * 2 + [HB] * 5,
         out_specs=[VM] * 7,
+        scratch_shapes=[
+            pltpu.VMEM((BLK, VOX, CH), BF),
+            pltpu.VMEM((BLK, VOX, CH), BF),
+            pltpu.VMEM((BLK, VOX), I32),
+            pltpu.SMEM((2, BLK), I32),
+            pltpu.SMEM((1, 2 * BLK), I32),
+            DMA((5,)),
+        ],
         compiler_params=PARAMS,
         name="pack",
-    )(sends, when, half, core, f, g, occ)
+    )(half, core, *map(in_place, (f, g, occ, sends, when)))
 
 
 def local_pass(table, core, xg, mask, w1, w2, halos):
@@ -264,7 +314,7 @@
             jax.ShapeDtypeStruct((27, CH, CH), F32),
             jax.ShapeDtypeStruct((27, CH, CH), BF),
         ],
-        in_specs=[SM] * 2 + [VM] * 9,
+        in_specs=[SM] + [VM] * 2 + [HB] * 3 + [VM] * 5,
         out_specs=[VM] * 3,
         scratch_shapes=[
             pltpu.VMEM((BLK, E + 4, (E + 4) * E, CH), F32),
@@ -274,25 +324,57 @@
             pltpu.VMEM((ROWS + BLK * RIM, 9 * CH), BF),
             pltpu.VMEM((3 * CH, 9 * CH), BF),
             pltpu.VMEM((9 * CH, 3 * CH), BF),
+            pltpu.SMEM((BLK, 27), I32),
+            pltpu.VMEM((27, CH, CH), BF),
+            pltpu.VMEM((27, CH, CH), BF),
+            DMA((3,)),
         ],
         compiler_params=PARAMS,
         name="local_pass",
-    )(table, core, xg, mask, w1, w2, *halos)
-
-
-def input_grad(block, gp, mask, cot, w1, *before):
+    )(core, xg, mask, *map(in_place, (table, w1, w2)), *halos)
+
+
+INPUT_SCRATCH = [pltpu.VMEM((VOX, 9 * CH), BF), pltpu.VMEM((3 * CH, 9 * CH), BF)]
+HALF_SCRATCH = [pltpu.VMEM((27, CH, CH), F32), DMA(())]
+
+
+def early_grad(gp, mask, cot, w1):
     return pl.pallas_call(
-        functools.partial(input_kernel, block),
-        out_shape=jax.ShapeDtypeStruct((BLK if before else 1, VOX, CH), BF),
-        in_specs=[VM] * (4 + len(before)),
+        early_kernel,
+        out_shape=jax.ShapeDtypeStruct((VOX, CH), BF),
+        in_specs=[VM] * 4,
         out_specs=VM,
-        scratch_shapes=[
-            pltpu.VMEM((VOX, 9 * CH), BF),
-            pltpu.VMEM((3 * CH, 9 * CH), BF),
-        ],
+        scratch_shapes=INPUT_SCRATCH,
         compiler_params=PARAMS,
-        name="input_grad%d" % block,
-    )(gp, mask, cot, w1, *before)
+        name="early_grad",
+    )(gp, mask, cot, w1)
+
+
+def late_grad(core, gp, mask, cot, w1, early, mine):
+    weights = jax.ShapeDtypeStruct((27, CH, CH), F32)
+    return pl.pallas_call(
+        late_kernel,
+        out_shape=[jax.ShapeDtypeStruct((BLK, VOX, CH), BF), weights, weights],
+        in_specs=[SM] + [VM] * 6,
+        out_specs=[VM, HB, HB],
+        scratch_shapes=INPUT_SCRATCH + HALF_SCRATCH,
+        compiler_params=PARAMS,
+        name="late_grad",
+    )(core, gp, mask, cot, w1, early, mine)
+
+
+def last_half(core, other, first, second):
+    weights = jax.ShapeDtypeStruct((27, CH, CH), F32)
+    return pl.pallas_call(
+        last_kernel,
+        out_shape=[weights, weights],
+        in_specs=[SM, VM, HB, HB],
+        out_specs=[HB, HB],
+        scratch_shapes=HALF_SCRATCH,
+        input_output_aliases={2: 0, 3: 1},
+        compiler_params=PARAMS,
+        name="last_half",
+    )(core, other, first, second)
 
 
 def swap(value, axis):
@@ -334,11 +416,7 @@
     total = spread(total, ("z",)).reshape(rows, CH)
     mine = spread(total, PLANE).reshape(27, CH, CH)
     mine, early = lax.optimization_barrier((mine, early))
-    other = swap(mine, "c")
-    even = lax.axis_index("c") == 0
-    second = jnp.where(even, mine, other).astype(F32)
-    first = jnp.where(even, other, mine).astype(F32)
-    return first, second, early
+    return mine, swap(mine, "c"), early
 
 
 def body(features, cotangent, w_first, w_second, occupancy, neighbors, send_space, send_time):
@@ -347,15 +425,16 @@
     core = lax.axis_index("c").astype(jnp.int32).reshape(1)
     sends = send_space.reshape(2, BLK)
     table = neighbors.reshape(BLK, 27)
-    when = send_time.reshape(2 * BLK)
+    when = send_time.reshape(1, 2 * BLK)
     xg, mask, *messages = pack(f, g, occupancy.reshape(BLK, VOX), sends, when, half, core)
     halos = exchange(messages)
     gp, keep, send = local_pass(table, core, xg, mask, w_first, w_second, halos)
-    early = input_grad(0, gp, mask, g, w_first)
+    early = early_grad(gp, mask, g, w_first)
     devices = math.prod(lax.axis_size(axis) for axis in (*SPACE, TIME))
     scale = 1.0 / math.sqrt(devices * ROWS)
-    first, second, early = reduce_all(keep, send, scale, early)
-    out = input_grad(1, gp, mask, g, w_first, early)
+    mine, other, early = reduce_all(keep, send, scale, early)
+    out, first, second = late_grad(core, gp, mask, g, w_first, early, mine)
+    first, second = last_half(core, other, first, second)
     return out.reshape(features.shape), first, second
 
 

time: 109 us -> 102 us (0.936)
  local copies, waits for them, and re-layouts: 7.1 us -> 0.18 us
  Pallas kernels: 12.5 us -> 16.4 us
  other arithmetic: 3.59 us -> 0.41 us
    unnamed x20 -> x4, local copies, waits for them, and re-layouts: 6.93 us -> 0.01 us
    convert_element_type x1 -> x0, other arithmetic: 3.19 us -> none  [reduce_all(): second = jnp.where(even, mine, other).astype(F32)]
    pallas_call x2 -> x3, Pallas kernels: 2.54 us -> 5.21 us  [the longest x1 2.96 us: late_grad(): pl.pallas_call(late_kernel, out_shape=[jax.ShapeDtypeStruct((BLK, VOX, CH...]
  transfers between devices with their start and end apart: 7 -> 7, of which waited for: 4 -> 3; matrix products, arithmetic and copies ran while one was open for 0% -> 0% of each run, Pallas kernels for 2% -> 4%
where the time goes in v4:
time: 102 us
  blocking collectives  63 us (62%)
  starting transfers between devices  17.1 us (17%)
  Pallas kernels  16.4 us (16%)
  waiting for transfers between devices  4.05 us (4%)
    all_to_all x2, blocking collectives, spread(): return lax.all_to_all(copies, axes, 0, 0)  24.2 us
    all_to_all x1, blocking collectives, reduce_all(): parts = lax.all_to_all(total.reshape(plane, rows, CH), PLANE, 0, 0)  21.7 us
    all_to_all x1, blocking collectives, reduce_all(): parts = lax.all_to_all(total.reshape(depth, rows // depth, CH), 'z', 0, 0)  17.1 us
    pallas_call x1, Pallas kernels, local_pass(): pl.pallas_call(local_kernel, out_shape=[jax.ShapeDtypeStruct((BLK, E + 2,...  9.74 us
    ppermute x3, starting transfers between devices, swap(): return lax.ppermute(value, axis, [(0, 1), (1, 0)])  7.69 us
    ppermute x1, starting transfers between devices, exchange(): lax.ppermute(odd_side, SPACE, both(1))  4.17 us
    ppermute x1, starting transfers between devices, exchange(): lax.ppermute(odd_diag, (*SPACE, TIME), cross(both(1)))  3.95 us
    pallas_call x1, Pallas kernels, late_grad(): pl.pallas_call(late_kernel, out_shape=[jax.ShapeDtypeStruct((BLK, VOX, CH...  2.96 us
  transfers between devices with their start and end apart: 7, of which 3 were waited for; matrix products, arithmetic and copies ran while one was open for 0% of the time, Pallas kernels for 4%

profile of v4, /device:TPU:1, one launch (start us, length us, event | category | flops | bytes accessed | tf_op | source)
XLA Modules:
  0.0 101.9 jit_solution(10014370449344314412)
XLA Ops:
  0.6 1.4 %pack.1 = (bf16[2,2,512,128]{3,2,1,0:T(8,128)(2,1)S(1)}, f32[2,512,128]{2,1,0:T(8,128)S(1)}, bf16[2,320,128]{2,1,0:T(8,128)(2,1)S(1)}, bf16[2,320,128]{2,1,0:T(8...) custom-call(s32[1]{0:T(128)} %bitcast.1.half, ...), custom_call_target="tpu_custom_call" | custom-call | tf_op jit(solution)/shard_map/pack/pallas_call | solution.py:287
  2.0 0.0 copy-start
  2.1 0.0 copy-start.1
  2.1 2.2 %collective-permute-start.2 = (bf16[2,336,128]{2,1,0:T(8,128)(2,1)S(1)}, bf16[2,336,128]{2,1,0:T(8,128)(2,1)S(1)}, u32[]{:S(2)}, u32[]{:S(2)}) collective-permute-start(bf16[2,336,128]{2,1,0:T(8,128)(2,1)S(1)} %get-tuple-element.26), channel_id=1, source_target_pairs={{0,1},{1,0},{2,3},{3,2},{4,5},{5,4},{6,7},{7,6},{8,9},{9,8},{10,11... | collective-permute-start | bytes 516104 | tf_op jit(solution)/shard_map/ppermute | solution.py:381
  4.3 1.2 %collective-permute-start = (bf16[2,320,128]{2,1,0:T(8,128)(2,1)S(1)}, bf16[2,320,128]{2,1,0:T(8,128)(2,1)S(1)}, u32[]{:S(2)}, u32[]{:S(2)}) collective-permute-start(bf16[2,320,128]{2,1,0:T(8,128)(2,1)S(1)} %get-tuple-element.24), channel_id=1, source_target_pairs={{0,2},{2,0},{4,6},{6,4},{8,10},{10,8},{12,14},{14,12},{16,18},{18,... | collective-permute-start | bytes 491528 | tf_op jit(solution)/shard_map/ppermute | solution.py:392
  5.5 4.2 %collective-permute-start.1 = (bf16[2,320,128]{2,1,0:T(8,128)(2,1)S(1)}, bf16[2,320,128]{2,1,0:T(8,128)(2,1)S(1)}, u32[]{:S(2)}, u32[]{:S(2)}) collective-permute-start(bf16[2,320,128]{2,1,0:T(8,128)(2,1)S(1)} %get-tuple-element.25), channel_id=1, source_target_pairs={{2,4},{4,2},{6,8},{8,6},{10,12},{12,10},{14,16},{16,14},{18,20},{2... | collective-permute-start | bytes 491528 | tf_op jit(solution)/shard_map/ppermute | solution.py:393
  9.6 0.1 collective-permute-start.3
  9.7 3.9 %collective-permute-start.4 = (bf16[2,80,128]{2,1,0:T(8,128)(2,1)S(1)}, bf16[2,80,128]{2,1,0:T(8,128)(2,1)S(1)}, u32[]{:S(2)}, u32[]{:S(2)}) collective-permute-start(bf16[2,80,128]{2,1,0:T(8,128)(2,1)S(1)} %get-tuple-element.28), channel_id=1, source_target_pairs={{2,5},{3,4},{4,3},{5,2},{6,9},{7,8},{8,7},{9,6},{10,13},{11,12},{1... | collective-permute-start | bytes 122888 | tf_op jit(solution)/shard_map/ppermute | solution.py:396
  13.7 1.3 %collective-permute-done.3.h3 = bf16[2,80,128]{2,1,0:T(8,128)(2,1)S(1)} collective-permute-done((bf16[2,80,128]{2,1,0:T(8,128)(2,1)S(1)}, bf16[2,80,128]{2,1,0:T(8,128)(2,1)S(1)}, u32[]{:S(2)}, u32[]{:S(2)}) %collective-permute-start.3) | collective-permute-done | bytes 40992 | tf_op jit(solution)/shard_map/ppermute | solution.py:395
  15.0 1.2 %collective-permute-done.4.h4 = bf16[2,80,128]{2,1,0:T(8,128)(2,1)S(1)} collective-permute-done((bf16[2,80,128]{2,1,0:T(8,128)(2,1)S(1)}, bf16[2,80,128]{2,1,0:T(8,128)(2,1)S(1)}, u32[]{:S(2)}, u32[]{:S(2)}) %collective-permute-start.4) | collective-permute-done | bytes 40992 | tf_op jit(solution)/shard_map/ppermute | solution.py:396
  16.3 0.0 collective-permute-done.h0
  16.3 0.0 collective-permute-done.1.h1
  16.3 0.0 collective-permute-done.2.h2
  16.3 9.7 %local_pass.1 = (f32[2,10,80,128]{3,2,1,0:T(8,128)S(1)}, f32[27,128,128]{2,1,0:T(8,128)S(1)}, bf16[27,128,128]{2,1,0:T(8,128)(2,1)S(1)}) custom-call(s32[1]{0:T(128)} %bitcast.core, bf16[2,2,512,128]{3,2,1,0:T(8,128)(2,1)S(1)} %get-tuple-element.22.xg, f32[2,512,128]{2,1,0:T(8,128)S(1)} %get-tuple-element.23.mask_ref, s32[2,27]{1,0:T(2,128)} %bitcast.20, ...), custom_call_target="tpu_custom_call" | custom-call | tf_op jit(solution)/shard_map/local_pass/pallas_call | solution.py:310
  26.0 0.1 collective-permute-start.5
  26.1 0.0 copy-done
  26.1 0.0 copy-done.1
  26.2 0.9 early_grad.1.early
  27.1 1.5 %collective-permute-done.5 = bf16[27,128,128]{2,1,0:T(8,128)(2,1)S(1)} collective-permute-done((bf16[27,128,128]{2,1,0:T(8,128)(2,1)S(1)}, bf16[27,128,128]{2,1,0:T(8,128)(2,1)S(1)}, u32[]{:S(2)}, u32[]{:S(2)}) %collective-permute-start.5) | collective-permute-done | bytes 884768 | tf_op jit(solution)/shard_map/ppermute | solution.py:381
  28.5 0.3 add_convert_fusion
  28.8 21.7 %all_to_all.20 = bf16[16,216,128]{2,1,0:T(8,128)(2,1)S(1)} all-to-all(bf16[16,216,128]{2,1,0:T(8,128)(2,1)S(1)} %bitcast.16), channel_id=1, replica_groups=mesh['z'=8,'x'=4,'yh'=2,'c'=2,'yl'=2] {'x','yh','yl'}, dimensions={0} | all-to-all | bytes 1769472 | tf_op jit(solution)/shard_map/all_to_all | solution.py:411
  50.5 0.1 convert_reduce_fusion
  50.6 17.1 %all_to_all.21 = f32[8,27,128]{2,1,0:T(8,128)S(1)} all-to-all(f32[8,27,128]{2,1,0:T(8,128)S(1)} %reshape.56), channel_id=1, replica_groups=mesh['z'=8,'x'=4,'yh'=2,'c'=2,'yl'=2] {'z'}, dimensions={0} | all-to-all | bytes 221184 | tf_op jit(solution)/shard_map/all_to_all | solution.py:414
  67.8 9.6 %all_to_all.22 = bf16[8,27,128]{2,1,0:T(8,128)(2,1)S(1)} all-to-all(bf16[8,27,128]{2,1,0:T(8,128)(2,1)S(1)} %broadcast_in_dim.6), channel_id=1, replica_groups=mesh['z'=8,'x'=4,'yh'=2,'c'=2,'yl'=2] {'z'}, dimensions={0} | all-to-all | bytes 110592 | tf_op jit(solution)/shard_map/all_to_all | solution.py:403
  77.5 0.1 broadcast_in_dim.15
  77.6 14.6 %all_to_all.23 = bf16[16,216,128]{2,1,0:T(8,128)(2,1)S(1)} all-to-all(bf16[16,216,128]{2,1,0:T(8,128)(2,1)S(1)} %broadcast_in_dim.15), channel_id=1, replica_groups=mesh['z'=8,'x'=4,'yh'=2,'c'=2,'yl'=2] {'x','yh','yl'}, dimensions={0} | all-to-all | bytes 1769472 | tf_op jit(solution)/shard_map/all_to_all | solution.py:403
  92.2 5.4 %collective-permute-start.6 = (bf16[27,128,128]{2,1,0:T(8,128)(2,1)S(1)}, bf16[27,128,128]{2,1,0:T(8,128)(2,1)S(1)}, u32[]{:S(2)}, u32[]{:S(2)}) collective-permute-start(bf16[27,128,128]{2,1,0:T(8,128)(2,1)S(1)} %bitcast.11), channel_id=1, source_target_pairs={{0,2},{2,0},{1,3},{3,1},{4,6},{6,4},{5,7},{7,5},{8,10},{10,8},{9,1... | collective-permute-start | bytes 2654216 | tf_op jit(solution)/shard_map/ppermute | solution.py:381
  97.6 3.0 %late_grad.1 = (bf16[2,512,128]{2,1,0:T(8,128)(2,1)}, f32[27,128,128]{2,1,0:T(8,128)}, f32[27,128,128]{2,1,0:T(8,128)}) custom-call(s32[1]{0:T(128)} %bitcast.core, f32[2,10,80,128]{3,2,1,0:T(8,128)S(1)} %get-tuple-element.29.gp, f32[2,512,128]{2,1,0:T(8,128)S(1)} %get-tuple-element.23.mask_ref, bf16[2,512,128]{2,1,0:T(8,128)(2,1)S(1)} %bitcast.15, ...), custom_call_target="tpu_custom_call" | custom-call | tf_op jit(solution)/shard_map/late_grad/pallas_call | solution.py:355
  100.6 0.0 collective-permute-done.6.other
  100.6 1.3 %last_half.1 = (f32[27,128,128]{2,1,0:T(8,128)}, f32[27,128,128]{2,1,0:T(8,128)}) custom-call(s32[1]{0:T(128)} %bitcast.core, bf16[27,128,128]{2,1,0:T(8,128)(2,1)S(1)} %collective-permute-done.6.other, f32[27,128,128]{2,1,0:T(8,128)} %get-tuple-element.37.first_in, ...), custom_call_target="tpu_custom_call", output_to_operand_aliasing={{0}: (2, {}), {1}: (3, {})} | custom-call | tf_op jit(solution)/shard_map/last_half/pallas_call | solution.py:368
  (5 shorter events, 0.1 us)
Async XLA Ops:
  2.0 24.1 %copy-start = (bf16[27,128,128]{2,1,0:T(8,128)(2,1)S(1)}, bf16[27,128,128]{2,1,0:T(8,128)(2,1)}, u32[]{:S(2)}) copy-start(bf16[27,128,128]{2,1,0:T(8,128)(2,1)} %w1.3) | copy-start | bytes 2654212
  2.1 24.1 %copy-start.1 = (bf16[1,1,2,512,128]{4,3,2,1,0:T(8,128)(2,1)S(1)}, bf16[1,1,2,512,128]{4,3,2,1,0:T(8,128)(2,1)}, u32[]{:S(2)}) copy-start(bf16[1,1,2,512,128]{4,3,2,1,0:T(8,128)(2,1)} %param.9) | copy-start | bytes 786436
  2.1 14.2 %collective-permute-start.2 = (bf16[2,336,128]{2,1,0:T(8,128)(2,1)S(1)}, bf16[2,336,128]{2,1,0:T(8,128)(2,1)S(1)}, u32[]{:S(2)}, u32[]{:S(2)}) collective-permute-start(bf16[2,336,128]{2,1,0:T(8,128)(2,1)S(1)} %get-tuple-element.26), channel_id=1, source_target_pairs={{0,1},{1,0},{2,3},{3,2},{4,5},{5,4},{6,7},{7,6},{8,9},{9,8},{10,11... | collective-permute-start | bytes 516104 | tf_op jit(solution)/shard_map/ppermute | solution.py:381
  4.3 12.0 %collective-permute-start = (bf16[2,320,128]{2,1,0:T(8,128)(2,1)S(1)}, bf16[2,320,128]{2,1,0:T(8,128)(2,1)S(1)}, u32[]{:S(2)}, u32[]{:S(2)}) collective-permute-start(bf16[2,320,128]{2,1,0:T(8,128)(2,1)S(1)} %get-tuple-element.24), channel_id=1, source_target_pairs={{0,2},{2,0},{4,6},{6,4},{8,10},{10,8},{12,14},{14,12},{16,18},{18,... | collective-permute-start | bytes 491528 | tf_op jit(solution)/shard_map/ppermute | solution.py:392
  5.5 10.8 %collective-permute-start.1 = (bf16[2,320,128]{2,1,0:T(8,128)(2,1)S(1)}, bf16[2,320,128]{2,1,0:T(8,128)(2,1)S(1)}, u32[]{:S(2)}, u32[]{:S(2)}) collective-permute-start(bf16[2,320,128]{2,1,0:T(8,128)(2,1)S(1)} %get-tuple-element.25), channel_id=1, source_target_pairs={{2,4},{4,2},{6,8},{8,6},{10,12},{12,10},{14,16},{16,14},{18,20},{2... | collective-permute-start | bytes 491528 | tf_op jit(solution)/shard_map/ppermute | solution.py:393
  9.6 5.4 %collective-permute-start.3 = (bf16[2,80,128]{2,1,0:T(8,128)(2,1)S(1)}, bf16[2,80,128]{2,1,0:T(8,128)(2,1)S(1)}, u32[]{:S(2)}, u32[]{:S(2)}) collective-permute-start(bf16[2,80,128]{2,1,0:T(8,128)(2,1)S(1)} %get-tuple-element.27), channel_id=1, source_target_pairs={{0,3},{1,2},{2,1},{3,0},{4,7},{5,6},{6,5},{7,4},{8,11},{9,10},{10,... | collective-permute-start | bytes 122888 | tf_op jit(solution)/shard_map/ppermute | solution.py:395
  9.7 6.5 %collective-permute-start.4 = (bf16[2,80,128]{2,1,0:T(8,128)(2,1)S(1)}, bf16[2,80,128]{2,1,0:T(8,128)(2,1)S(1)}, u32[]{:S(2)}, u32[]{:S(2)}) collective-permute-start(bf16[2,80,128]{2,1,0:T(8,128)(2,1)S(1)} %get-tuple-element.28), channel_id=1, source_target_pairs={{2,5},{3,4},{4,3},{5,2},{6,9},{7,8},{8,7},{9,6},{10,13},{11,12},{1... | collective-permute-start | bytes 122888 | tf_op jit(solution)/shard_map/ppermute | solution.py:396
  26.0 2.5 %collective-permute-start.5 = (bf16[27,128,128]{2,1,0:T(8,128)(2,1)S(1)}, bf16[27,128,128]{2,1,0:T(8,128)(2,1)S(1)}, u32[]{:S(2)}, u32[]{:S(2)}) collective-permute-start(bf16[27,128,128]{2,1,0:T(8,128)(2,1)S(1)} %get-tuple-element.31), channel_id=1, source_target_pairs={{0,2},{2,0},{1,3},{3,1},{4,6},{6,4},{5,7},{7,5},{8,10},{10,8},{9,1... | collective-permute-start | bytes 2654216 | tf_op jit(solution)/shard_map/ppermute | solution.py:381
  92.2 8.4 %collective-permute-start.6 = (bf16[27,128,128]{2,1,0:T(8,128)(2,1)S(1)}, bf16[27,128,128]{2,1,0:T(8,128)(2,1)S(1)}, u32[]{:S(2)}, u32[]{:S(2)}) collective-permute-start(bf16[27,128,128]{2,1,0:T(8,128)(2,1)S(1)} %bitcast.11), channel_id=1, source_target_pairs={{0,2},{2,0},{1,3},{3,1},{4,6},{6,4},{5,7},{7,5},{8,10},{10,8},{9,1... | collective-permute-start | bytes 2654216 | tf_op jit(solution)/shard_map/ppermute | solution.py:381

commit v5 on v4

--- a/solution.py
+++ b/solution.py
@@ -20,7 +20,11 @@
 VOX = E * FACE
 BLK = 2
 ROWS = BLK * VOX
-RIM = 4 * FACE + 4 * E
+INNER = [(1, E - 2, 1, E - 2)]
+OWN = [(0, 1, 0, E), (E - 1, 1, 0, E), (1, E - 2, 0, 1), (1, E - 2, E - 1, 1)]
+RIM = [(-1, 1, -1, E + 2), (E, 1, -1, E + 2), (0, E, -1, 1), (0, E, E, 1)]
+ALL = [(0, E, 0, E)]
+EACH = range(BLK)
 BF = jnp.bfloat16
 F32 = jnp.float32
 
@@ -55,12 +59,13 @@
     for b in range(BLK):
         row = occ_ref[b : b + 1, :].astype(F32)
         mask = jnp.broadcast_to(row, (CH, VOX)).T
-        mask_ref[b] = mask
+        mask_ref[b] = mask.reshape(E, FACE, CH)
         values = []
         for i, ref in enumerate((f_ref, g_ref)):
             masked = ref[b].astype(F32) * mask
+            masked = masked.reshape(E, FACE, CH)
             xg_ref[i, b] = masked.astype(BF)
-            values.append(masked.reshape(E, FACE, CH))
+            values.append(masked)
         mask = mask.reshape(E, FACE, CH)
         low = stack_rows([v[:, : 2 * E] for v in values] + [mask[:, :E]])
         high = stack_rows([v[:, FACE - 2 * E :] for v in values] + [mask[:, FACE - E :]])
@@ -145,23 +150,30 @@
                 tile[b, to_t, to_x] = value
 
 
-def pieces(tile, b, w, dt, dx):
-    cut = lambda t, nt, x, nx: tile[
-        b, w + t + dt : w + t + dt + nt, E * (w + x + dx) : E * (w + x + dx + nx)
-    ].reshape(nt * nx * E, CH)
-    rim = [(-1, 1, -1, E + 2), (E, 1, -1, E + 2), (0, E, -1, 1), (0, E, E, 1)]
-    return cut(0, E, 0, E), lambda: [cut(*part) for part in rim]
-
-
-def columns(tile, w, sign, cols, blocks, rim):
+def size(part):
+    return part[1] * part[3] * E
+
+
+def span(part, w, dt=0, dx=0):
+    t, nt, x, nx = part
+    return (
+        slice(w + t + dt, w + t + dt + nt),
+        slice(E * (w + x + dx), E * (w + x + dx + nx)),
+    )
+
+
+def cut(tile, w, groups, dt=0, dx=0):
+    return [
+        tile[(b, *span(part, w, dt, dx))].reshape(size(part), CH)
+        for b, parts in groups
+        for part in parts
+    ]
+
+
+def columns(tile, w, sign, cols, groups):
     for k, (dt, dx) in enumerate(WINDOWS):
-        lane = slice(k * CH, (k + 1) * CH)
-        for i, b in enumerate(blocks):
-            core, ring = pieces(tile, b, w, sign * dt, sign * dx)
-            cols[i * VOX : (i + 1) * VOX, lane] = core.astype(BF)
-            if rim:
-                at = ROWS + i * RIM
-                cols[at : at + RIM, lane] = jnp.concatenate(ring(), axis=0).astype(BF)
+        rows = jnp.concatenate(cut(tile, w, groups, sign * dt, sign * dx), axis=0)
+        cols[:, k * CH : (k + 1) * CH] = rows.astype(BF)
 
 
 def shift(value, step):
@@ -178,28 +190,69 @@
     return lanes(parts, 0) + shift(lanes(parts, 1), sign) + shift(lanes(parts, -1), -sign)
 
 
-def transposed(cols, w_ref, wide):
+def transposed(cols, wide):
+    parts = lax.dot_general(
+        cols[...], wide[...], (((1,), (1,)), ((), ())), preferred_element_type=F32
+    )
+    return gather_y(parts, -1)
+
+
+def arrange(w_ref, tall, wide):
     for k in range(27):
         w, d = divmod(k, 3)
-        wide[d * CH : (d + 1) * CH, w * CH : (w + 1) * CH] = w_ref[k]
-    parts = lax.dot_general(
-        cols[...], wide[...], (((1,), (1,)), ((), ())), preferred_element_type=F32
-    )
-    return gather_y(parts, -1)
+        if tall is not None:
+            tall[w * CH : (w + 1) * CH, d * CH : (d + 1) * CH] = w_ref[k]
+        if wide is not None:
+            wide[d * CH : (d + 1) * CH, w * CH : (w + 1) * CH] = w_ref[k]
 
 
 def outer(left, right):
     return lax.dot_general(left, right, (((0,), (0,)), ((), ())), preferred_element_type=F32)
 
 
-def local_kernel(
-    core, xg, mask_ref, table_in, w1_in, w2_in, h0, h1, h2, h3, h4,
-    gp_ref, keep_ref, send_ref,
-    xtile, gtile, mtile, xcol, gcol, wide, tall, table, w1, w2, sems,
+def local_math(xcol, gcol, mask, tall, wide, own):
+    pre = gather_y(jnp.dot(xcol[...], tall[...], preferred_element_type=F32), 1)
+    sig = jax.nn.sigmoid(pre)
+    hidden = (pre[:own] * sig[:own] * mask[:own]).astype(BF).astype(F32)
+    shifted = jnp.concatenate([shift(hidden, -1), hidden, shift(hidden, 1)], axis=1).astype(BF)
+    second = outer(shifted, gcol[:own])
+    grad_hidden = transposed(gcol, wide)
+    grad_pre = (grad_hidden * sig * (1.0 + pre * (1.0 - sig)) * mask).astype(BF).astype(F32)
+    mine = grad_pre[:own]
+    shifted = jnp.concatenate([shift(mine, 1), mine, shift(mine, -1)], axis=1).astype(BF)
+    first = outer(xcol[:own], shifted)
+    return grad_pre, first, second
+
+
+def inner_kernel(
+    xg, mask_ref, w1_in, w2_in, gp_ref, first_ref, second_ref, tall, wide1, wide2,
+    xtile, gtile, xcol, gcol, w1, w2, sems,
 ):
-    copies = load(sems, [(table_in, table), (w1_in, w1), (w2_in, w2)])
-    owns = [[xg[i, b].astype(F32).reshape(E, FACE, CH) for b in range(BLK)] for i in range(2)]
-    owns.append([mask_ref[b].reshape(E, FACE, CH) for b in range(BLK)])
+    copies = load(sems, [(w1_in, w1), (w2_in, w2)])
+    groups = [(b, INNER) for b in EACH]
+    xtile[...] = xg[0].astype(F32)
+    gtile[...] = xg[1].astype(F32)
+    columns(xtile, 0, 1, xcol, groups)
+    columns(gtile, 0, -1, gcol, groups)
+    mask = jnp.concatenate(cut(mask_ref, 0, groups), axis=0)
+    for copy in copies:
+        copy.wait()
+    arrange(w1, tall, wide1)
+    arrange(w2, None, wide2)
+    rows = BLK * size(INNER[0])
+    grad_pre, first, second = local_math(xcol, gcol, mask, tall, wide2, rows)
+    first_ref[...] = first
+    second_ref[...] = second
+    gp_ref[...] = grad_pre.reshape(gp_ref.shape)
+
+
+def outer_kernel(
+    core, xg, mask_ref, table_in, tall, wide2, inner, first_in, second_in, h0, h1, h2, h3, h4,
+    gp_ref, keep_ref, send_ref, xtile, gtile, mtile, xcol, gcol, table, sems,
+):
+    copies = load(sems, [(table_in, table)])
+    owns = [[xg[i, b].astype(F32) for b in EACH] for i in range(2)]
+    owns.append([mask_ref[b] for b in EACH])
     targets = [
         (xtile, 2, 0, 0),
         (gtile, 2, 2 * FACE, 4 * E),
@@ -207,53 +260,34 @@
     ]
     even = core[0] == 0
     build(targets, owns, table, copies[0].wait, even, (h0, h1, h2, h3, h4))
-    columns(xtile, 2, 1, xcol, range(BLK), True)
-    columns(gtile, 2, -1, gcol, range(BLK), True)
-    parts = [pieces(mtile, b, 1, 0, 0) for b in range(BLK)]
-    mask = jnp.concatenate([p[0] for p in parts] + parts[0][1]() + parts[1][1](), axis=0)
-    copies[1].wait()
+    groups = [(b, OWN) for b in EACH] + [(b, RIM) for b in EACH]
+    columns(xtile, 2, 1, xcol, groups)
+    columns(gtile, 2, -1, gcol, groups)
+    mask = jnp.concatenate(cut(mtile, 1, groups), axis=0)
+    rows = BLK * sum(size(part) for part in OWN)
+    grad_pre, first, second = local_math(xcol, gcol, mask, tall, wide2, rows)
+    at = 0
+    for b, parts in groups:
+        for part in parts:
+            rows = grad_pre[at : at + size(part)].reshape(part[1], part[3] * E, CH)
+            gp_ref[(b, *span(part, 1))] = rows
+            at += size(part)
+    for b in EACH:
+        gp_ref[(b, *span(INNER[0], 1))] = inner[b]
     for k in range(27):
         w, d = divmod(k, 3)
-        tall[w * CH : (w + 1) * CH, d * CH : (d + 1) * CH] = w1[k]
-    parts = jnp.dot(xcol[...], tall[...], preferred_element_type=F32)
-    pre = gather_y(parts, 1)
-    sig = jax.nn.sigmoid(pre)
-    hidden = (pre[:ROWS] * sig[:ROWS] * mask[:ROWS]).astype(BF).astype(F32)
-    shifted = jnp.concatenate([shift(hidden, -1), hidden, shift(hidden, 1)], axis=1).astype(BF)
-    second = outer(shifted, gcol[:ROWS])
-    copies[2].wait()
-    grad_hidden = transposed(gcol, w2, wide)
-    grad_pre = (grad_hidden * sig * (1.0 + pre * (1.0 - sig)) * mask).astype(BF).astype(F32)
-    for b in range(BLK):
-        at = ROWS + b * RIM
-        side = (E + 2) * E
-        gp_ref[b, 1 : E + 1, E : E + FACE] = grad_pre[b * VOX : (b + 1) * VOX].reshape(E, FACE, CH)
-        gp_ref[b, 0] = grad_pre[at : at + side]
-        gp_ref[b, E + 1] = grad_pre[at + side : at + 2 * side]
-        at += 2 * side
-        gp_ref[b, 1 : E + 1, 0:E] = grad_pre[at : at + FACE].reshape(E, E, CH)
-        gp_ref[b, 1 : E + 1, E + FACE :] = grad_pre[at + FACE : at + 2 * FACE].reshape(E, E, CH)
-    grad_pre = grad_pre[:ROWS]
-    shifted = jnp.concatenate(
-        [shift(grad_pre, 1), grad_pre, shift(grad_pre, -1)], axis=1
-    ).astype(BF)
-    first = outer(xcol[:ROWS], shifted)
-    for k in range(27):
-        w, d = divmod(k, 3)
-        a = second[d * CH : (d + 1) * CH, w * CH : (w + 1) * CH]
-        b = first[w * CH : (w + 1) * CH, d * CH : (d + 1) * CH]
+        ws, ds = slice(w * CH, (w + 1) * CH), slice(d * CH, (d + 1) * CH)
+        a = second[ds, ws] + second_in[ds, ws]
+        b = first[ws, ds] + first_in[ws, ds]
         keep_ref[k] = jnp.where(even, a, b)
         send_ref[k] = jnp.where(even, b, a).astype(BF)
 
 
-def input_block(block, gp, mask_ref, cot, w1, dcol, wide):
-    columns(gp, 1, -1, dcol, [block], False)
-    total = transposed(dcol, w1, wide) * mask_ref[block]
-    return (cot[block].astype(F32) + total).astype(BF)
-
-
-def early_kernel(gp, mask_ref, cot, w1, out, dcol, wide):
-    out[...] = input_block(0, gp, mask_ref, cot, w1, dcol, wide)
+def grad_kernel(gp, mask_ref, cot, wide, out, dcol):
+    columns(gp, 1, -1, dcol, [(b, ALL) for b in EACH])
+    total = transposed(dcol, wide) * mask_ref[...].reshape(ROWS, CH)
+    total = cot[...].astype(F32).reshape(ROWS, CH) + total
+    out[...] = total.astype(BF).reshape(BLK, VOX, CH)
 
 
 def to_half(core, mine, value, first, second, sem, act):
@@ -263,12 +297,9 @@
         pl.when(flag)(copy.start if act == "start" else copy.wait)
 
 
-def late_kernel(core, gp, mask_ref, cot, w1, early, mine, out, first, second, *scratch):
-    dcol, wide, value, sem = scratch
+def mine_kernel(core, mine, first, second, value, sem):
     value[...] = mine[...].astype(F32)
     to_half(core, True, value, first, second, sem, "start")
-    out[0] = early[...]
-    out[1] = input_block(1, gp, mask_ref, cot, w1, dcol, wide)
     to_half(core, True, value, first, second, sem, "wait")
 
 
@@ -287,8 +318,8 @@
     return pl.pallas_call(
         pack_kernel,
         out_shape=[
-            jax.ShapeDtypeStruct((2, BLK, VOX, CH), BF),
-            jax.ShapeDtypeStruct((BLK, VOX, CH), F32),
+            jax.ShapeDtypeStruct((2, BLK, E, FACE, CH), BF),
+            jax.ShapeDtypeStruct((BLK, E, FACE, CH), F32),
             *[jax.ShapeDtypeStruct((BLK, rows, CH), BF) for rows in shapes],
         ],
         in_specs=[SM] * 2 + [HB] * 5,
@@ -306,61 +337,86 @@
     )(half, core, *map(in_place, (f, g, occ, sends, when)))
 
 
-def local_pass(table, core, xg, mask, w1, w2, halos):
+def inner_pass(xg, mask, w1, w2):
+    rows = BLK * size(INNER[0])
+    tall, wide = (9 * CH, 3 * CH), (3 * CH, 9 * CH)
     return pl.pallas_call(
-        local_kernel,
+        inner_kernel,
+        out_shape=[
+            jax.ShapeDtypeStruct((BLK, E - 2, (E - 2) * E, CH), F32),
+            jax.ShapeDtypeStruct(tall, F32),
+            jax.ShapeDtypeStruct(wide, F32),
+            jax.ShapeDtypeStruct(tall, BF),
+            jax.ShapeDtypeStruct(wide, BF),
+            jax.ShapeDtypeStruct(wide, BF),
+        ],
+        in_specs=[VM] * 2 + [HB] * 2,
+        out_specs=[VM] * 6,
+        scratch_shapes=[
+            pltpu.VMEM((BLK, E, FACE, CH), F32),
+            pltpu.VMEM((BLK, E, FACE, CH), F32),
+            pltpu.VMEM((rows, 9 * CH), BF),
+            pltpu.VMEM((rows, 9 * CH), BF),
+            pltpu.VMEM((27, CH, CH), BF),
+            pltpu.VMEM((27, CH, CH), BF),
+            DMA((2,)),
+        ],
+        compiler_params=PARAMS,
+        name="inner_pass",
+    )(xg, mask, *map(in_place, (w1, w2)))
+
+
+def outer_pass(core, xg, mask, table, tall, wide2, inner, first, second, halos):
+    rows = BLK * sum(size(part) for part in OWN + RIM)
+    return pl.pallas_call(
+        outer_kernel,
         out_shape=[
             jax.ShapeDtypeStruct((BLK, E + 2, (E + 2) * E, CH), F32),
             jax.ShapeDtypeStruct((27, CH, CH), F32),
             jax.ShapeDtypeStruct((27, CH, CH), BF),
         ],
-        in_specs=[SM] + [VM] * 2 + [HB] * 3 + [VM] * 5,
+        in_specs=[SM] + [VM] * 2 + [HB] + [VM] * 10,
         out_specs=[VM] * 3,
         scratch_shapes=[
             pltpu.VMEM((BLK, E + 4, (E + 4) * E, CH), F32),
             pltpu.VMEM((BLK, E + 4, (E + 4) * E, CH), F32),
             pltpu.VMEM((BLK, E + 2, (E + 2) * E, CH), F32),
-            pltpu.VMEM((ROWS + BLK * RIM, 9 * CH), BF),
-            pltpu.VMEM((ROWS + BLK * RIM, 9 * CH), BF),
-            pltpu.VMEM((3 * CH, 9 * CH), BF),
-            pltpu.VMEM((9 * CH, 3 * CH), BF),
+            pltpu.VMEM((rows, 9 * CH), BF),
+            pltpu.VMEM((rows, 9 * CH), BF),
             pltpu.SMEM((BLK, 27), I32),
-            pltpu.VMEM((27, CH, CH), BF),
-            pltpu.VMEM((27, CH, CH), BF),
-            DMA((3,)),
+            DMA((1,)),
         ],
         compiler_params=PARAMS,
-        name="local_pass",
-    )(core, xg, mask, *map(in_place, (table, w1, w2)), *halos)
-
-
-INPUT_SCRATCH = [pltpu.VMEM((VOX, 9 * CH), BF), pltpu.VMEM((3 * CH, 9 * CH), BF)]
-HALF_SCRATCH = [pltpu.VMEM((27, CH, CH), F32), DMA(())]
-
-
-def early_grad(gp, mask, cot, w1):
+        name="outer_pass",
+    )(core, xg, mask, in_place(table), tall, wide2, inner, first, second, *halos)
+
+
+def input_grad(gp, mask, cot, wide):
     return pl.pallas_call(
-        early_kernel,
-        out_shape=jax.ShapeDtypeStruct((VOX, CH), BF),
+        grad_kernel,
+        out_shape=jax.ShapeDtypeStruct((BLK, VOX, CH), BF),
         in_specs=[VM] * 4,
         out_specs=VM,
-        scratch_shapes=INPUT_SCRATCH,
+        scratch_shapes=[pltpu.VMEM((ROWS, 9 * CH), BF)],
         compiler_params=PARAMS,
-        name="early_grad",
-    )(gp, mask, cot, w1)
-
-
-def late_grad(core, gp, mask, cot, w1, early, mine):
+        name="input_grad",
+    )(gp, mask, cot, wide)
+
+
+HALF_SCRATCH = [pltpu.VMEM((27, CH, CH), F32), DMA(())]
+
+
+def mine_half(core, mine):
     weights = jax.ShapeDtypeStruct((27, CH, CH), F32)
     return pl.pallas_call(
-        late_kernel,
-        out_shape=[jax.ShapeDtypeStruct((BLK, VOX, CH), BF), weights, weights],
-        in_specs=[SM] + [VM] * 6,
-        out_specs=[VM, HB, HB],
-        scratch_shapes=INPUT_SCRATCH + HALF_SCRATCH,
+        mine_kernel,
+        out_shape=[weights, weights],
+        in_specs=[SM, VM],
+        out_specs=[HB, HB],
+        scratch_shapes=HALF_SCRATCH,
         compiler_params=PARAMS,
-        name="late_grad",
-    )(core, gp, mask, cot, w1, early, mine)
+        name="mine_half",
+    )(core, mine)
 
 
 def last_half(core, other, first, second):
@@ -415,7 +471,6 @@
     total = (jnp.sum(parts, axis=0) * scale).astype(BF)
     total = spread(total, ("z",)).reshape(rows, CH)
     mine = spread(total, PLANE).reshape(27, CH, CH)
-    mine, early = lax.optimization_barrier((mine, early))
     return mine, swap(mine, "c"), early
 
 
@@ -428,12 +483,15 @@
     when = send_time.reshape(1, 2 * BLK)
     xg, mask, *messages = pack(f, g, occupancy.reshape(BLK, VOX), sends, when, half, core)
     halos = exchange(messages)
-    gp, keep, send = local_pass(table, core, xg, mask, w_first, w_second, halos)
-    early = early_grad(gp, mask, g, w_first)
+    inner, first, second, tall, wide1, wide2 = inner_pass(xg, mask, w_first, w_second)
+    gp, keep, send = outer_pass(
+        core, xg, mask, table, tall, wide2, inner, first, second, halos
+    )
+    out = input_grad(gp, mask, g, wide1)
     devices = math.prod(lax.axis_size(axis) for axis in (*SPACE, TIME))
     scale = 1.0 / math.sqrt(devices * ROWS)
-    mine, other, early = reduce_all(keep, send, scale, early)
-    out, first, second = late_grad(core, gp, mask, g, w_first, early, mine)
+    mine, other, out = reduce_all(keep, send, scale, out)
+    first, second = mine_half(core, mine)
     first, second = last_half(core, other, first, second)
     return out.reshape(features.shape), first, second
 

time: 102 us -> 99.4 us (0.975)
  waiting for transfers between devices: 4.05 us -> 0.81 us
  Pallas kernels: 16.4 us -> 18.1 us
  blocking collectives: 63 us -> 61.4 us
    pallas_call x4 -> x5, Pallas kernels: 15 us -> 16.7 us  [the longest x1 5.93 us: outer_pass(): pl.pallas_call(outer_kernel, out_shape=[jax.ShapeDtypeStruct((BLK, E + 2,...]
    ppermute x1, waiting for transfers between devices: 1.33 us -> 0.01 us  [exchange(): lax.ppermute(even_diag, (*SPACE, TIME), cross(both(0)))]
    ppermute x1, waiting for transfers between devices: 1.24 us -> 0.01 us  [exchange(): lax.ppermute(odd_diag, (*SPACE, TIME), cross(both(1)))]
    all_to_all x1, blocking collectives: 17.1 us -> 15.9 us  [reduce_all(): parts = lax.all_to_all(total.reshape(depth, rows // depth, CH), 'z', 0, 0)]
  transfers between devices with their start and end apart: 7 -> 7, of which waited for: 3 -> 2; matrix products, arithmetic and copies ran while one was open for 0% -> 0% of each run, Pallas kernels for 4% -> 9%
where the time goes in v5:
time: 99.4 us; the launch traced here: 99.1 us
  blocking collectives  61.4 us (62%)
  Pallas kernels  18.1 us (18%)
  starting transfers between devices  17.3 us (17%)
    all_to_all x2, blocking collectives, spread(): return lax.all_to_all(copies, axes, 0, 0)  24.3 us
    all_to_all x1, blocking collectives, reduce_all(): parts = lax.all_to_all(total.reshape(plane, rows, CH), PLANE, 0, 0)  21.2 us
    all_to_all x1, blocking collectives, reduce_all(): parts = lax.all_to_all(total.reshape(depth, rows // depth, CH), 'z', 0, 0)  15.9 us
    ppermute x3, starting transfers between devices, swap(): return lax.ppermute(value, axis, [(0, 1), (1, 0)])  7.93 us
    pallas_call x1, Pallas kernels, outer_pass(): pl.pallas_call(outer_kernel, out_shape=[jax.ShapeDtypeStruct((BLK, E + 2,...  5.93 us
    pallas_call x1, Pallas kernels, inner_pass(): pl.pallas_call(inner_kernel, out_shape=[jax.ShapeDtypeStruct((BLK, E - 2,...  5.74 us
    ppermute x1, starting transfers between devices, exchange(): lax.ppermute(odd_side, SPACE, both(1))  4.17 us
    ppermute x1, starting transfers between devices, exchange(): lax.ppermute(odd_diag, (*SPACE, TIME), cross(both(1)))  3.95 us
  transfers between devices with their start and end apart: 7, of which 2 were waited for; matrix products, arithmetic and copies ran while one was open for 0% of the time, Pallas kernels for 9%

profile of v5, /device:TPU:1, one launch (start us, length us, event | category | flops | bytes accessed | tf_op | source)
XLA Modules:
  0.0 99.1 jit_solution(4578512122278660814)
XLA Ops:
  0.6 1.4 %pack.1 = (bf16[2,2,8,64,128]{4,3,2,1,0:T(8,128)(2,1)S(1)}, f32[2,8,64,128]{3,2,1,0:T(8,128)S(1)}, bf16[2,320,128]{2,1,0:T(8,128)(2,1)S(1)}, bf16[2,320,128]{2,1...) custom-call(s32[1]{0:T(128)} %bitcast.1.half, ...), custom_call_target="tpu_custom_call" | custom-call | tf_op jit(solution)/shard_map/pack/pallas_call | solution.py:318
  2.0 2.2 %collective-permute-start.2 = (bf16[2,336,128]{2,1,0:T(8,128)(2,1)S(1)}, bf16[2,336,128]{2,1,0:T(8,128)(2,1)S(1)}, u32[]{:S(2)}, u32[]{:S(2)}) collective-permute-start(bf16[2,336,128]{2,1,0:T(8,128)(2,1)S(1)} %get-tuple-element.34), channel_id=1, source_target_pairs={{0,1},{1,0},{2,3},{3,2},{4,5},{5,4},{6,7},{7,6},{8,9},{9,8},{10,11... | collective-permute-start | bytes 516104 | tf_op jit(solution)/shard_map/ppermute | solution.py:437
  4.3 1.2 %collective-permute-start = (bf16[2,320,128]{2,1,0:T(8,128)(2,1)S(1)}, bf16[2,320,128]{2,1,0:T(8,128)(2,1)S(1)}, u32[]{:S(2)}, u32[]{:S(2)}) collective-permute-start(bf16[2,320,128]{2,1,0:T(8,128)(2,1)S(1)} %get-tuple-element.32), channel_id=1, source_target_pairs={{0,2},{2,0},{4,6},{6,4},{8,10},{10,8},{12,14},{14,12},{16,18},{18,... | collective-permute-start | bytes 491528 | tf_op jit(solution)/shard_map/ppermute | solution.py:448
  5.4 4.2 %collective-permute-start.1 = (bf16[2,320,128]{2,1,0:T(8,128)(2,1)S(1)}, bf16[2,320,128]{2,1,0:T(8,128)(2,1)S(1)}, u32[]{:S(2)}, u32[]{:S(2)}) collective-permute-start(bf16[2,320,128]{2,1,0:T(8,128)(2,1)S(1)} %get-tuple-element.33), channel_id=1, source_target_pairs={{2,4},{4,2},{6,8},{8,6},{10,12},{12,10},{14,16},{16,14},{18,20},{2... | collective-permute-start | bytes 491528 | tf_op jit(solution)/shard_map/ppermute | solution.py:449
  9.6 0.1 collective-permute-start.3
  9.7 3.9 %collective-permute-start.4 = (bf16[2,80,128]{2,1,0:T(8,128)(2,1)S(1)}, bf16[2,80,128]{2,1,0:T(8,128)(2,1)S(1)}, u32[]{:S(2)}, u32[]{:S(2)}) collective-permute-start(bf16[2,80,128]{2,1,0:T(8,128)(2,1)S(1)} %get-tuple-element.36), channel_id=1, source_target_pairs={{2,5},{3,4},{4,3},{5,2},{6,9},{7,8},{8,7},{9,6},{10,13},{11,12},{1... | collective-permute-start | bytes 122888 | tf_op jit(solution)/shard_map/ppermute | solution.py:452
  13.7 5.7 %inner_pass.1 = (f32[2,6,48,128]{3,2,1,0:T(8,128)S(1)}, f32[1152,384]{1,0:T(8,128)S(1)}, f32[384,1152]{1,0:T(8,128)S(1)}, bf16[1152,384]{1,0:T(8,128)(2,1)S(1)},...) custom-call(bf16[2,2,8,64,128]{4,3,2,1,0:T(8,128)(2,1)S(1)} %get-tuple-element.25.xg, ...), custom_call_target="tpu_custom_call" | custom-call | tf_op jit(solution)/shard_map/inner_pass/pallas_call | solution.py:343
  19.4 0.0 collective-permute-done.3.h3
  19.4 0.0 collective-permute-done.4.h4
  19.4 0.0 collective-permute-done.h0
  19.5 0.0 collective-permute-done.1.h1
  19.5 0.0 collective-permute-done.2.h2
  19.5 0.0 copy-start
  19.5 5.9 %outer_pass.1 = (f32[2,10,80,128]{3,2,1,0:T(8,128)S(1)}, f32[27,128,128]{2,1,0:T(8,128)S(1)}, bf16[27,128,128]{2,1,0:T(8,128)(2,1)S(1)}) custom-call(s32[1]{0:T(128)} %bitcast.core, bf16[2,2,8,64,128]{4,3,2,1,0:T(8,128)(2,1)S(1)} %get-tuple-element.25.xg, f32[2,8,64,128]{3,2,1,0:T(8,128)S(1)} %get-tuple-element.26.mask_ref, s32[2,27]{1,0:T(2,128)} %bitcast.20, ...), custom_call_target="tpu_custom_call" | custom-call | tf_op jit(solution)/shard_map/outer_pass/pallas_call | solution.py:371
  25.4 0.3 collective-permute-start.5
  25.7 0.0 copy-done
  25.7 2.3 %input_grad.1 = bf16[2,512,128]{2,1,0:T(8,128)(2,1)} custom-call(f32[2,10,80,128]{3,2,1,0:T(8,128)S(1)} %get-tuple-element.39.gp, f32[2,8,64,128]{3,2,1,0:T(8,128)S(1)} %get-tuple-element.26.mask_ref, bf16[2,512,128]{2,1,0:T(8,128)(2,1)S(1)} %bitcast.14, bf16[384,1152]{1,0:T(8,128)(2,1)S(1)} %get-tuple-element.40.wide), custom_call_target="tpu_custom_call" | custom-call | tf_op jit(solution)/shard_map/input_grad/pallas_call | solution.py:395
  28.0 0.1 collective-permute-done.5
  28.1 0.2 add_convert_fusion
  28.4 21.2 %all_to_all.20 = bf16[16,216,128]{2,1,0:T(8,128)(2,1)S(1)} all-to-all(bf16[16,216,128]{2,1,0:T(8,128)(2,1)S(1)} %bitcast.15), channel_id=1, replica_groups=mesh['z'=8,'x'=4,'yh'=2,'c'=2,'yl'=2] {'x','yh','yl'}, dimensions={0} | all-to-all | bytes 1769472 | tf_op jit(solution)/shard_map/all_to_all | solution.py:467
  49.5 0.1 convert_reduce_fusion
  49.7 15.9 %all_to_all.21 = f32[8,27,128]{2,1,0:T(8,128)S(1)} all-to-all(f32[8,27,128]{2,1,0:T(8,128)S(1)} %reshape.57), channel_id=1, replica_groups=mesh['z'=8,'x'=4,'yh'=2,'c'=2,'yl'=2] {'z'}, dimensions={0} | all-to-all | bytes 221184 | tf_op jit(solution)/shard_map/all_to_all | solution.py:470
  65.7 9.6 %all_to_all.22 = bf16[8,27,128]{2,1,0:T(8,128)(2,1)S(1)} all-to-all(bf16[8,27,128]{2,1,0:T(8,128)(2,1)S(1)} %broadcast_in_dim.6), channel_id=1, replica_groups=mesh['z'=8,'x'=4,'yh'=2,'c'=2,'yl'=2] {'z'}, dimensions={0} | all-to-all | bytes 110592 | tf_op jit(solution)/shard_map/all_to_all | solution.py:459
  75.3 0.1 broadcast_in_dim.15
  75.4 14.7 %all_to_all.23 = bf16[16,216,128]{2,1,0:T(8,128)(2,1)S(1)} all-to-all(bf16[16,216,128]{2,1,0:T(8,128)(2,1)S(1)} %broadcast_in_dim.15), channel_id=1, replica_groups=mesh['z'=8,'x'=4,'yh'=2,'c'=2,'yl'=2] {'x','yh','yl'}, dimensions={0} | all-to-all | bytes 1769472 | tf_op jit(solution)/shard_map/all_to_all | solution.py:459
  90.1 5.5 %collective-permute-start.6 = (bf16[27,128,128]{2,1,0:T(8,128)(2,1)S(1)}, bf16[27,128,128]{2,1,0:T(8,128)(2,1)S(1)}, u32[]{:S(2)}, u32[]{:S(2)}) collective-permute-start(bf16[27,128,128]{2,1,0:T(8,128)(2,1)S(1)} %bitcast.11), channel_id=1, source_target_pairs={{0,2},{2,0},{1,3},{3,1},{4,6},{6,4},{5,7},{7,5},{8,10},{10,8},{9,1... | collective-permute-start | bytes 2654216 | tf_op jit(solution)/shard_map/ppermute | solution.py:437
  95.6 1.3 %mine_half.1 = (f32[27,128,128]{2,1,0:T(8,128)}, f32[27,128,128]{2,1,0:T(8,128)}) custom-call(s32[1]{0:T(128)} %bitcast.core, bf16[27,128,128]{2,1,0:T(8,128)(2,1)S(1)} %bitcast.12), custom_call_target="tpu_custom_call" | custom-call | tf_op jit(solution)/shard_map/mine_half/pallas_call | solution.py:411
  96.9 0.7 collective-permute-done.6.other
  97.6 1.3 %last_half.1 = (f32[27,128,128]{2,1,0:T(8,128)}, f32[27,128,128]{2,1,0:T(8,128)}) custom-call(s32[1]{0:T(128)} %bitcast.core, bf16[27,128,128]{2,1,0:T(8,128)(2,1)S(1)} %collective-permute-done.6.other, f32[27,128,128]{2,1,0:T(8,128)} %get-tuple-element.43.first_in, ...), custom_call_target="tpu_custom_call", output_to_operand_aliasing={{0}: (2, {}), {1}: (3, {})} | custom-call | tf_op jit(solution)/shard_map/last_half/pallas_call | solution.py:424
  (5 shorter events, 0.1 us)
Async XLA Ops:
  2.0 17.4 %collective-permute-start.2 = (bf16[2,336,128]{2,1,0:T(8,128)(2,1)S(1)}, bf16[2,336,128]{2,1,0:T(8,128)(2,1)S(1)}, u32[]{:S(2)}, u32[]{:S(2)}) collective-permute-start(bf16[2,336,128]{2,1,0:T(8,128)(2,1)S(1)} %get-tuple-element.34), channel_id=1, source_target_pairs={{0,1},{1,0},{2,3},{3,2},{4,5},{5,4},{6,7},{7,6},{8,9},{9,8},{10,11... | collective-permute-start | bytes 516104 | tf_op jit(solution)/shard_map/ppermute | solution.py:437
  4.3 15.2 %collective-permute-start = (bf16[2,320,128]{2,1,0:T(8,128)(2,1)S(1)}, bf16[2,320,128]{2,1,0:T(8,128)(2,1)S(1)}, u32[]{:S(2)}, u32[]{:S(2)}) collective-permute-start(bf16[2,320,128]{2,1,0:T(8,128)(2,1)S(1)} %get-tuple-element.32), channel_id=1, source_target_pairs={{0,2},{2,0},{4,6},{6,4},{8,10},{10,8},{12,14},{14,12},{16,18},{18,... | collective-permute-start | bytes 491528 | tf_op jit(solution)/shard_map/ppermute | solution.py:448
  5.4 14.0 %collective-permute-start.1 = (bf16[2,320,128]{2,1,0:T(8,128)(2,1)S(1)}, bf16[2,320,128]{2,1,0:T(8,128)(2,1)S(1)}, u32[]{:S(2)}, u32[]{:S(2)}) collective-permute-start(bf16[2,320,128]{2,1,0:T(8,128)(2,1)S(1)} %get-tuple-element.33), channel_id=1, source_target_pairs={{2,4},{4,2},{6,8},{8,6},{10,12},{12,10},{14,16},{16,14},{18,20},{2... | collective-permute-start | bytes 491528 | tf_op jit(solution)/shard_map/ppermute | solution.py:449
  9.6 9.8 %collective-permute-start.3 = (bf16[2,80,128]{2,1,0:T(8,128)(2,1)S(1)}, bf16[2,80,128]{2,1,0:T(8,128)(2,1)S(1)}, u32[]{:S(2)}, u32[]{:S(2)}) collective-permute-start(bf16[2,80,128]{2,1,0:T(8,128)(2,1)S(1)} %get-tuple-element.35), channel_id=1, source_target_pairs={{0,3},{1,2},{2,1},{3,0},{4,7},{5,6},{6,5},{7,4},{8,11},{9,10},{10,... | collective-permute-start | bytes 122888 | tf_op jit(solution)/shard_map/ppermute | solution.py:451
  9.7 9.7 %collective-permute-start.4 = (bf16[2,80,128]{2,1,0:T(8,128)(2,1)S(1)}, bf16[2,80,128]{2,1,0:T(8,128)(2,1)S(1)}, u32[]{:S(2)}, u32[]{:S(2)}) collective-permute-start(bf16[2,80,128]{2,1,0:T(8,128)(2,1)S(1)} %get-tuple-element.36), channel_id=1, source_target_pairs={{2,5},{3,4},{4,3},{5,2},{6,9},{7,8},{8,7},{9,6},{10,13},{11,12},{1... | collective-permute-start | bytes 122888 | tf_op jit(solution)/shard_map/ppermute | solution.py:452
  19.5 6.2 %copy-start = (bf16[1,1,2,512,128]{4,3,2,1,0:T(8,128)(2,1)S(1)}, bf16[1,1,2,512,128]{4,3,2,1,0:T(8,128)(2,1)}, u32[]{:S(2)}) copy-start(bf16[1,1,2,512,128]{4,3,2,1,0:T(8,128)(2,1)} %param.9) | copy-start | bytes 786436
  25.4 2.7 %collective-permute-start.5 = (bf16[27,128,128]{2,1,0:T(8,128)(2,1)S(1)}, bf16[27,128,128]{2,1,0:T(8,128)(2,1)S(1)}, u32[]{:S(2)}, u32[]{:S(2)}) collective-permute-start(bf16[27,128,128]{2,1,0:T(8,128)(2,1)S(1)} %get-tuple-element.38), channel_id=1, source_target_pairs={{0,2},{2,0},{1,3},{3,1},{4,6},{6,4},{5,7},{7,5},{8,10},{10,8},{9,1... | collective-permute-start | bytes 2654216 | tf_op jit(solution)/shard_map/ppermute | solution.py:437
  90.1 7.5 %collective-permute-start.6 = (bf16[27,128,128]{2,1,0:T(8,128)(2,1)S(1)}, bf16[27,128,128]{2,1,0:T(8,128)(2,1)S(1)}, u32[]{:S(2)}, u32[]{:S(2)}) collective-permute-start(bf16[27,128,128]{2,1,0:T(8,128)(2,1)S(1)} %bitcast.11), channel_id=1, source_target_pairs={{0,2},{2,0},{1,3},{3,1},{4,6},{6,4},{5,7},{7,5},{8,10},{10,8},{9,1... | collective-permute-start | bytes 2654216 | tf_op jit(solution)/shard_map/ppermute | solution.py:437

commit v6 on v5

--- a/solution.py
+++ b/solution.py
@@ -52,14 +52,18 @@
 def pack_kernel(half, core, f, g, occ, sends_in, when_in, xg_ref, mask_ref, *refs):
     even_ref, odd_ref, time_ref, even_diag, odd_diag, *scratch, sems = refs
     f_ref, g_ref, occ_ref, sends, when = scratch
-    for copy in load(sems, list(zip((f, g, occ, sends_in, when_in), scratch))):
-        copy.wait()
+    copies = load(sems, list(zip((f, g, occ, sends_in, when_in), scratch)))
     even = core[0] == 0
-    sides, times, corners = [], [], []
+    sides, times, corners, masks = [], [], [], []
+    copies[2].wait()
     for b in range(BLK):
         row = occ_ref[b : b + 1, :].astype(F32)
-        mask = jnp.broadcast_to(row, (CH, VOX)).T
-        mask_ref[b] = mask.reshape(E, FACE, CH)
+        masks.append(jnp.broadcast_to(row, (CH, VOX)).T)
+        mask_ref[b] = masks[b].reshape(E, FACE, CH)
+    for copy in copies[:2] + copies[3:]:
+        copy.wait()
+    for b in range(BLK):
+        mask = masks[b]
         values = []
         for i, ref in enumerate((f_ref, g_ref)):
             masked = ref[b].astype(F32) * mask
@@ -211,7 +215,9 @@
 
 
 def local_math(xcol, gcol, mask, tall, wide, own):
-    pre = gather_y(jnp.dot(xcol[...], tall[...], preferred_element_type=F32), 1)
+    product = lambda n: jnp.dot(xcol[...], tall[:, n], preferred_element_type=F32)
+    parts = [product(slice(0, 2 * CH)), product(slice(2 * CH, 3 * CH))]
+    pre = gather_y(jnp.concatenate(parts, axis=1), 1)
     sig = jax.nn.sigmoid(pre)
     hidden = (pre[:own] * sig[:own] * mask[:own]).astype(BF).astype(F32)
     shifted = jnp.concatenate([shift(hidden, -1), hidden, shift(hidden, 1)], axis=1).astype(BF)
@@ -290,23 +296,29 @@
     out[...] = total.astype(BF).reshape(BLK, VOX, CH)
 
 
-def to_half(core, mine, value, first, second, sem, act):
+def put_half(core, mine, source, first, second, value, sems):
     even = (core[0] == 0) if mine else (core[0] != 0)
-    for flag, target in ((even, second), (~even, first)):
-        copy = pltpu.make_async_copy(value, target, sem)
-        pl.when(flag)(copy.start if act == "start" else copy.wait)
-
-
-def mine_kernel(core, mine, first, second, value, sem):
-    value[...] = mine[...].astype(F32)
-    to_half(core, True, value, first, second, sem, "start")
-    to_half(core, True, value, first, second, sem, "wait")
-
-
-def last_kernel(core, other, first_in, second_in, first, second, value, sem):
-    value[...] = other[...].astype(F32)
-    to_half(core, False, value, first, second, sem, "start")
-    to_half(core, False, value, first, second, sem, "wait")
+    step = 27 // PIECES
+
+    def each(act):
+        for flag, target in ((even, second), (~even, first)):
+            for n in [act] if isinstance(act, int) else range(PIECES):
+                taps = pl.ds(n * step, step)
+                copy = pltpu.make_async_copy(value.at[taps], target.at[taps], sems.at[n])
+                pl.when(flag)(copy.start if isinstance(act, int) else copy.wait)
+
+    for n in range(PIECES):
+        value[n * step : (n + 1) * step] = source[n * step : (n + 1) * step].astype(F32)
+        each(n)
+    each("all")
+
+
+def mine_kernel(core, mine, first, second, value, sems):
+    put_half(core, True, mine, first, second, value, sems)
+
+
+def last_kernel(core, other, first_in, second_in, first, second, value, sems):
+    put_half(core, False, other, first, second, value, sems)
 
 
 def in_place(value):
@@ -403,7 +415,8 @@
     )(gp, mask, cot, wide)
 
 
-HALF_SCRATCH = [pltpu.VMEM((27, CH, CH), F32), DMA(())]
+PIECES = 3
+HALF_SCRATCH = [pltpu.VMEM((27, CH, CH), F32), DMA((PIECES,))]
 
 
 def mine_half(core, mine):

time: 99.4 us -> 99.4 us (level)
  no operation moved by 1% of the time
where the time goes in v6:
time: 99.4 us; the launch traced here: 99 us
  blocking collectives  61.4 us (62%)
  Pallas kernels  17.9 us (18%)
  starting transfers between devices  17.3 us (17%)
    all_to_all x2, blocking collectives, spread(): return lax.all_to_all(copies, axes, 0, 0)  24.3 us
    all_to_all x1, blocking collectives, reduce_all(): parts = lax.all_to_all(total.reshape(plane, rows, CH), PLANE, 0, 0)  21.2 us
    all_to_all x1, blocking collectives, reduce_all(): parts = lax.all_to_all(total.reshape(depth, rows // depth, CH), 'z', 0, 0)  15.9 us
    ppermute x3, starting transfers between devices, swap(): return lax.ppermute(value, axis, [(0, 1), (1, 0)])  7.93 us
    pallas_call x1, Pallas kernels, outer_pass(): pl.pallas_call(outer_kernel, out_shape=[jax.ShapeDtypeStruct((BLK, E + 2,...  5.92 us
    pallas_call x1, Pallas kernels, inner_pass(): pl.pallas_call(inner_kernel, out_shape=[jax.ShapeDtypeStruct((BLK, E - 2,...  5.74 us
    ppermute x1, starting transfers between devices, exchange(): lax.ppermute(odd_side, SPACE, both(1))  4.17 us
    ppermute x1, starting transfers between devices, exchange(): lax.ppermute(odd_diag, (*SPACE, TIME), cross(both(1)))  3.95 us
  transfers between devices with their start and end apart: 7, of which 2 were waited for; matrix products, arithmetic and copies ran while one was open for 0% of the time, Pallas kernels for 9%

profile of v6, /device:TPU:1, one launch (start us, length us, event | category | flops | bytes accessed | tf_op | source)
XLA Modules:
  0.0 99.0 jit_solution(13819672603857551049)
XLA Ops:
  0.6 1.4 %pack.1 = (bf16[2,2,8,64,128]{4,3,2,1,0:T(8,128)(2,1)S(1)}, f32[2,8,64,128]{3,2,1,0:T(8,128)S(1)}, bf16[2,320,128]{2,1,0:T(8,128)(2,1)S(1)}, bf16[2,320,128]{2,1...) custom-call(s32[1]{0:T(128)} %bitcast.1.half, ...), custom_call_target="tpu_custom_call" | custom-call | tf_op jit(solution)/shard_map/pack/pallas_call | solution.py:330
  2.0 2.2 %collective-permute-start.2 = (bf16[2,336,128]{2,1,0:T(8,128)(2,1)S(1)}, bf16[2,336,128]{2,1,0:T(8,128)(2,1)S(1)}, u32[]{:S(2)}, u32[]{:S(2)}) collective-permute-start(bf16[2,336,128]{2,1,0:T(8,128)(2,1)S(1)} %get-tuple-element.34), channel_id=1, source_target_pairs={{0,1},{1,0},{2,3},{3,2},{4,5},{5,4},{6,7},{7,6},{8,9},{9,8},{10,11... | collective-permute-start | bytes 516104 | tf_op jit(solution)/shard_map/ppermute | solution.py:450
  4.2 1.2 %collective-permute-start = (bf16[2,320,128]{2,1,0:T(8,128)(2,1)S(1)}, bf16[2,320,128]{2,1,0:T(8,128)(2,1)S(1)}, u32[]{:S(2)}, u32[]{:S(2)}) collective-permute-start(bf16[2,320,128]{2,1,0:T(8,128)(2,1)S(1)} %get-tuple-element.32), channel_id=1, source_target_pairs={{0,2},{2,0},{4,6},{6,4},{8,10},{10,8},{12,14},{14,12},{16,18},{18,... | collective-permute-start | bytes 491528 | tf_op jit(solution)/shard_map/ppermute | solution.py:461
  5.4 4.2 %collective-permute-start.1 = (bf16[2,320,128]{2,1,0:T(8,128)(2,1)S(1)}, bf16[2,320,128]{2,1,0:T(8,128)(2,1)S(1)}, u32[]{:S(2)}, u32[]{:S(2)}) collective-permute-start(bf16[2,320,128]{2,1,0:T(8,128)(2,1)S(1)} %get-tuple-element.33), channel_id=1, source_target_pairs={{2,4},{4,2},{6,8},{8,6},{10,12},{12,10},{14,16},{16,14},{18,20},{2... | collective-permute-start | bytes 491528 | tf_op jit(solution)/shard_map/ppermute | solution.py:462
  9.6 0.1 collective-permute-start.3
  9.7 3.9 %collective-permute-start.4 = (bf16[2,80,128]{2,1,0:T(8,128)(2,1)S(1)}, bf16[2,80,128]{2,1,0:T(8,128)(2,1)S(1)}, u32[]{:S(2)}, u32[]{:S(2)}) collective-permute-start(bf16[2,80,128]{2,1,0:T(8,128)(2,1)S(1)} %get-tuple-element.36), channel_id=1, source_target_pairs={{2,5},{3,4},{4,3},{5,2},{6,9},{7,8},{8,7},{9,6},{10,13},{11,12},{1... | collective-permute-start | bytes 122888 | tf_op jit(solution)/shard_map/ppermute | solution.py:465
  13.6 5.7 %inner_pass.1 = (f32[2,6,48,128]{3,2,1,0:T(8,128)S(1)}, f32[1152,384]{1,0:T(8,128)S(1)}, f32[384,1152]{1,0:T(8,128)S(1)}, bf16[1152,384]{1,0:T(8,128)(2,1)S(1)},...) custom-call(bf16[2,2,8,64,128]{4,3,2,1,0:T(8,128)(2,1)S(1)} %get-tuple-element.25.xg, ...), custom_call_target="tpu_custom_call" | custom-call | tf_op jit(solution)/shard_map/inner_pass/pallas_call | solution.py:355
  19.4 0.0 collective-permute-done.3.h3
  19.4 0.0 collective-permute-done.4.h4
  19.4 0.0 collective-permute-done.h0
  19.4 0.0 collective-permute-done.1.h1
  19.4 0.0 collective-permute-done.2.h2
  19.4 0.0 copy-start
  19.5 5.9 %outer_pass.1 = (f32[2,10,80,128]{3,2,1,0:T(8,128)S(1)}, f32[27,128,128]{2,1,0:T(8,128)S(1)}, bf16[27,128,128]{2,1,0:T(8,128)(2,1)S(1)}) custom-call(s32[1]{0:T(128)} %bitcast.core, bf16[2,2,8,64,128]{4,3,2,1,0:T(8,128)(2,1)S(1)} %get-tuple-element.25.xg, f32[2,8,64,128]{3,2,1,0:T(8,128)S(1)} %get-tuple-element.26.mask_ref, s32[2,27]{1,0:T(2,128)} %bitcast.20, ...), custom_call_target="tpu_custom_call" | custom-call | tf_op jit(solution)/shard_map/outer_pass/pallas_call | solution.py:383
  25.4 0.3 collective-permute-start.5
  25.7 0.0 copy-done
  25.7 2.3 %input_grad.1 = bf16[2,512,128]{2,1,0:T(8,128)(2,1)} custom-call(f32[2,10,80,128]{3,2,1,0:T(8,128)S(1)} %get-tuple-element.39.gp, f32[2,8,64,128]{3,2,1,0:T(8,128)S(1)} %get-tuple-element.26.mask_ref, bf16[2,512,128]{2,1,0:T(8,128)(2,1)S(1)} %bitcast.14, bf16[384,1152]{1,0:T(8,128)(2,1)S(1)} %get-tuple-element.40.wide), custom_call_target="tpu_custom_call" | custom-call | tf_op jit(solution)/shard_map/input_grad/pallas_call | solution.py:407
  28.0 0.1 collective-permute-done.5
  28.1 0.2 add_convert_fusion
  28.3 21.2 %all_to_all.20 = bf16[16,216,128]{2,1,0:T(8,128)(2,1)S(1)} all-to-all(bf16[16,216,128]{2,1,0:T(8,128)(2,1)S(1)} %bitcast.15), channel_id=1, replica_groups=mesh['z'=8,'x'=4,'yh'=2,'c'=2,'yl'=2] {'x','yh','yl'}, dimensions={0} | all-to-all | bytes 1769472 | tf_op jit(solution)/shard_map/all_to_all | solution.py:480
  49.5 0.1 convert_reduce_fusion
  49.7 15.9 %all_to_all.21 = f32[8,27,128]{2,1,0:T(8,128)S(1)} all-to-all(f32[8,27,128]{2,1,0:T(8,128)S(1)} %reshape.57), channel_id=1, replica_groups=mesh['z'=8,'x'=4,'yh'=2,'c'=2,'yl'=2] {'z'}, dimensions={0} | all-to-all | bytes 221184 | tf_op jit(solution)/shard_map/all_to_all | solution.py:483
  65.6 9.6 %all_to_all.22 = bf16[8,27,128]{2,1,0:T(8,128)(2,1)S(1)} all-to-all(bf16[8,27,128]{2,1,0:T(8,128)(2,1)S(1)} %broadcast_in_dim.6), channel_id=1, replica_groups=mesh['z'=8,'x'=4,'yh'=2,'c'=2,'yl'=2] {'z'}, dimensions={0} | all-to-all | bytes 110592 | tf_op jit(solution)/shard_map/all_to_all | solution.py:472
  75.3 0.1 broadcast_in_dim.15
  75.4 14.7 %all_to_all.23 = bf16[16,216,128]{2,1,0:T(8,128)(2,1)S(1)} all-to-all(bf16[16,216,128]{2,1,0:T(8,128)(2,1)S(1)} %broadcast_in_dim.15), channel_id=1, replica_groups=mesh['z'=8,'x'=4,'yh'=2,'c'=2,'yl'=2] {'x','yh','yl'}, dimensions={0} | all-to-all | bytes 1769472 | tf_op jit(solution)/shard_map/all_to_all | solution.py:472
  90.1 5.5 %collective-permute-start.6 = (bf16[27,128,128]{2,1,0:T(8,128)(2,1)S(1)}, bf16[27,128,128]{2,1,0:T(8,128)(2,1)S(1)}, u32[]{:S(2)}, u32[]{:S(2)}) collective-permute-start(bf16[27,128,128]{2,1,0:T(8,128)(2,1)S(1)} %bitcast.11), channel_id=1, source_target_pairs={{0,2},{2,0},{1,3},{3,1},{4,6},{6,4},{5,7},{7,5},{8,10},{10,8},{9,1... | collective-permute-start | bytes 2654216 | tf_op jit(solution)/shard_map/ppermute | solution.py:450
  95.5 1.3 %mine_half.1 = (f32[27,128,128]{2,1,0:T(8,128)}, f32[27,128,128]{2,1,0:T(8,128)}) custom-call(s32[1]{0:T(128)} %bitcast.core, bf16[27,128,128]{2,1,0:T(8,128)(2,1)S(1)} %bitcast.12), custom_call_target="tpu_custom_call" | custom-call | tf_op jit(solution)/shard_map/mine_half/pallas_call | solution.py:424
  96.8 0.8 collective-permute-done.6.other
  97.6 1.3 %last_half.1 = (f32[27,128,128]{2,1,0:T(8,128)}, f32[27,128,128]{2,1,0:T(8,128)}) custom-call(s32[1]{0:T(128)} %bitcast.core, bf16[27,128,128]{2,1,0:T(8,128)(2,1)S(1)} %collective-permute-done.6.other, f32[27,128,128]{2,1,0:T(8,128)} %get-tuple-element.43.first_in, ...), custom_call_target="tpu_custom_call", output_to_operand_aliasing={{0}: (2, {}), {1}: (3, {})} | custom-call | tf_op jit(solution)/shard_map/last_half/pallas_call | solution.py:437
  (5 shorter events, 0.1 us)
Async XLA Ops:
  2.0 17.4 %collective-permute-start.2 = (bf16[2,336,128]{2,1,0:T(8,128)(2,1)S(1)}, bf16[2,336,128]{2,1,0:T(8,128)(2,1)S(1)}, u32[]{:S(2)}, u32[]{:S(2)}) collective-permute-start(bf16[2,336,128]{2,1,0:T(8,128)(2,1)S(1)} %get-tuple-element.34), channel_id=1, source_target_pairs={{0,1},{1,0},{2,3},{3,2},{4,5},{5,4},{6,7},{7,6},{8,9},{9,8},{10,11... | collective-permute-start | bytes 516104 | tf_op jit(solution)/shard_map/ppermute | solution.py:450
  4.2 15.2 %collective-permute-start = (bf16[2,320,128]{2,1,0:T(8,128)(2,1)S(1)}, bf16[2,320,128]{2,1,0:T(8,128)(2,1)S(1)}, u32[]{:S(2)}, u32[]{:S(2)}) collective-permute-start(bf16[2,320,128]{2,1,0:T(8,128)(2,1)S(1)} %get-tuple-element.32), channel_id=1, source_target_pairs={{0,2},{2,0},{4,6},{6,4},{8,10},{10,8},{12,14},{14,12},{16,18},{18,... | collective-permute-start | bytes 491528 | tf_op jit(solution)/shard_map/ppermute | solution.py:461
  5.4 14.0 %collective-permute-start.1 = (bf16[2,320,128]{2,1,0:T(8,128)(2,1)S(1)}, bf16[2,320,128]{2,1,0:T(8,128)(2,1)S(1)}, u32[]{:S(2)}, u32[]{:S(2)}) collective-permute-start(bf16[2,320,128]{2,1,0:T(8,128)(2,1)S(1)} %get-tuple-element.33), channel_id=1, source_target_pairs={{2,4},{4,2},{6,8},{8,6},{10,12},{12,10},{14,16},{16,14},{18,20},{2... | collective-permute-start | bytes 491528 | tf_op jit(solution)/shard_map/ppermute | solution.py:462
  9.6 9.8 %collective-permute-start.3 = (bf16[2,80,128]{2,1,0:T(8,128)(2,1)S(1)}, bf16[2,80,128]{2,1,0:T(8,128)(2,1)S(1)}, u32[]{:S(2)}, u32[]{:S(2)}) collective-permute-start(bf16[2,80,128]{2,1,0:T(8,128)(2,1)S(1)} %get-tuple-element.35), channel_id=1, source_target_pairs={{0,3},{1,2},{2,1},{3,0},{4,7},{5,6},{6,5},{7,4},{8,11},{9,10},{10,... | collective-permute-start | bytes 122888 | tf_op jit(solution)/shard_map/ppermute | solution.py:464
  9.7 9.7 %collective-permute-start.4 = (bf16[2,80,128]{2,1,0:T(8,128)(2,1)S(1)}, bf16[2,80,128]{2,1,0:T(8,128)(2,1)S(1)}, u32[]{:S(2)}, u32[]{:S(2)}) collective-permute-start(bf16[2,80,128]{2,1,0:T(8,128)(2,1)S(1)} %get-tuple-element.36), channel_id=1, source_target_pairs={{2,5},{3,4},{4,3},{5,2},{6,9},{7,8},{8,7},{9,6},{10,13},{11,12},{1... | collective-permute-start | bytes 122888 | tf_op jit(solution)/shard_map/ppermute | solution.py:465
  19.4 6.2 %copy-start = (bf16[1,1,2,512,128]{4,3,2,1,0:T(8,128)(2,1)S(1)}, bf16[1,1,2,512,128]{4,3,2,1,0:T(8,128)(2,1)}, u32[]{:S(2)}) copy-start(bf16[1,1,2,512,128]{4,3,2,1,0:T(8,128)(2,1)} %param.9) | copy-start | bytes 786436
  25.4 2.7 %collective-permute-start.5 = (bf16[27,128,128]{2,1,0:T(8,128)(2,1)S(1)}, bf16[27,128,128]{2,1,0:T(8,128)(2,1)S(1)}, u32[]{:S(2)}, u32[]{:S(2)}) collective-permute-start(bf16[27,128,128]{2,1,0:T(8,128)(2,1)S(1)} %get-tuple-element.38), channel_id=1, source_target_pairs={{0,2},{2,0},{1,3},{3,1},{4,6},{6,4},{5,7},{7,5},{8,10},{10,8},{9,1... | collective-permute-start | bytes 2654216 | tf_op jit(solution)/shard_map/ppermute | solution.py:450
  90.1 7.5 %collective-permute-start.6 = (bf16[27,128,128]{2,1,0:T(8,128)(2,1)S(1)}, bf16[27,128,128]{2,1,0:T(8,128)(2,1)S(1)}, u32[]{:S(2)}, u32[]{:S(2)}) collective-permute-start(bf16[27,128,128]{2,1,0:T(8,128)(2,1)S(1)} %bitcast.11), channel_id=1, source_target_pairs={{0,2},{2,0},{1,3},{3,1},{4,6},{6,4},{5,7},{7,5},{8,10},{10,8},{9,1... | collective-permute-start | bytes 2654216 | tf_op jit(solution)/shard_map/ppermute | solution.py:450
